TPU v7x, 256 devices: a whole 4x4x8 slice. The times are simulated.
256 devices in a mesh: dp: 4 (over z_hi, core), seq: 64 (over z_lo, y, x).
Axes of the slice: x: 4, y: 4, z: 8 (z_hi: 2, z_lo: 4; z = z_hi * 4 + z_lo), core: 2. Of those that a mesh axis runs over, the one named last changes fastest.
Arguments:
- inputs: bfloat16 [4, 128, 262144], P('dp', None, 'seq'), may hold values from -6 to 6
- grad_out: bfloat16 [4, 128, 262144], P('dp', None, 'seq'), may hold values from -6 to 6
- factor_one: bfloat16 [512, 512], replicated, may hold values from -0.25 to 0.25
- factor_two: bfloat16 [512, 512], replicated, may hold values from -0.25 to 0.25
- factor_three: bfloat16 [512, 512], replicated, may hold values from -0.25 to 0.25
- factor_four: bfloat16 [512, 512], replicated, may hold values from -0.25 to 0.25
- twiddle_in: bfloat16 [512, 512], P('seq'), may hold values from 0.5 to 1.5
- twiddle_out: bfloat16 [512, 512], P('seq'), may hold values from 0.5 to 1.5
- filter_freq: bfloat16 [128, 512, 512], P(None, 'seq'), may hold values from -6 to 6
- skip_gain: float32 [128], replicated, may hold values from 0.5 to 1.5
Outputs:
- outputs: bfloat16 [4, 128, 262144], P('dp', None, 'seq')
- filter_grad: bfloat16 [128, 512, 512], P(None, 'seq')
All inputs are finite; a program needn't handle non-finite values.
Results may differ from a plain program's by a relative error of at most 0.013.
Values may be sent and summed in bfloat16 or wider, within the bound.
No kernel may reach another device: no remote copies, remote signals or barrier semaphores. Data moves between devices by JAX's collectives and lax.ppermute only.
A program may use at most 64 MiB of HBM per device.

v0:
```python
import jax
import jax.numpy as jnp
from jax import lax
from jax.sharding import PartitionSpec as P


def contract(data, matrix):
    return jnp.einsum("bcrk,kj->bcrj", data, matrix, preferred_element_type=jnp.float32)


def contract_back(data, matrix):
    return jnp.einsum("bcrm,km->bcrk", data, matrix, preferred_element_type=jnp.float32)


def shards(
    inputs,
    grad_out,
    factor_one,
    factor_two,
    factor_three,
    factor_four,
    twiddle_in,
    twiddle_out,
    filter_freq,
    skip_gain,
):
    parts = lax.axis_size("seq")
    batch, chans, local_len = inputs.shape
    row_count, width_q = twiddle_in.shape
    col_count, width_p = twiddle_out.shape
    signal = inputs.reshape(batch, chans, row_count, width_q)
    upstream = grad_out.reshape(batch, chans, row_count, width_q)

    def columns_ready(block):
        shaped = block.reshape(batch, chans, row_count, parts, col_count)
        return jnp.transpose(shaped, (0, 1, 3, 4, 2)).reshape(
            batch, chans, parts, col_count * row_count
        )

    def columns_done(block):
        shaped = block.reshape(batch, chans, parts, col_count, row_count)
        return jnp.transpose(shaped, (0, 1, 3, 2, 4)).reshape(batch, chans, col_count, width_p)

    first = contract(signal, factor_one)
    back_raw = contract_back(upstream, factor_four)
    twisted = (first * twiddle_in.astype(jnp.float32)).astype(jnp.bfloat16)
    back_rows = back_raw.astype(jnp.bfloat16)
    moved_fwd = lax.all_to_all(
        columns_ready(twisted), "seq", split_axis=2, concat_axis=2, tiled=True
    )
    moved_back = lax.all_to_all(
        columns_ready(back_rows), "seq", split_axis=2, concat_axis=2, tiled=True
    )
    spread_in = columns_done(moved_fwd)
    back_cols = columns_done(moved_back)
    spread = contract(spread_in, factor_two).astype(jnp.bfloat16)
    filtered = (spread.astype(jnp.float32) * filter_freq.astype(jnp.float32)[None]).astype(
        jnp.bfloat16
    )
    third = contract(filtered, factor_three)
    mixed = (third * twiddle_out.astype(jnp.float32)).astype(jnp.bfloat16)
    shaped = mixed.reshape(batch, chans, col_count, parts, row_count)
    block = lax.all_to_all(
        jnp.transpose(shaped, (0, 1, 3, 2, 4)).reshape(batch, chans, parts, col_count * row_count),
        "seq",
        split_axis=2,
        concat_axis=2,
        tiled=True,
    )
    rows_shaped = block.reshape(batch, chans, parts, col_count, row_count)
    returned = jnp.transpose(rows_shaped, (0, 1, 4, 2, 3)).reshape(batch, chans, row_count, width_q)
    fourth = contract(returned, factor_four)
    gains = skip_gain[None, :, None, None]
    outputs = (
        (fourth + gains * signal.astype(jnp.float32))
        .astype(jnp.bfloat16)
        .reshape(batch, chans, local_len)
    )
    back_twist = (back_cols.astype(jnp.float32) * twiddle_out.astype(jnp.float32)).astype(
        jnp.bfloat16
    )
    grads = contract_back(back_twist, factor_three)
    terms = jnp.sum(spread.astype(jnp.float32) * grads, axis=0)
    filter_grad = lax.psum(terms.astype(jnp.bfloat16), "dp")
    return (outputs, filter_grad)


def solution(mesh):
    in_specs = (
        P("dp", None, "seq"),
        P("dp", None, "seq"),
        P(),
        P(),
        P(),
        P(),
        P("seq", None),
        P("seq", None),
        P(None, "seq", None),
        P(),
    )
    out_specs = (P("dp", None, "seq"), P(None, "seq", None))
    return jax.shard_map(shards, mesh=mesh, in_specs=in_specs, out_specs=out_specs, check_vma=False)
```

profile of v0, /device:TPU:35, one launch (start us, length us, event | category | flops | bytes accessed | tf_op | source)
XLA Modules:
  0.0 188.9 jit_solution(17808480000447588075)
XLA Ops:
  7.2 0.0 copy-start
  7.2 0.0 copy-start.4
  7.2 0.8 convert_element_type.67
  8.0 1.6 copy.35
  9.6 0.0 copy-done.4
  9.6 0.7 multiply_convert_fusion.2
  10.3 1.3 copy.37
  11.7 3.4 %copy.83 = bf16[1,128,64,8,8]{1,4,3,2,0:T(8,128)(2,1)} copy(bf16[1,128,64,8,8]{1,3,2,4,0:T(8,128)(2,1)} %bitcast.76) | data formatting | bytes 2097152 | tf_op jit(solution)/shard_map/transpose | solution.py:36
  15.1 0.0 copy-start.8
  15.1 11.2 %all-to-all-start = ((bf16[1,128,64,64]{1,3,0,2:T(8,128)(2,1)}), bf16[1,128,64,64]{1,3,0,2:T(8,128)(2,1)S(1)}, u32[]{:S(2)}, u32[]{:S(2)}) async-start(bf16[1,128,64,64]{1,3,0,2:T(8,128)(2,1)} %bitcast.75), calls=%async_computation | async-start | bytes 2097152 | tf_op jit(solution)/shard_map/all_to_all | solution.py:48
  26.3 1.6 copy.65
  27.9 0.0 copy-done.8
  27.9 1.7 convolution_convert_fusion
  29.6 2.3 %copy.51 = bf16[128,8,512]{0,2,1:T(8,128)(2,1)} copy(bf16[128,8,512]{2,0,1:T(8,128)(2,1)} %convolution_convert_fusion) | data formatting | bytes 2097152 | tf_op jit(solution)/shard_map/convert_element_type | solution.py:47
  31.9 3.5 %copy.82 = bf16[1,128,64,8,8]{1,4,3,2,0:T(8,128)(2,1)} copy(bf16[1,128,64,8,8]{1,3,2,4,0:T(8,128)(2,1)} %bitcast.77) | data formatting | bytes 2097152 | tf_op jit(solution)/shard_map/transpose | solution.py:36
  35.4 14.6 %all-to-all-done = bf16[1,128,64,64]{1,3,0,2:T(8,128)(2,1)S(1)} async-done(((bf16[1,128,64,64]{1,3,0,2:T(8,128)(2,1)}), bf16[1,128,64,64]{1,3,0,2:T(8,128)(2,1)S(1)}, u32[]{:S(2)}, u32[]{:S(2)}) %all-to-all-start) | async-done | bytes 1048608 | tf_op jit(solution)/shard_map/all_to_all | solution.py:48
  50.0 1.0 copy-done.1
  51.0 9.4 %all-to-all-start.2 = ((bf16[1,128,64,64]{1,3,0,2:T(8,128)(2,1)}), bf16[1,128,64,64]{1,3,0,2:T(8,128)(2,1)S(1)}, u32[]{:S(2)}, u32[]{:S(2)}) async-start(bf16[1,128,64,64]{1,3,0,2:T(8,128)(2,1)} %bitcast.74), calls=%async_computation.2 | async-start | bytes 2097152 | tf_op jit(solution)/shard_map/all_to_all | solution.py:51
  60.4 0.0 copy-done.6
  60.4 0.0 copy-start.7
  60.4 0.0 copy-done.5
  60.4 2.0 %convolution_convert_fusion.1 = bf16[128,8,512]{2,0,1:T(8,128)(2,1)S(1)} fusion(bf16[512,512]{1,0:T(8,128)(2,1)S(1)} %copy-done.5, bf16[1,128,64,64]{1,3,0,2:T(8,128)(2,1)} %copy-done.1), kind=kOutput, calls=%fused_computation.11 | convolution fusion | flops 537395200 | bytes 2621440 | tf_op jit(solution)/shard_map/bcrk,kj->bcrj/dot_general | solution.py:8
  62.5 0.0 copy-start.2
  62.5 1.0 copy-done.2
  63.5 0.0 copy-done
  63.5 0.0 copy-done.7
  63.5 1.7 multiply_convert_fusion.1
  65.2 2.3 %copy.43 = bf16[128,8,512]{0,2,1:T(8,128)(2,1)} copy(bf16[128,8,512]{2,0,1:T(8,128)(2,1)} %multiply_convert_fusion.1) | data formatting | bytes 2097152 | tf_op jit(solution)/shard_map/convert_element_type | solution.py:61
  67.5 2.5 %copy_bitcast_fusion.2 = bf16[1,128,64,64]{1,3,0,2:T(8,128)(2,1)} fusion(bf16[128,8,512]{0,2,1:T(8,128)(2,1)} %copy.43), kind=kLoop, calls=%fused_computation.16 | loop fusion | bytes 2097152 | tf_op jit(solution)/shard_map/reshape | solution.py:64
  70.0 13.9 %all-to-all-done.2 = bf16[1,128,64,64]{1,3,0,2:T(8,128)(2,1)S(1)} async-done(((bf16[1,128,64,64]{1,3,0,2:T(8,128)(2,1)}), bf16[1,128,64,64]{1,3,0,2:T(8,128)(2,1)S(1)}, u32[]{:S(2)}, u32[]{:S(2)}) %all-to-all-start.2) | async-done | bytes 1048608 | tf_op jit(solution)/shard_map/all_to_all | solution.py:51
  83.9 9.7 %all-to-all-start.1 = ((bf16[1,128,64,64]{1,3,0,2:T(8,128)(2,1)}), bf16[1,128,64,64]{1,3,0,2:T(8,128)(2,1)}, u32[]{:S(2)}, u32[]{:S(2)}) async-start(bf16[1,128,64,64]{1,3,0,2:T(8,128)(2,1)} %copy_bitcast_fusion.2), calls=%async_computation.1 | async-start | bytes 2097152 | tf_op jit(solution)/shard_map/all_to_all | solution.py:63
  93.6 0.2 all-reduce.2.cloned.1.call-start
  93.8 1.5 copy_bitcast_fusion
  95.3 3.0 %copy.56 = f32[128,8,512]{2,0,1:T(8,128)} copy(f32[128,8,512]{0,2,1:T(8,128)} %copy_bitcast_fusion) | data formatting | bytes 4194304 | tf_op jit(solution)/shard_map/convert_element_type | solution.py:79
  98.3 0.0 copy-done.3
  98.3 3.3 %fusion.1 = bf16[128,8,512]{2,0,1:T(8,128)(2,1)} fusion(bf16[128,8,512]{2,0,1:T(8,128)(2,1)S(1)} %copy-done.3, f32[128,8,512]{2,0,1:T(8,128)} %copy.56, f32[8,512]{1,0:T(8,128)S(1)} %convert_element_type.73, bf16[512,512]{1,0:T(8,128)(2,1)S(1)} %copy-done), kind=kOutput, calls=%fused_computation.3 | convolution fusion | flops 539492352 | bytes 4734976 | tf_op jit(solution)/shard_map/bcrm,km->bcrk/dot_general | solution.py:12
  101.6 0.0 all-reduce.2.cloned.1.call-update
  101.6 0.0 copy-start.9
  101.6 0.0 copy-start.10
  101.6 0.5 copy.48
  102.2 71.3 %all-reduce.2.cloned.1.call-done = bf16[128,8,512]{2,0,1:T(8,128)(2,1)} async-done(((bf16[128,8,512]{2,0,1:T(8,128)(2,1)}), bf16[128,8,512]{2,0,1:T(8,128)(2,1)}) %all-reduce.2.cloned.1.call-update) | async-done | bytes 1048592 | tf_op jit(solution)/shard_map/psum | solution.py:84
  173.4 2.8 %copy.58 = bf16[128,8,512]{2,1,0:T(8,128)(2,1)} copy(bf16[128,8,512]{2,0,1:T(8,128)(2,1)} %all-reduce.2.cloned.1.call-done) | data formatting | bytes 2097152
  176.2 0.0 all-to-all-done.1
  176.2 0.0 copy-done.9
  176.2 0.0 copy-done.10
  176.2 2.9 %add_convert_fusion = bf16[128,8,512]{2,0,1:T(8,128)(2,1)} fusion(bf16[128,8,512]{2,0,1:T(8,128)(2,1)S(1)} %copy.48, bf16[128,8,512]{0,1,2:T(8,128)(2,1)} %bitcast.17, f32[128]{0:T(128)S(1)} %copy-done.10, bf16[512,512]{1,0:T(8,128)(2,1)S(1)} %copy-done.9), kind=kOutput, calls=%fused_computation.7 | convolution fusion | flops 538968064 | bytes 3670528 | tf_op jit(solution)/shard_map/bcrk,kj->bcrj/dot_general | solution.py:8
  179.2 1.6 copy.49
  180.8 1.3 copy.57
  (5 shorter events, 0.0 us)
Async XLA Ops:
  7.2 56.3 %copy-start = (bf16[512,512]{1,0:T(8,128)(2,1)S(1)}, bf16[512,512]{1,0:T(8,128)(2,1)}, u32[]{:S(2)}) copy-start(bf16[512,512]{1,0:T(8,128)(2,1)} %param.14) | copy-start | bytes 1572868
  7.2 2.4 %copy-start.4 = (bf16[512,512]{1,0:T(8,128)(2,1)S(1)}, bf16[512,512]{1,0:T(8,128)(2,1)}, u32[]{:S(2)}) copy-start(bf16[512,512]{1,0:T(8,128)(2,1)} %param.12) | copy-start | bytes 1572868
  15.1 12.8 %copy-start.8 = (bf16[512,512]{1,0:T(8,128)(2,1)S(1)}, bf16[512,512]{1,0:T(8,128)(2,1)}, u32[]{:S(2)}) copy-start(bf16[512,512]{1,0:T(8,128)(2,1)} %param.15) | copy-start | bytes 1572868
  15.1 34.9 %all-to-all-start = ((bf16[1,128,64,64]{1,3,0,2:T(8,128)(2,1)}), bf16[1,128,64,64]{1,3,0,2:T(8,128)(2,1)S(1)}, u32[]{:S(2)}, u32[]{:S(2)}) async-start(bf16[1,128,64,64]{1,3,0,2:T(8,128)(2,1)} %bitcast.75), calls=%async_computation | async-start | bytes 2097152 | tf_op jit(solution)/shard_map/all_to_all | solution.py:48
  31.9 28.5 %copy-start.6 = (bf16[8,512]{1,0:T(8,128)(2,1)S(1)}, bf16[8,512]{1,0:T(8,128)(2,1)}, u32[]{:S(2)}) copy-start(bf16[8,512]{1,0:T(8,128)(2,1)} %param.17) | copy-start | bytes 24580
  31.9 28.5 %copy-start.5 = (bf16[512,512]{1,0:T(8,128)(2,1)S(1)}, bf16[512,512]{1,0:T(8,128)(2,1)}, u32[]{:S(2)}) copy-start(bf16[512,512]{1,0:T(8,128)(2,1)} %param.13) | copy-start | bytes 1572868
  50.0 1.0 copy-start.1
  51.0 32.9 %all-to-all-start.2 = ((bf16[1,128,64,64]{1,3,0,2:T(8,128)(2,1)}), bf16[1,128,64,64]{1,3,0,2:T(8,128)(2,1)S(1)}, u32[]{:S(2)}, u32[]{:S(2)}) async-start(bf16[1,128,64,64]{1,3,0,2:T(8,128)(2,1)} %bitcast.74), calls=%async_computation.2 | async-start | bytes 2097152 | tf_op jit(solution)/shard_map/all_to_all | solution.py:51
  60.4 3.1 %copy-start.7 = (bf16[128,8,512]{2,1,0:T(8,128)(2,1)S(1)}, bf16[128,8,512]{2,1,0:T(8,128)(2,1)}, u32[]{:S(2)}) copy-start(bf16[128,8,512]{2,1,0:T(8,128)(2,1)} %param.18) | copy-start | bytes 3145732
  62.5 1.0 copy-start.2
  83.9 92.4 %all-to-all-start.1 = ((bf16[1,128,64,64]{1,3,0,2:T(8,128)(2,1)}), bf16[1,128,64,64]{1,3,0,2:T(8,128)(2,1)}, u32[]{:S(2)}, u32[]{:S(2)}) async-start(bf16[1,128,64,64]{1,3,0,2:T(8,128)(2,1)} %copy_bitcast_fusion.2), calls=%async_computation.1 | async-start | bytes 2097152 | tf_op jit(solution)/shard_map/all_to_all | solution.py:63
  93.6 79.9 %all-reduce.2.cloned.1.call-start = ((), (), s32[]{:S(2)}) async-start(), calls=%async_computation.3 | async-start | bytes 2097152 | tf_op jit(solution)/shard_map/psum | solution.py:84
  95.3 3.0 %copy-start.3 = (bf16[128,8,512]{2,0,1:T(8,128)(2,1)S(1)}, bf16[128,8,512]{2,0,1:T(8,128)(2,1)}, u32[]{:S(2)}) copy-start(bf16[128,8,512]{2,0,1:T(8,128)(2,1)} %copy-done.2) | copy-start | bytes 3145732
  101.6 74.6 %copy-start.9 = (bf16[512,512]{1,0:T(8,128)(2,1)S(1)}, bf16[512,512]{1,0:T(8,128)(2,1)}, u32[]{:S(2)}) copy-start(bf16[512,512]{1,0:T(8,128)(2,1)} %param.15) | copy-start | bytes 1572868
  101.6 74.6 %copy-start.10 = (f32[128]{0:T(128)S(1)}, f32[128]{0:T(128)}, u32[]{:S(2)}) copy-start(f32[128]{0:T(128)} %param.19) | copy-start | bytes 1540
Sparse Core Ops, SparseCore 0:
  101.7 71.6 all-reduce.1
where the time goes:
time: 192 us; the launch traced here: 189 us
  waiting for transfers between devices  99.7 us (52%)
  starting transfers between devices  30.5 us (16%)
  local copies, waits for them, and re-layouts  29.7 us (15%)
  between operations  14.2 us (7%)
  matrix products  12.5 us (7%)
  other arithmetic  2.25 us (1%)
    psum x1, waiting for transfers between devices, shards(): filter_grad = lax.psum(terms.astype(jnp.bfloat16), 'dp')  71.3 us
    all_to_all x1, waiting for transfers between devices, shards(): lax.all_to_all(columns_ready(twisted), 'seq', split_axis=2, concat_axis=2...  14.6 us
    all_to_all x1, waiting for transfers between devices, shards(): lax.all_to_all(columns_ready(back_rows), 'seq', split_axis=2, concat_axis...  13.9 us
    all_to_all x1, starting transfers between devices, shards(): lax.all_to_all(columns_ready(twisted), 'seq', split_axis=2, concat_axis=2...  11.2 us
    all_to_all x1, starting transfers between devices, shards(): lax.all_to_all(jnp.transpose(shaped, (0, 1, 3, 2, 4)).reshape(batch, chan...  9.71 us
    all_to_all x1, starting transfers between devices, shards(): lax.all_to_all(columns_ready(back_rows), 'seq', split_axis=2, concat_axis...  9.39 us
    unnamed x26, local copies, waits for them, and re-layouts  9.32 us
    dot_general x4, matrix products, contract(): jnp.einsum('bcrk,kj->bcrj', data, matrix, preferred_element_type=jnp.floa...  7.45 us
  transfers between devices with their start and end apart: 4, of which 3 were waited for; matrix products, arithmetic and copies ran while one was open for 15% of the time, Pallas kernels for 0%

commit v1 on v0

v1 whole, which is shorter than its diff:
```python
import jax
import jax.numpy as jnp
from jax import lax
from jax.experimental import pallas as pl
from jax.experimental.pallas import tpu as pltpu
from jax.sharding import PartitionSpec as P

F32 = jnp.float32
BF16 = jnp.bfloat16
LANES = 128
ROWS = 8
WIDTH = 512
Z_LO = 4
YX = 16
PART = WIDTH // Z_LO
MSG = ROWS * ROWS
PARAMS = pltpu.CompilerParams(vmem_limit_bytes=32 * 1024 * 1024)

NT = (((1,), (1,)), ((), ()))
NN = (((1,), (0,)), ((), ()))
TN = (((0,), (0,)), ((), ()))


def dot(left, right, dims=NN):
    return lax.dot_general(left, right, dims, preferred_element_type=F32)


def my_z():
    return lax.axis_index("seq") // YX


def my_core():
    return lax.axis_index("dp") % 2


def part(z, e):
    return pl.ds(pl.multiple_of((z ^ e) * PART, PART), PART)


def struct(shape, dtype=BF16):
    return jax.ShapeDtypeStruct(shape, dtype)


def vmem(n):
    return [pl.BlockSpec(memory_space=pltpu.VMEM) for _ in range(n)]


def call(body, outs, scratch, *args):
    return pl.pallas_call(
        body,
        out_shape=outs,
        in_specs=vmem(len(args)),
        out_specs=jax.tree.map(lambda _: pl.BlockSpec(memory_space=pltpu.VMEM), outs),
        scratch_shapes=scratch,
        compiler_params=PARAMS,
    )(*args)


BLOCKS = [struct((YX, MSG, LANES))] * Z_LO


def rows_out(weight_scr, x_ref, twist, scr, out_refs):
    for pair in range(ROWS // 2):
        left = x_ref[:, (2 * pair) * WIDTH : (2 * pair + 1) * WIDTH]
        right = x_ref[:, (2 * pair + 1) * WIDTH : (2 * pair + 2) * WIDTH]
        both = dot(weight_scr[...], jnp.concatenate([left, right], axis=0), NT)
        for half in range(2):
            r = 2 * pair + half
            value = both[:, half * LANES : (half + 1) * LANES]
            if twist is not None:
                value = value * twist[:, r : r + 1]
            scr[pl.ds(r, WIDTH, stride=ROWS), :] = value
    step = WIDTH * ROWS // Z_LO
    for e, out in enumerate(out_refs):
        out[...] = scr[e * step : (e + 1) * step, :].astype(BF16).reshape(YX, MSG, LANES)


def first_body(x_ref, f_ref, tw_ref, o0, o1, o2, o3, fscr, scr):
    z = my_z()
    twist = []
    for e in range(Z_LO):
        fscr[e * PART : (e + 1) * PART, :] = f_ref[:, part(z, e)].T
        twist.append(tw_ref[:, part(z, e)].astype(F32).T)
    rows_out(fscr, x_ref, jnp.concatenate(twist, axis=0), scr, (o0, o1, o2, o3))


def back_body(x_ref, f_ref, o0, o1, o2, o3, fscr, scr):
    z = my_z()
    for e in range(Z_LO):
        fscr[e * PART : (e + 1) * PART, :] = f_ref[part(z, e), :]
    rows_out(fscr, x_ref, None, scr, (o0, o1, o2, o3))


def columns(recv_ref, pair):
    got = [[], []]
    for e in range(Z_LO):
        block = recv_ref[:, e, pair * 16 : (pair + 1) * 16, :].astype(F32)
        block = block.reshape(YX, 2, ROWS, LANES)
        for half in range(2):
            got[half].append(block[:, half].reshape(PART, LANES))
    return [jnp.concatenate(parts, axis=0) for parts in got]


def twist_columns(tw_ref, z):
    return jnp.concatenate(
        [tw_ref[:, part(z, e)].astype(F32).T for e in range(Z_LO)], axis=0
    )


def middle_body(u_ref, f2t_ref, f3t_ref, tw_ref, filt_ref, zt_ref, o0, o1, o2, o3, f2s, f3s):
    z = my_z()
    for e in range(Z_LO):
        f2s[:, e * PART : (e + 1) * PART] = f2t_ref[:, part(z, e)]
        f3s[e * PART : (e + 1) * PART, :] = f3t_ref[part(z, e), :]
    twist = twist_columns(tw_ref, z)
    for pair in range(ROWS // 2):
        k = 2 * pair
        cols = columns(u_ref, pair)
        rhs = jnp.concatenate([c.astype(BF16) for c in cols], axis=1)
        spread = dot(f2s[...], rhs).astype(BF16)
        zt_ref[k] = spread[:, :LANES]
        zt_ref[k + 1] = spread[:, LANES:]
        filt = jnp.concatenate([filt_ref[k], filt_ref[k + 1]], axis=1)
        filtered = (spread.astype(F32) * filt.astype(F32)).astype(BF16)
        third = dot(f3s[...], filtered)
        first = third[:, :LANES] * twist[:, k : k + 1]
        second = third[:, LANES:] * twist[:, k + 1 : k + 2]
        shaped = jnp.concatenate(
            [first.reshape(Z_LO * YX, ROWS, LANES), second.reshape(Z_LO * YX, ROWS, LANES)],
            axis=1,
        ).astype(BF16)
        for e, out in enumerate((o0, o1, o2, o3)):
            out[:, pair * 16 : (pair + 1) * 16, :] = shaped[e * YX : (e + 1) * YX]


def grad_body(d_ref, f3_ref, tw_ref, zt_ref, keep_ref, send_ref, f3s):
    z = my_z()
    core = my_core()
    half = WIDTH // 2
    mine = pl.ds(pl.multiple_of(core * half, half), half)
    other = pl.ds(pl.multiple_of((1 - core) * half, half), half)
    for e in range(Z_LO):
        f3s[:half, e * PART : (e + 1) * PART] = f3_ref[mine, part(z, e)]
        f3s[half:, e * PART : (e + 1) * PART] = f3_ref[other, part(z, e)]
    twist = twist_columns(tw_ref, z)
    for pair in range(ROWS // 2):
        k = 2 * pair
        cols = columns(d_ref, pair)
        rhs = jnp.concatenate(
            [(cols[h] * twist[:, k + h : k + h + 1]).astype(BF16) for h in range(2)], axis=1
        )
        grads = dot(f3s[...], rhs)
        for h in range(2):
            value = grads[:, h * LANES : (h + 1) * LANES]
            keep_ref[k + h] = (zt_ref[k + h, mine, :].astype(F32) * value[:half]).astype(BF16)
            send_ref[k + h] = (zt_ref[k + h, other, :].astype(F32) * value[half:]).astype(BF16)


def last_body(s_ref, f_ref, x_ref, g_ref, o_ref, fscr, scr):
    z = my_z()
    step = YX * MSG
    for e in range(Z_LO):
        fscr[e * PART : (e + 1) * PART, :] = f_ref[part(z, e), :]
        scr[e * step : (e + 1) * step, :] = s_ref[:, e].astype(F32).reshape(step, LANES)
    gains = g_ref[...]
    for r in range(ROWS):
        rows = scr[pl.ds(r, WIDTH, stride=ROWS), :].astype(BF16)
        fourth = dot(rows, fscr[...], TN)
        signal = x_ref[:, r * WIDTH : (r + 1) * WIDTH].astype(F32)
        o_ref[:, r * WIDTH : (r + 1) * WIDTH] = (fourth + gains * signal).astype(BF16)


def add_body(a_ref, b_ref, o_ref):
    o_ref[...] = (a_ref[...].astype(F32) + b_ref[...].astype(F32)).astype(BF16)


def total_body(a_ref, b_ref, o_ref, scr):
    for side in range(2):
        span = slice(side * LANES, (side + 1) * LANES)
        for k in range(ROWS):
            total = a_ref[k, span, :].astype(F32) + b_ref[k, span, :].astype(F32)
            scr[pl.ds(k, LANES, stride=ROWS), :] = total.T
        o_ref[:, span] = scr[...].astype(BF16)


def join_body(a_ref, b_ref, o_ref):
    core = my_core()
    half = WIDTH // 2
    o_ref[:, pl.ds(pl.multiple_of(core * half, half), half)] = a_ref[...]
    o_ref[:, pl.ds(pl.multiple_of((1 - core) * half, half), half)] = b_ref[...]


def across_z(blocks):
    moved = [blocks[0]]
    for e in range(1, Z_LO):
        moved.append(
            lax.ppermute(blocks[e], "seq", [(i, i ^ (e * YX)) for i in range(Z_LO * YX)])
        )
    return moved


def across_yx(blocks):
    groups = [[g * YX + t for t in range(YX)] for g in range(Z_LO)]
    return lax.all_to_all(
        jnp.stack(blocks, axis=1),
        "seq",
        split_axis=0,
        concat_axis=0,
        axis_index_groups=groups,
        tiled=True,
    )


def swap(block, bit):
    return lax.ppermute(block, "dp", [(i, i ^ bit) for i in range(4)])


def shards(
    inputs,
    grad_out,
    factor_one,
    factor_two,
    factor_three,
    factor_four,
    twiddle_in,
    twiddle_out,
    filter_freq,
    skip_gain,
):
    batch, chans, local_len = inputs.shape
    signal = inputs.reshape(chans, local_len)
    upstream = grad_out.reshape(chans, local_len)
    square = pltpu.VMEM((WIDTH, WIDTH), BF16)
    tall = pltpu.VMEM((WIDTH * ROWS, LANES), F32)

    sent = call(first_body, BLOCKS, [square, tall], signal, factor_one, twiddle_in)
    got = across_yx(across_z(sent))
    back = call(back_body, BLOCKS, [square, tall], upstream, factor_four)
    back_got = across_yx(across_z(back))

    filt = jnp.transpose(filter_freq, (1, 2, 0))
    spread, *mixed = call(
        middle_body,
        [struct((ROWS, WIDTH, LANES))] + BLOCKS,
        [square, square],
        got,
        factor_two.T,
        factor_three.T,
        twiddle_out,
        filt,
    )
    returned = across_yx(across_z(mixed))

    half = struct((ROWS, WIDTH // 2, LANES))
    keep, send = call(
        grad_body, [half, half], [square], back_got, factor_three, twiddle_out, spread
    )
    pair = call(add_body, half, [], keep, swap(send, 1))
    flat = struct((LANES * ROWS, WIDTH // 2))
    mine = call(
        total_body, flat, [pltpu.VMEM((LANES * ROWS, LANES), F32)], pair, swap(pair, 2)
    )
    filter_grad = call(join_body, struct((LANES * ROWS, WIDTH)), [], mine, swap(mine, 1))

    outputs = call(
        last_body,
        struct((chans, local_len)),
        [square, tall],
        returned,
        factor_four,
        signal,
        skip_gain.reshape(chans, 1),
    )
    return (
        outputs.reshape(batch, chans, local_len),
        filter_grad.reshape(chans, ROWS, WIDTH),
    )


def solution(mesh):
    in_specs = (
        P("dp", None, "seq"),
        P("dp", None, "seq"),
        P(),
        P(),
        P(),
        P(),
        P("seq", None),
        P("seq", None),
        P(None, "seq", None),
        P(),
    )
    out_specs = (P("dp", None, "seq"), P(None, "seq", None))
    return jax.shard_map(shards, mesh=mesh, in_specs=in_specs, out_specs=out_specs, check_vma=False)
```

time: 192 us -> 168 us (0.88)
  the two profiles are of different devices: /device:TPU:35 before, /device:TPU:192 now
where the time goes in v1:
time: 168 us; the launch traced here: 167 us
  waiting for transfers between devices  102 us (61%)
  starting transfers between devices  31.9 us (19%)
  local copies, waits for them, and re-layouts  17.2 us (10%)
  Pallas kernels  11.5 us (7%)
  other arithmetic  3.29 us (2%)
    ppermute x9, waiting for transfers between devices, across_z(): lax.ppermute(blocks[e], 'seq', [(i, i ^ e * YX) for i in range(Z_LO * YX)])  85.1 us
    all_to_all x3, starting transfers between devices, across_yx(): lax.all_to_all(jnp.stack(blocks, axis=1), 'seq', split_axis=0, concat_axi...  18.8 us
    unnamed x43, local copies, waits for them, and re-layouts  17.1 us
    all_to_all x3, waiting for transfers between devices, across_yx(): lax.all_to_all(jnp.stack(blocks, axis=1), 'seq', split_axis=0, concat_axi...  17 us
    ppermute x9, starting transfers between devices, across_z(): lax.ppermute(blocks[e], 'seq', [(i, i ^ e * YX) for i in range(Z_LO * YX)])  11.6 us
    pallas_call x8, Pallas kernels, call(): pl.pallas_call(body, out_shape=outs, in_specs=vmem(len(args)), out_specs=...  11.5 us
  transfers between devices with their start and end apart: 15, of which 10 were waited for; matrix products, arithmetic and copies ran while one was open for 5% of the time, Pallas kernels for 4%

profile of v1, /device:TPU:192, one launch (start us, length us, event | category | flops | bytes accessed | tf_op | source)
XLA Modules:
  0.0 166.9 jit_solution(8589562823974133241)
XLA Ops:
  0.6 1.2 copy-done
  1.9 1.0 copy-done.10
  2.9 0.7 copy-done.12
  3.6 1.0 shard_map.113
  4.6 1.1 collective-permute-start
  5.8 1.4 collective-permute-start.1
  7.2 1.0 collective-permute-start.2
  8.2 7.7 %collective-permute-done = bf16[16,64,128]{2,1,0:T(8,128)(2,1)S(1)} collective-permute-done((bf16[16,64,128]{2,1,0:T(8,128)(2,1)S(1)}, bf16[16,64,128]{2,1,0:T(8,128)(2,1)S(1)}, u32[]{:S(2)}, u32[]{:S(2)}) %collective-permute-start) | collective-permute-done | bytes 262176 | tf_op jit(solution)/shard_map/ppermute | solution.py:197
  15.9 9.3 %collective-permute-done.1 = bf16[16,64,128]{2,1,0:T(8,128)(2,1)S(1)} collective-permute-done((bf16[16,64,128]{2,1,0:T(8,128)(2,1)S(1)}, bf16[16,64,128]{2,1,0:T(8,128)(2,1)S(1)}, u32[]{:S(2)}, u32[]{:S(2)}) %collective-permute-start.1) | collective-permute-done | bytes 262176 | tf_op jit(solution)/shard_map/ppermute | solution.py:197
  25.2 5.7 %collective-permute-done.2 = bf16[16,64,128]{2,1,0:T(8,128)(2,1)S(1)} collective-permute-done((bf16[16,64,128]{2,1,0:T(8,128)(2,1)S(1)}, bf16[16,64,128]{2,1,0:T(8,128)(2,1)S(1)}, u32[]{:S(2)}, u32[]{:S(2)}) %collective-permute-start.2) | collective-permute-done | bytes 262176 | tf_op jit(solution)/shard_map/ppermute | solution.py:197
  30.9 1.1 pad_maximum_fusion
  32.0 7.2 %all-to-all-start = ((bf16[16,4,64,128]{3,2,1,0:T(8,128)(2,1)}), bf16[16,4,64,128]{3,2,1,0:T(8,128)(2,1)S(1)}, u32[]{:S(2)}, u32[]{:S(2)}) async-start(bf16[16,4,64,128]{3,2,1,0:T(8,128)(2,1)} %pad_maximum_fusion), calls=%async_computation | async-start | bytes 2097152 | tf_op jit(solution)/shard_map/all_to_all | solution.py:204
  39.2 0.9 shard_map.116
  40.2 2.5 %collective-permute-start.7 = (bf16[16,64,128]{2,1,0:T(8,128)(2,1)S(1)}, bf16[16,64,128]{2,1,0:T(8,128)(2,1)S(1)}, u32[]{:S(2)}, u32[]{:S(2)}) collective-permute-start(bf16[16,64,128]{2,1,0:T(8,128)(2,1)S(1)} %get-tuple-element.27), channel_id=1, source_target_pairs={{0,32},{1,33},{2,34},{3,35},{4,36},{5,37},{6,38},{7,39},{8,40},{9,... | collective-permute-start | bytes 786440 | tf_op jit(solution)/shard_map/ppermute | solution.py:197
  42.6 1.0 collective-permute-start.8
  43.6 5.8 %collective-permute-done.6 = bf16[16,64,128]{2,1,0:T(8,128)(2,1)S(1)} collective-permute-done((bf16[16,64,128]{2,1,0:T(8,128)(2,1)S(1)}, bf16[16,64,128]{2,1,0:T(8,128)(2,1)S(1)}, u32[]{:S(2)}, u32[]{:S(2)}) %collective-permute-start.6) | collective-permute-done | bytes 262176 | tf_op jit(solution)/shard_map/ppermute | solution.py:197
  49.4 10.9 %collective-permute-done.7 = bf16[16,64,128]{2,1,0:T(8,128)(2,1)S(1)} collective-permute-done((bf16[16,64,128]{2,1,0:T(8,128)(2,1)S(1)}, bf16[16,64,128]{2,1,0:T(8,128)(2,1)S(1)}, u32[]{:S(2)}, u32[]{:S(2)}) %collective-permute-start.7) | collective-permute-done | bytes 262176 | tf_op jit(solution)/shard_map/ppermute | solution.py:197
  60.3 4.5 %collective-permute-done.8 = bf16[16,64,128]{2,1,0:T(8,128)(2,1)S(1)} collective-permute-done((bf16[16,64,128]{2,1,0:T(8,128)(2,1)S(1)}, bf16[16,64,128]{2,1,0:T(8,128)(2,1)S(1)}, u32[]{:S(2)}, u32[]{:S(2)}) %collective-permute-start.8) | collective-permute-done | bytes 262176 | tf_op jit(solution)/shard_map/ppermute | solution.py:197
  64.8 1.1 pad_maximum_fusion.2
  65.9 6.9 %all-to-all-start.2 = ((bf16[16,4,64,128]{3,2,1,0:T(8,128)(2,1)}), bf16[16,4,64,128]{3,2,1,0:T(8,128)(2,1)S(1)}, u32[]{:S(2)}, u32[]{:S(2)}) async-start(bf16[16,4,64,128]{3,2,1,0:T(8,128)(2,1)} %pad_maximum_fusion.2), calls=%async_computation.2 | async-start | bytes 2097152 | tf_op jit(solution)/shard_map/all_to_all | solution.py:204
  72.9 1.9 %copy.14 = bf16[128,8,512]{0,2,1:T(8,128)(2,1)S(1)} copy(bf16[128,8,512]{2,1,0:T(8,128)(2,1)} %param.18) | data formatting | bytes 2097152 | tf_op args[8]
  74.8 2.0 %copy.12 = bf16[512,512]{0,1:T(8,128)(2,1)} copy(bf16[512,512]{1,0:T(8,128)(2,1)} %param.13) | data formatting | bytes 1048576 | tf_op args[3]
  76.9 2.0 %copy.13 = bf16[512,512]{0,1:T(8,128)(2,1)} copy(bf16[512,512]{1,0:T(8,128)(2,1)} %f3_ref.1) | data formatting | bytes 1048576 | tf_op args[4]
  78.9 1.0 copy-done.5
  80.0 1.0 copy-done.6
  81.0 1.6 shard_map.114
  82.6 1.0 copy-done.8
  83.6 0.7 copy-done.13
  84.3 0.7 copy-done.15
  85.0 0.7 copy-done.17
  85.7 2.6 %all-to-all-done.2.d_ref = bf16[16,4,64,128]{3,2,1,0:T(8,128)(2,1)S(1)} async-done(((bf16[16,4,64,128]{3,2,1,0:T(8,128)(2,1)}), bf16[16,4,64,128]{3,2,1,0:T(8,128)(2,1)S(1)}, u32[]{:S(2)}, u32[]{:S(2)}) %all-to-all-start.2) | async-done | bytes 1048608 | tf_op jit(solution)/shard_map/all_to_all | solution.py:204
  88.2 1.0 copy-done.4
  89.3 1.2 copy-done.9
  90.5 1.0 shard_map.117
  91.8 1.1 collective-permute-start.5
  92.9 3.2 %collective-permute-start.3 = (bf16[16,64,128]{2,1,0:T(8,128)(2,1)S(1)}, bf16[16,64,128]{2,1,0:T(8,128)(2,1)S(1)}, u32[]{:S(2)}, u32[]{:S(2)}) collective-permute-start(bf16[16,64,128]{2,1,0:T(8,128)(2,1)S(1)} %copy-done.14), channel_id=1, source_target_pairs={{0,16},{1,17},{2,18},{3,19},{4,20},{5,21},{6,22},{7,23},{8,24},{9,... | collective-permute-start | bytes 786440 | tf_op jit(solution)/shard_map/ppermute | solution.py:197
  96.2 0.1 shard_map.118.a_ref
  96.3 1.4 collective-permute-start.10
  97.7 12.0 %collective-permute-done.4 = bf16[16,64,128]{2,1,0:T(8,128)(2,1)S(1)} collective-permute-done((bf16[16,64,128]{2,1,0:T(8,128)(2,1)S(1)}, bf16[16,64,128]{2,1,0:T(8,128)(2,1)S(1)}, u32[]{:S(2)}, u32[]{:S(2)}) %collective-permute-start.4) | collective-permute-done | bytes 262176 | tf_op jit(solution)/shard_map/ppermute | solution.py:197
  109.8 29.3 %collective-permute-done.5 = bf16[16,64,128]{2,1,0:T(8,128)(2,1)S(1)} collective-permute-done((bf16[16,64,128]{2,1,0:T(8,128)(2,1)S(1)}, bf16[16,64,128]{2,1,0:T(8,128)(2,1)S(1)}, u32[]{:S(2)}, u32[]{:S(2)}) %collective-permute-start.5) | collective-permute-done | bytes 262176 | tf_op jit(solution)/shard_map/ppermute | solution.py:197
  139.0 1.1 pad_maximum_fusion.1
  140.1 4.7 %all-to-all-start.1 = ((bf16[16,4,64,128]{3,2,1,0:T(8,128)(2,1)}), bf16[16,4,64,128]{3,2,1,0:T(8,128)(2,1)S(1)}, u32[]{:S(2)}, u32[]{:S(2)}) async-start(bf16[16,4,64,128]{3,2,1,0:T(8,128)(2,1)} %pad_maximum_fusion.1), calls=%async_computation.1 | async-start | bytes 2097152 | tf_op jit(solution)/shard_map/all_to_all | solution.py:204
  144.8 2.4 %shard_map.119.a_ref = bf16[1024,256]{1,0:T(8,128)(2,1)} custom-call(bf16[8,256,128]{2,1,0:T(8,128)(2,1)S(1)} %shard_map.118.a_ref, bf16[8,256,128]{2,1,0:T(8,128)(2,1)} %collective-permute-done.10.b_ref), custom_call_target="tpu_custom_call" | custom-call | tf_op jit(solution)/shard_map/pallas_call | solution.py:49
  147.2 0.7 copy-done.19
  147.9 0.1 copy.15.g_ref
  148.0 14.5 %all-to-all-done.1.s_ref = bf16[16,4,64,128]{3,2,1,0:T(8,128)(2,1)S(1)} async-done(((bf16[16,4,64,128]{3,2,1,0:T(8,128)(2,1)}), bf16[16,4,64,128]{3,2,1,0:T(8,128)(2,1)S(1)}, u32[]{:S(2)}, u32[]{:S(2)}) %all-to-all-start.1) | async-done | bytes 1048608 | tf_op jit(solution)/shard_map/all_to_all | solution.py:204
  162.4 2.3 %shard_map.115 = bf16[128,4096]{1,0:T(8,128)(2,1)} custom-call(bf16[16,4,64,128]{3,2,1,0:T(8,128)(2,1)S(1)} %all-to-all-done.1.s_ref, bf16[512,512]{1,0:T(8,128)(2,1)S(1)} %copy-done.3, bf16[128,4096]{1,0:T(8,128)(2,1)S(1)} %bitcast.21, f32[128,1]{1,0:T(8,128)S(1)} %copy.15.g_ref), custom_call_target="tpu_custom_call" | custom-call | tf_op jit(solution)/shard_map/pallas_call | solution.py:49
  164.7 2.2 %shard_map.120 = bf16[1024,512]{1,0:T(8,128)(2,1)} custom-call(bf16[1024,256]{1,0:T(8,128)(2,1)} %shard_map.119.a_ref, bf16[1024,256]{1,0:T(8,128)(2,1)S(1)} %collective-permute-done.11.b_ref), custom_call_target="tpu_custom_call" | custom-call | tf_op jit(solution)/shard_map/pallas_call | solution.py:49
  (37 shorter events, 0.4 us)
Async XLA Ops:
  0.6 1.2 copy-start
  1.9 1.0 copy-start.10
  2.9 0.7 copy-start.12
  4.6 11.2 %collective-permute-start = (bf16[16,64,128]{2,1,0:T(8,128)(2,1)S(1)}, bf16[16,64,128]{2,1,0:T(8,128)(2,1)S(1)}, u32[]{:S(2)}, u32[]{:S(2)}) collective-permute-start(bf16[16,64,128]{2,1,0:T(8,128)(2,1)S(1)} %get-tuple-element.18), channel_id=1, source_target_pairs={{0,16},{1,17},{2,18},{3,19},{4,20},{5,21},{6,22},{7,23},{8,24},{9,... | collective-permute-start | bytes 786440 | tf_op jit(solution)/shard_map/ppermute | solution.py:197
  5.8 19.4 %collective-permute-start.1 = (bf16[16,64,128]{2,1,0:T(8,128)(2,1)S(1)}, bf16[16,64,128]{2,1,0:T(8,128)(2,1)S(1)}, u32[]{:S(2)}, u32[]{:S(2)}) collective-permute-start(bf16[16,64,128]{2,1,0:T(8,128)(2,1)S(1)} %get-tuple-element.19), channel_id=1, source_target_pairs={{0,32},{1,33},{2,34},{3,35},{4,36},{5,37},{6,38},{7,39},{8,40},{9,... | collective-permute-start | bytes 786440 | tf_op jit(solution)/shard_map/ppermute | solution.py:197
  7.2 23.6 %collective-permute-start.2 = (bf16[16,64,128]{2,1,0:T(8,128)(2,1)S(1)}, bf16[16,64,128]{2,1,0:T(8,128)(2,1)S(1)}, u32[]{:S(2)}, u32[]{:S(2)}) collective-permute-start(bf16[16,64,128]{2,1,0:T(8,128)(2,1)S(1)} %get-tuple-element.20), channel_id=1, source_target_pairs={{0,48},{1,49},{2,50},{3,51},{4,52},{5,53},{6,54},{7,55},{8,56},{9,... | collective-permute-start | bytes 786440 | tf_op jit(solution)/shard_map/ppermute | solution.py:197
  32.0 7.2 %copy-start.2 = (bf16[512,512]{1,0:T(8,128)(2,1)S(1)}, bf16[512,512]{1,0:T(8,128)(2,1)}, u32[]{:S(2)}) copy-start(bf16[512,512]{1,0:T(8,128)(2,1)} %f_ref.5) | copy-start | bytes 1572868
  32.0 7.2 %copy-start.7 = (bf16[1,128,4096]{2,1,0:T(8,128)(2,1)S(1)}, bf16[1,128,4096]{2,1,0:T(8,128)(2,1)}, u32[]{:S(2)}) copy-start(bf16[1,128,4096]{2,1,0:T(8,128)(2,1)} %param.11) | copy-start | bytes 3145732
  32.0 34.0 %all-to-all-start = ((bf16[16,4,64,128]{3,2,1,0:T(8,128)(2,1)}), bf16[16,4,64,128]{3,2,1,0:T(8,128)(2,1)S(1)}, u32[]{:S(2)}, u32[]{:S(2)}) async-start(bf16[16,4,64,128]{3,2,1,0:T(8,128)(2,1)} %pad_maximum_fusion), calls=%async_computation | async-start | bytes 2097152 | tf_op jit(solution)/shard_map/all_to_all | solution.py:204
  40.1 9.3 %collective-permute-start.6 = (bf16[16,64,128]{2,1,0:T(8,128)(2,1)S(1)}, bf16[16,64,128]{2,1,0:T(8,128)(2,1)S(1)}, u32[]{:S(2)}, u32[]{:S(2)}) collective-permute-start(bf16[16,64,128]{2,1,0:T(8,128)(2,1)S(1)} %get-tuple-element.26), channel_id=1, source_target_pairs={{0,16},{1,17},{2,18},{3,19},{4,20},{5,21},{6,22},{7,23},{8,24},{9,... | collective-permute-start | bytes 786440 | tf_op jit(solution)/shard_map/ppermute | solution.py:197
  40.2 20.2 %collective-permute-start.7 = (bf16[16,64,128]{2,1,0:T(8,128)(2,1)S(1)}, bf16[16,64,128]{2,1,0:T(8,128)(2,1)S(1)}, u32[]{:S(2)}, u32[]{:S(2)}) collective-permute-start(bf16[16,64,128]{2,1,0:T(8,128)(2,1)S(1)} %get-tuple-element.27), channel_id=1, source_target_pairs={{0,32},{1,33},{2,34},{3,35},{4,36},{5,37},{6,38},{7,39},{8,40},{9,... | collective-permute-start | bytes 786440 | tf_op jit(solution)/shard_map/ppermute | solution.py:197
  42.6 22.2 %collective-permute-start.8 = (bf16[16,64,128]{2,1,0:T(8,128)(2,1)S(1)}, bf16[16,64,128]{2,1,0:T(8,128)(2,1)S(1)}, u32[]{:S(2)}, u32[]{:S(2)}) collective-permute-start(bf16[16,64,128]{2,1,0:T(8,128)(2,1)S(1)} %get-tuple-element.28), channel_id=1, source_target_pairs={{0,48},{1,49},{2,50},{3,51},{4,52},{5,53},{6,54},{7,55},{8,56},{9,... | collective-permute-start | bytes 786440 | tf_op jit(solution)/shard_map/ppermute | solution.py:197
  65.9 22.3 %all-to-all-start.2 = ((bf16[16,4,64,128]{3,2,1,0:T(8,128)(2,1)}), bf16[16,4,64,128]{3,2,1,0:T(8,128)(2,1)S(1)}, u32[]{:S(2)}, u32[]{:S(2)}) async-start(bf16[16,4,64,128]{3,2,1,0:T(8,128)(2,1)} %pad_maximum_fusion.2), calls=%async_computation.2 | async-start | bytes 2097152 | tf_op jit(solution)/shard_map/all_to_all | solution.py:204
  76.9 2.1 %copy-start.11 = (bf16[8,512]{1,0:T(8,128)(2,1)S(1)}, bf16[8,512]{1,0:T(8,128)(2,1)}, u32[]{:S(2)}) copy-start(bf16[8,512]{1,0:T(8,128)(2,1)} %tw_ref.5) | copy-start | bytes 24580
  78.9 1.0 copy-start.5
  80.0 1.0 copy-start.6
  82.6 1.0 copy-start.8
  83.6 0.7 copy-start.13
  84.3 0.7 copy-start.15
  85.0 0.7 copy-start.17
  88.2 1.0 copy-start.4
  89.3 1.2 copy-start.9
  90.5 1.2 copy-start.18
  90.5 1.3 copy-start.16
  90.5 2.4 %copy-start.14 = (bf16[16,64,128]{2,1,0:T(8,128)(2,1)S(1)}, bf16[16,64,128]{2,1,0:T(8,128)(2,1)}, u32[]{:S(2)}) copy-start(bf16[16,64,128]{2,1,0:T(8,128)(2,1)} %copy-done.13) | copy-start | bytes 786436
  91.6 4.6 %collective-permute-start.9 = (bf16[8,256,128]{2,1,0:T(8,128)(2,1)S(1)}, bf16[8,256,128]{2,1,0:T(8,128)(2,1)S(1)}, u32[]{:S(2)}, u32[]{:S(2)}) collective-permute-start(bf16[8,256,128]{2,1,0:T(8,128)(2,1)S(1)} %get-tuple-element.31), channel_id=1, source_target_pairs={{0,64},{64,0},{128,192},{192,128},{1,65},{65,1},{129,193},{193,129... | collective-permute-start | bytes 1572872 | tf_op jit(solution)/shard_map/ppermute | solution.py:215
  91.7 18.1 %collective-permute-start.4 = (bf16[16,64,128]{2,1,0:T(8,128)(2,1)S(1)}, bf16[16,64,128]{2,1,0:T(8,128)(2,1)S(1)}, u32[]{:S(2)}, u32[]{:S(2)}) collective-permute-start(bf16[16,64,128]{2,1,0:T(8,128)(2,1)S(1)} %copy-done.18), channel_id=1, source_target_pairs={{0,32},{1,33},{2,34},{3,35},{4,36},{5,37},{6,38},{7,39},{8,40},{9,... | collective-permute-start | bytes 786440 | tf_op jit(solution)/shard_map/ppermute | solution.py:197
  91.8 47.2 %collective-permute-start.5 = (bf16[16,64,128]{2,1,0:T(8,128)(2,1)S(1)}, bf16[16,64,128]{2,1,0:T(8,128)(2,1)S(1)}, u32[]{:S(2)}, u32[]{:S(2)}) collective-permute-start(bf16[16,64,128]{2,1,0:T(8,128)(2,1)S(1)} %copy-done.16), channel_id=1, source_target_pairs={{0,48},{1,49},{2,50},{3,51},{4,52},{5,53},{6,54},{7,55},{8,56},{9,... | collective-permute-start | bytes 786440 | tf_op jit(solution)/shard_map/ppermute | solution.py:197
  92.9 46.1 %collective-permute-start.3 = (bf16[16,64,128]{2,1,0:T(8,128)(2,1)S(1)}, bf16[16,64,128]{2,1,0:T(8,128)(2,1)S(1)}, u32[]{:S(2)}, u32[]{:S(2)}) collective-permute-start(bf16[16,64,128]{2,1,0:T(8,128)(2,1)S(1)} %copy-done.14), channel_id=1, source_target_pairs={{0,16},{1,17},{2,18},{3,19},{4,20},{5,21},{6,22},{7,23},{8,24},{9,... | collective-permute-start | bytes 786440 | tf_op jit(solution)/shard_map/ppermute | solution.py:197
  96.3 48.5 %collective-permute-start.10 = (bf16[8,256,128]{2,1,0:T(8,128)(2,1)S(1)}, bf16[8,256,128]{2,1,0:T(8,128)(2,1)}, u32[]{:S(2)}, u32[]{:S(2)}) collective-permute-start(bf16[8,256,128]{2,1,0:T(8,128)(2,1)S(1)} %shard_map.118.a_ref), channel_id=1, source_target_pairs={{0,128},{64,192},{128,0},{192,64},{1,129},{65,193},{129,1},{193,65... | collective-permute-start | bytes 1572872 | tf_op jit(solution)/shard_map/ppermute | solution.py:215
  140.1 22.3 %all-to-all-start.1 = ((bf16[16,4,64,128]{3,2,1,0:T(8,128)(2,1)}), bf16[16,4,64,128]{3,2,1,0:T(8,128)(2,1)S(1)}, u32[]{:S(2)}, u32[]{:S(2)}) async-start(bf16[16,4,64,128]{3,2,1,0:T(8,128)(2,1)} %pad_maximum_fusion.1), calls=%async_computation.1 | async-start | bytes 2097152 | tf_op jit(solution)/shard_map/all_to_all | solution.py:204
  144.8 17.6 %copy-start.1 = (bf16[1,128,4096]{2,1,0:T(8,128)(2,1)S(1)}, bf16[1,128,4096]{2,1,0:T(8,128)(2,1)}, u32[]{:S(2)}) copy-start(bf16[1,128,4096]{2,1,0:T(8,128)(2,1)} %param.10) | copy-start | bytes 3145732
  144.8 17.6 %copy-start.3 = (bf16[512,512]{1,0:T(8,128)(2,1)S(1)}, bf16[512,512]{1,0:T(8,128)(2,1)}, u32[]{:S(2)}) copy-start(bf16[512,512]{1,0:T(8,128)(2,1)} %f_ref.5) | copy-start | bytes 1572868
  147.2 0.7 copy-start.19
  147.2 17.5 %collective-permute-start.11 = (bf16[1024,256]{1,0:T(8,128)(2,1)}, bf16[1024,256]{1,0:T(8,128)(2,1)S(1)}, u32[]{:S(2)}, u32[]{:S(2)}) collective-permute-start(bf16[1024,256]{1,0:T(8,128)(2,1)} %shard_map.119.a_ref), channel_id=1, source_target_pairs={{0,64},{64,0},{128,192},{192,128},{1,65},{65,1},{129,193},{193,129... | collective-permute-start | bytes 1572872 | tf_op jit(solution)/shard_map/ppermute | solution.py:215

commit v2 on v1

v2 whole, which is shorter than its diff:
```python
import jax
import jax.numpy as jnp
from jax import lax
from jax.experimental import pallas as pl
from jax.experimental.pallas import tpu as pltpu
from jax.sharding import PartitionSpec as P

F32 = jnp.float32
BF16 = jnp.bfloat16
LANES = 128
ROWS = 8
WIDTH = 512
HALF = WIDTH // 2
Z_LO = 4
YX = 16
PART = WIDTH // Z_LO
MSG = ROWS * ROWS
PAIRS = ROWS // 2
MIDDLE_US = 60
GRAD_US = 60

NT = (((1,), (1,)), ((), ()))
NN = (((1,), (0,)), ((), ()))
TN = (((0,), (0,)), ((), ()))


def dot(left, right, dims=NN):
    return lax.dot_general(left, right, dims, preferred_element_type=F32)


def my_z():
    return lax.axis_index("seq") // YX


def my_core():
    return lax.axis_index("dp") % 2


def part(z, e):
    return pl.ds(pl.multiple_of((z ^ e) * PART, PART), PART)


def halves(core):
    return pl.ds(pl.multiple_of(core * HALF, HALF), HALF)


def struct(shape, dtype=BF16):
    return jax.ShapeDtypeStruct(shape, dtype)


BLOCK = struct((YX, MSG, LANES))
WHOLE = struct((YX, Z_LO, MSG, LANES))
SQUARE = pltpu.VMEM((WIDTH, WIDTH), BF16)
TALL = pltpu.VMEM((WIDTH * ROWS, LANES), F32)


class Copies:
    def __init__(self, sems):
        self.sems = sems
        self.started = []
        self.waited = set()
        self.inputs = {}

    def start(self, src, dst):
        copy = pltpu.make_async_copy(src, dst, self.sems.at[len(self.started)])
        copy.start()
        self.started.append(copy)

    def fetch(self, arg, src, dst):
        self.inputs[arg] = len(self.started)
        self.start(src, dst)

    def wait(self, *args):
        for arg in args:
            self.finish(self.inputs.get(arg))

    def finish(self, n):
        if n is not None and n not in self.waited:
            self.waited.add(n)
            self.started[n].wait()

    def finish_all(self):
        for n in range(len(self.started)):
            self.finish(n)


class Far:
    def __init__(self, value, pinned=True):
        self.value = value
        self.pinned = pinned


def call(body, outs, scratch, *args, copies=0, weight_us=0):
    n_in, n_out = len(args), len(outs)
    far_in = [n for n, a in enumerate(args) if isinstance(a, Far)]
    far_out = [n for n, o in enumerate(outs) if isinstance(o, Far)]
    pinned = [n for n in far_in if args[n].pinned]
    args = [a.value if isinstance(a, Far) else a for a in args]
    outs = [o.value if isinstance(o, Far) else o for o in outs]
    hbm = pl.BlockSpec(memory_space=pltpu.HBM)
    free = pl.BlockSpec(memory_space=pl.ANY)
    vmem = pl.BlockSpec(memory_space=pltpu.VMEM)

    def space(n):
        return hbm if n in pinned else free if n in far_in else vmem

    def wrapped(*refs):
        refs = list(refs)
        ins, refs = refs[:n_in], refs[n_in:]
        results, refs = refs[:n_out], refs[n_out:]
        flow = Copies(refs.pop(0))
        for n in far_in:
            near = refs.pop(0)
            flow.fetch(n, ins[n], near)
            ins[n] = near
        near_results = list(results)
        for n in far_out:
            near_results[n] = refs.pop(0)
        body(flow, ins, results, near_results, *refs)
        flow.finish_all()

    return pl.pallas_call(
        wrapped,
        out_shape=[
            pltpu.HBM(o.shape, o.dtype) if n in far_out else o for n, o in enumerate(outs)
        ],
        in_specs=[space(n) for n in range(n_in)],
        out_specs=[hbm if n in far_out else vmem for n in range(n_out)],
        scratch_shapes=[pltpu.SemaphoreType.DMA((max(1, len(far_in) + copies),))]
        + [pltpu.VMEM(args[n].shape, args[n].dtype) for n in far_in]
        + [pltpu.VMEM(outs[n].shape, outs[n].dtype) for n in far_out]
        + scratch,
        compiler_params=pltpu.CompilerParams(vmem_limit_bytes=16 * 1024 * 1024),
        cost_estimate=pl.CostEstimate(
            flops=weight_us * 10**9, bytes_accessed=weight_us * 3 * 10**6, transcendentals=0
        ),
    )(
        *[
            pltpu.with_memory_space_constraint(a, pltpu.HBM) if n in pinned else a
            for n, a in enumerate(args)
        ]
    )


def rows_out(weight_scr, x_ref, twist, scr, finish):
    for pair in range(PAIRS):
        left = x_ref[:, (2 * pair) * WIDTH : (2 * pair + 1) * WIDTH]
        right = x_ref[:, (2 * pair + 1) * WIDTH : (2 * pair + 2) * WIDTH]
        both = dot(weight_scr[...], jnp.concatenate([left, right], axis=0), NT)
        for half in range(2):
            r = 2 * pair + half
            value = both[:, half * LANES : (half + 1) * LANES]
            if twist is not None:
                value = value * twist[:, r : r + 1]
            scr[pl.ds(r, WIDTH, stride=ROWS), :] = value
    step = WIDTH * ROWS // Z_LO
    for e in range(Z_LO):
        finish(e, scr[e * step : (e + 1) * step, :].astype(BF16).reshape(YX, MSG, LANES))


def first_body(flow, ins, results, outs, fscr, scr):
    f_ref, tw_ref, x_ref = ins
    z = my_z()
    flow.wait(0, 1)
    twist = []
    for e in range(Z_LO):
        fscr[e * PART : (e + 1) * PART, :] = f_ref[:, part(z, e)].T
        twist.append(tw_ref[:, part(z, e)].astype(F32).T)
    flow.wait(2)

    def finish(e, block):
        outs[0][:, e] = block
        flow.start(outs[0].at[:, e], results[0].at[:, e])

    rows_out(fscr, x_ref, jnp.concatenate(twist, axis=0), scr, finish)


def back_body(flow, ins, results, outs, fscr, scr):
    f_ref, x_ref = ins
    z = my_z()
    flow.wait(0)
    for e in range(Z_LO):
        fscr[e * PART : (e + 1) * PART, :] = f_ref[part(z, e), :]
    flow.wait(1)

    def finish(e, block):
        outs[e][...] = block

    rows_out(fscr, x_ref, None, scr, finish)


def columns(refs, pair):
    got = [[], []]
    for ref in refs:
        block = ref[:, pair * 16 : (pair + 1) * 16, :].astype(F32)
        block = block.reshape(YX, 2, ROWS, LANES)
        for half in range(2):
            got[half].append(block[:, half].reshape(PART, LANES))
    return [jnp.concatenate(parts, axis=0) for parts in got]


def twist_columns(tw_ref, z):
    return jnp.concatenate(
        [tw_ref[:, part(z, e)].astype(F32).T for e in range(Z_LO)], axis=0
    )


def middle_body(flow, ins, results, outs, f2s, f3s):
    f2t_ref, tw_ref, u0, u1, u2, u3, filt_ref, f3t_ref = ins
    zt_ref, *blocks = outs
    z = my_z()
    flow.wait(0, 1)
    for e in range(Z_LO):
        f2s[:, e * PART : (e + 1) * PART] = f2t_ref[:, part(z, e)]
    twist = twist_columns(tw_ref, z)
    for pair in range(PAIRS):
        k = 2 * pair
        cols = columns((u0, u1, u2, u3), pair)
        rhs = jnp.concatenate([c.astype(BF16) for c in cols], axis=1)
        spread = dot(f2s[...], rhs).astype(BF16)
        zt_ref[k] = spread[:, :LANES]
        zt_ref[k + 1] = spread[:, LANES:]
        if pair == 0:
            flow.wait(6, 7)
            for e in range(Z_LO):
                f3s[e * PART : (e + 1) * PART, :] = f3t_ref[part(z, e), :]
        filt = jnp.concatenate([filt_ref[k], filt_ref[k + 1]], axis=1)
        filtered = (spread.astype(F32) * filt.astype(F32)).astype(BF16)
        third = dot(f3s[...], filtered)
        first = third[:, :LANES] * twist[:, k : k + 1]
        second = third[:, LANES:] * twist[:, k + 1 : k + 2]
        shaped = jnp.concatenate(
            [first.reshape(Z_LO * YX, ROWS, LANES), second.reshape(Z_LO * YX, ROWS, LANES)],
            axis=1,
        ).astype(BF16)
        rows = slice(pair * 16, (pair + 1) * 16)
        for e, block in enumerate(blocks):
            block[:, rows, :] = shaped[e * YX : (e + 1) * YX]
        flow.start(zt_ref.at[k : k + 2], results[0].at[k : k + 2])


def grad_body(flow, ins, results, outs, f3s):
    f3_ref, tw_ref, d_ref, zt_ref = ins
    z = my_z()
    core = my_core()
    spans = (halves(core), halves(1 - core))
    flow.wait(0, 1)
    for n, span in enumerate(spans):
        for e in range(Z_LO):
            f3s[n * HALF : (n + 1) * HALF, e * PART : (e + 1) * PART] = f3_ref[span, part(z, e)]
    twist = twist_columns(tw_ref, z)
    for pair in range(PAIRS):
        k = 2 * pair
        cols = columns([d_ref.at[:, e] for e in range(Z_LO)], pair)
        rhs = jnp.concatenate(
            [(cols[h] * twist[:, k + h : k + h + 1]).astype(BF16) for h in range(2)], axis=1
        )
        grads = dot(f3s[...], rhs)
        flow.wait(3)
        for h in range(2):
            value = grads[:, h * LANES : (h + 1) * LANES]
            for n, (span, out) in enumerate(zip(spans, outs)):
                spread = zt_ref[k + h, span, :].astype(F32)
                out[k + h] = (spread * value[n * HALF : (n + 1) * HALF]).astype(BF16)


def last_body(flow, ins, results, outs, fscr, scr):
    f_ref, g_ref, s_ref, x_ref = ins
    o_ref = outs[0]
    z = my_z()
    step = YX * MSG
    flow.wait(0)
    for e in range(Z_LO):
        fscr[e * PART : (e + 1) * PART, :] = f_ref[part(z, e), :]
        scr[e * step : (e + 1) * step, :] = s_ref[:, e].astype(F32).reshape(step, LANES)
    flow.wait(1, 3)
    gains = g_ref[...]
    for r in range(ROWS):
        rows = scr[pl.ds(r, WIDTH, stride=ROWS), :].astype(BF16)
        fourth = dot(rows, fscr[...], TN)
        span = slice(r * WIDTH, (r + 1) * WIDTH)
        signal = x_ref[:, span].astype(F32)
        o_ref[:, span] = (fourth + gains * signal).astype(BF16)
        flow.start(o_ref.at[:, span], results[0].at[:, span])


def add_body(flow, ins, results, outs):
    outs[0][...] = (ins[0][...].astype(F32) + ins[1][...].astype(F32)).astype(BF16)


def total_body(flow, ins, results, outs, scr):
    a_ref, b_ref = ins
    for side in range(2):
        span = slice(side * LANES, (side + 1) * LANES)
        for k in range(ROWS):
            total = a_ref[k, span, :].astype(F32) + b_ref[k, span, :].astype(F32)
            scr[pl.ds(k, LANES, stride=ROWS), :] = total.T
        outs[0][:, span] = scr[...].astype(BF16)


def join_body(flow, ins, results, outs):
    core = my_core()
    outs[0][:, halves(core)] = ins[0][...]
    outs[0][:, halves(1 - core)] = ins[1][...]
    flow.start(outs[0], results[0])


def gather_body(flow, ins, results, outs):
    for e, block in enumerate(ins):
        outs[0][:, e] = block[...]
        flow.start(outs[0].at[:, e], results[0].at[:, e])


def spread_body(flow, ins, results, outs):
    for e, block in enumerate(outs):
        block[...] = ins[0][:, e]


def gathered(blocks):
    return call(gather_body, [Far(WHOLE)], [], *blocks, copies=Z_LO)[0]


def scattered(whole):
    return call(spread_body, [BLOCK] * Z_LO, [], whole)


def across_z(blocks):
    moved = [blocks[0]]
    for e in range(1, Z_LO):
        moved.append(
            lax.ppermute(blocks[e], "seq", [(i, i ^ (e * YX)) for i in range(Z_LO * YX)])
        )
    return moved


def tied(*values):
    return lax.optimization_barrier(values)


def across_yx(whole):
    groups = [[g * YX + t for t in range(YX)] for g in range(Z_LO)]
    return lax.all_to_all(
        whole, "seq", split_axis=0, concat_axis=0, axis_index_groups=groups, tiled=True
    )


def swap(block, bit):
    return lax.ppermute(block, "dp", [(i, i ^ bit) for i in range(4)])


def shards(
    inputs,
    grad_out,
    factor_one,
    factor_two,
    factor_three,
    factor_four,
    twiddle_in,
    twiddle_out,
    filter_freq,
    skip_gain,
):
    batch, chans, local_len = inputs.shape
    signal = inputs.reshape(chans, local_len)
    upstream = grad_out.reshape(chans, local_len)

    sent = call(
        first_body,
        [Far(WHOLE)],
        [SQUARE, TALL],
        Far(factor_one),
        Far(twiddle_in),
        Far(signal),
        copies=Z_LO,
    )[0]
    back = call(back_body, [BLOCK] * Z_LO, [SQUARE, TALL], Far(factor_four), Far(upstream))
    filt = jnp.transpose(filter_freq, (1, 2, 0))
    gains = skip_gain.reshape(chans, 1)
    moved, filt, two, three, gains = tied(
        across_yx(sent), filt, factor_two.T, factor_three.T, gains
    )
    got = across_z(scattered(moved))
    back_got = across_yx(gathered(across_z(back)))

    spread, *mixed = call(
        middle_body,
        [Far(struct((ROWS, WIDTH, LANES)))] + [BLOCK] * Z_LO,
        [SQUARE, SQUARE],
        Far(two),
        Far(twiddle_out),
        *got,
        Far(filt),
        Far(three),
        copies=PAIRS,
        weight_us=MIDDLE_US,
    )
    half = struct((ROWS, HALF, LANES))
    keep, send = call(
        grad_body,
        [half, half],
        [SQUARE],
        Far(factor_three),
        Far(twiddle_out),
        back_got,
        Far(spread),
        weight_us=GRAD_US,
    )
    mixed_arrived, keep, send = tied(across_z(mixed), keep, send)
    pair = call(add_body, [half], [], keep, swap(send, 1))[0]
    far = swap(pair, 2)
    returned = across_yx(gathered(mixed_arrived))
    flat = struct((LANES * ROWS, HALF))
    mine = call(total_body, [flat], [pltpu.VMEM((LANES * ROWS, LANES), F32)], pair, far)[0]
    filter_grad = call(
        join_body, [Far(struct((LANES * ROWS, WIDTH)))], [], mine, swap(mine, 1), copies=1
    )[0]

    outputs = call(
        last_body,
        [Far(struct((chans, local_len)))],
        [SQUARE, TALL],
        Far(factor_four),
        Far(gains),
        returned,
        Far(signal),
        copies=ROWS,
    )[0]
    return (
        outputs.reshape(batch, chans, local_len),
        filter_grad.reshape(chans, ROWS, WIDTH),
    )


def solution(mesh):
    in_specs = (
        P("dp", None, "seq"),
        P("dp", None, "seq"),
        P(),
        P(),
        P(),
        P(),
        P("seq", None),
        P("seq", None),
        P(None, "seq", None),
        P(),
    )
    out_specs = (P("dp", None, "seq"), P(None, "seq", None))
    return jax.shard_map(shards, mesh=mesh, in_specs=in_specs, out_specs=out_specs, check_vma=False)
```

time: 168 us -> 131 us (0.78)
  the two profiles are of different devices: /device:TPU:192 before, /device:TPU:35 now
where the time goes in v2:
time: 131 us; the launch traced here: 129 us
  waiting for transfers between devices  54.7 us (42%)
  starting transfers between devices  45.9 us (35%)
  Pallas kernels  21 us (16%)
  local copies, waits for them, and re-layouts  6.46 us (5%)
    ppermute x9, waiting for transfers between devices, across_z(): lax.ppermute(blocks[e], 'seq', [(i, i ^ e * YX) for i in range(Z_LO * YX)])  35.6 us
    all_to_all x3, starting transfers between devices, across_yx(): lax.all_to_all(whole, 'seq', split_axis=0, concat_axis=0, axis_index_grou...  27 us
    pallas_call x11, Pallas kernels, call(): pl.pallas_call(wrapped, out_shape=[pltpu.HBM(o.shape, o.dtype) if n in fa...  21 us
    ppermute x3, waiting for transfers between devices, swap(): return lax.ppermute(block, 'dp', [(i, i ^ bit) for i in range(4)])  16.3 us
    ppermute x3, starting transfers between devices, swap(): return lax.ppermute(block, 'dp', [(i, i ^ bit) for i in range(4)])  9.46 us
    ppermute x9, starting transfers between devices, across_z(): lax.ppermute(blocks[e], 'seq', [(i, i ^ e * YX) for i in range(Z_LO * YX)])  9.43 us
    unnamed x7, local copies, waits for them, and re-layouts  5.73 us
    all_to_all x3, waiting for transfers between devices, across_yx(): lax.all_to_all(whole, 'seq', split_axis=0, concat_axis=0, axis_index_grou...  2.85 us
  transfers between devices with their start and end apart: 15, of which 9 were waited for; matrix products, arithmetic and copies ran while one was open for 5% of the time, Pallas kernels for 13%

profile of v2, /device:TPU:35, one launch (start us, length us, event | category | flops | bytes accessed | tf_op | source)
XLA Modules:
  0.0 129.0 jit_solution(1963014945151640319)
XLA Ops:
  0.6 3.2 %shard_map.113 = bf16[16,4,64,128]{3,2,1,0:T(8,128)(2,1)} custom-call(bf16[512,512]{1,0:T(8,128)(2,1)} %refs_0_.4, bf16[8,512]{1,0:T(8,128)(2,1)} %refs_1_.3, bf16[128,4096]{1,0:T(8,128)(2,1)} %bitcast.8), custom_call_target="tpu_custom_call" | custom-call | tf_op jit(solution)/shard_map/pallas_call | solution.py:122
  3.8 6.9 %all-to-all-start = ((bf16[16,4,64,128]{3,2,1,0:T(8,128)(2,1)}), bf16[16,4,64,128]{3,2,1,0:T(8,128)(2,1)S(1)}, u32[]{:S(2)}, u32[]{:S(2)}) async-start(bf16[16,4,64,128]{3,2,1,0:T(8,128)(2,1)} %shard_map.113), calls=%async_computation | async-start | bytes 2097152 | tf_op jit(solution)/shard_map/all_to_all | solution.py:342
  10.8 3.0 %shard_map.116 = (bf16[16,64,128]{2,1,0:T(8,128)(2,1)S(1)}, bf16[16,64,128]{2,1,0:T(8,128)(2,1)}, bf16[16,64,128]{2,1,0:T(8,128)(2,1)}, bf16[16,64,128]{2,1,0:T(8,128)(2,1)S(1)}) custom-call(bf16[512,512]{1,0:T(8,128)(2,1)} %refs_0_.7, bf16[128,4096]{1,0:T(8,128)(2,1)} %bitcast.11), custom_call_target="tpu_custom_call" | custom-call | tf_op jit(solution)/shard_map/pallas_call | solution.py:122
  13.7 0.1 collective-permute-start.6
  13.8 3.1 %collective-permute-start.7 = (bf16[16,64,128]{2,1,0:T(8,128)(2,1)}, bf16[16,64,128]{2,1,0:T(8,128)(2,1)S(1)}, u32[]{:S(2)}, u32[]{:S(2)}) collective-permute-start(bf16[16,64,128]{2,1,0:T(8,128)(2,1)} %get-tuple-element.43), channel_id=1, source_target_pairs={{0,32},{1,33},{2,34},{3,35},{4,36},{5,37},{6,38},{7,39},{8,40},{9,... | collective-permute-start | bytes 786440 | tf_op jit(solution)/shard_map/ppermute | solution.py:331
  16.9 0.0 copy-start
  16.9 0.2 collective-permute-start.8
  17.1 2.7 %copy.12 = bf16[128,8,512]{0,2,1:T(8,128)(2,1)} copy(bf16[128,8,512]{2,1,0:T(8,128)(2,1)} %param.18) | data formatting | bytes 2097152 | tf_op args[8]
  19.8 0.0 copy-done
  19.8 1.0 copy.13
  20.8 2.1 %copy.14 = bf16[512,512]{0,1:T(8,128)(2,1)} copy(bf16[512,512]{1,0:T(8,128)(2,1)} %refs_0_.6) | data formatting | bytes 1048576 | tf_op args[4]
  22.8 2.8 %all-to-all-done.refs_0_ = bf16[16,4,64,128]{3,2,1,0:T(8,128)(2,1)S(1)} async-done(((bf16[16,4,64,128]{3,2,1,0:T(8,128)(2,1)}), bf16[16,4,64,128]{3,2,1,0:T(8,128)(2,1)S(1)}, u32[]{:S(2)}, u32[]{:S(2)}) %all-to-all-start) | async-done | bytes 1048608 | tf_op jit(solution)/shard_map/all_to_all | solution.py:342
  25.7 0.9 shard_map.114
  26.5 0.1 collective-permute-start
  26.6 3.1 %collective-permute-start.1 = (bf16[16,64,128]{2,1,0:T(8,128)(2,1)}, bf16[16,64,128]{2,1,0:T(8,128)(2,1)S(1)}, u32[]{:S(2)}, u32[]{:S(2)}) collective-permute-start(bf16[16,64,128]{2,1,0:T(8,128)(2,1)} %get-tuple-element.33), channel_id=1, source_target_pairs={{0,32},{1,33},{2,34},{3,35},{4,36},{5,37},{6,38},{7,39},{8,40},{9,... | collective-permute-start | bytes 786440 | tf_op jit(solution)/shard_map/ppermute | solution.py:331
  29.7 0.0 collective-permute-done.6.refs_1_
  29.7 0.2 collective-permute-start.2
  29.9 0.0 collective-permute-done.7.refs_2_
  29.9 10.0 %collective-permute-done.8.refs_3_ = bf16[16,64,128]{2,1,0:T(8,128)(2,1)S(1)} collective-permute-done((bf16[16,64,128]{2,1,0:T(8,128)(2,1)S(1)}, bf16[16,64,128]{2,1,0:T(8,128)(2,1)S(1)}, u32[]{:S(2)}, u32[]{:S(2)}) %collective-permute-start.8) | collective-permute-done | bytes 262176 | tf_op jit(solution)/shard_map/ppermute | solution.py:331
  39.9 1.1 shard_map.117
  41.0 13.4 %all-to-all-start.1 = ((bf16[16,4,64,128]{3,2,1,0:T(8,128)(2,1)}), bf16[16,4,64,128]{3,2,1,0:T(8,128)(2,1)S(1)}, u32[]{:S(2)}, u32[]{:S(2)}) async-start(bf16[16,4,64,128]{3,2,1,0:T(8,128)(2,1)} %shard_map.117), calls=%async_computation.1 | async-start | bytes 2097152 | tf_op jit(solution)/shard_map/all_to_all | solution.py:342
  54.4 0.0 collective-permute-done.refs_3_
  54.4 1.0 collective-permute-done.1.refs_4_
  55.4 6.5 %collective-permute-done.2.refs_5_ = bf16[16,64,128]{2,1,0:T(8,128)(2,1)} collective-permute-done((bf16[16,64,128]{2,1,0:T(8,128)(2,1)S(1)}, bf16[16,64,128]{2,1,0:T(8,128)(2,1)}, u32[]{:S(2)}, u32[]{:S(2)}) %collective-permute-start.2) | collective-permute-done | bytes 262176 | tf_op jit(solution)/shard_map/ppermute | solution.py:331
  62.0 4.3 %shard_map.115 = (bf16[8,512,128]{2,1,0:T(8,128)(2,1)}, bf16[16,64,128]{2,1,0:T(8,128)(2,1)S(1)}, bf16[16,64,128]{2,1,0:T(8,128)(2,1)S(1)}, bf16[16,64,128]{2,1,0:T(8,128)(2,1)S(1)}, bf16[16,64,128]{2,1,0:T(8,128)(2,1)S(1)}) custom-call(bf16[512,512]{1,0:T(8,128)(2,1)} %bitcast.14, bf16[8,512]{1,0:T(8,128)(2,1)} %refs_1_.5, ...), custom_call_target="tpu_custom_call" | custom-call | flops 60000002048 | bytes 180000000 | tf_op jit(solution)/shard_map/pallas_call | solution.py:122
  66.2 0.1 collective-permute-start.3
  66.3 2.4 %collective-permute-start.4 = (bf16[16,64,128]{2,1,0:T(8,128)(2,1)S(1)}, bf16[16,64,128]{2,1,0:T(8,128)(2,1)S(1)}, u32[]{:S(2)}, u32[]{:S(2)}) collective-permute-start(bf16[16,64,128]{2,1,0:T(8,128)(2,1)S(1)} %get-tuple-element.39), channel_id=1, source_target_pairs={{0,32},{1,33},{2,34},{3,35},{4,36},{5,37},{6,38},{7,39},{8,40},{9,... | collective-permute-start | bytes 786440 | tf_op jit(solution)/shard_map/ppermute | solution.py:331
  68.8 0.2 collective-permute-start.5
  69.0 0.0 all-to-all-done.1.refs_2_
  69.0 2.6 %shard_map.118 = (bf16[8,256,128]{2,1,0:T(8,128)(2,1)S(1)}, bf16[8,256,128]{2,1,0:T(8,128)(2,1)S(1)}) custom-call(bf16[512,512]{1,0:T(8,128)(2,1)} %refs_0_.6, bf16[8,512]{1,0:T(8,128)(2,1)} %refs_1_.5, bf16[16,4,64,128]{3,2,1,0:T(8,128)(2,1)S(1)} %all-to-all-done.1.refs_2_, bf16[8,512,128]{2,1,0:T(8,128)(2,1)} %get-tuple-element.45.refs_3_), custom_call_target="tpu_custom_call" | custom-call | flops 60000002048 | bytes 180000000 | tf_op jit(solution)/shard_map/pallas_call | solution.py:122
  71.6 1.3 collective-permute-done.3.refs_1_
  72.9 5.7 %collective-permute-done.4.refs_2_ = bf16[16,64,128]{2,1,0:T(8,128)(2,1)S(1)} collective-permute-done((bf16[16,64,128]{2,1,0:T(8,128)(2,1)S(1)}, bf16[16,64,128]{2,1,0:T(8,128)(2,1)S(1)}, u32[]{:S(2)}, u32[]{:S(2)}) %collective-permute-start.4) | collective-permute-done | bytes 262176 | tf_op jit(solution)/shard_map/ppermute | solution.py:331
  78.6 11.0 %collective-permute-done.5.refs_3_ = bf16[16,64,128]{2,1,0:T(8,128)(2,1)S(1)} collective-permute-done((bf16[16,64,128]{2,1,0:T(8,128)(2,1)S(1)}, bf16[16,64,128]{2,1,0:T(8,128)(2,1)S(1)}, u32[]{:S(2)}, u32[]{:S(2)}) %collective-permute-start.5) | collective-permute-done | bytes 262176 | tf_op jit(solution)/shard_map/ppermute | solution.py:331
  89.6 3.5 %collective-permute-start.9 = (bf16[8,256,128]{2,1,0:T(8,128)(2,1)S(1)}, bf16[8,256,128]{2,1,0:T(8,128)(2,1)S(1)}, u32[]{:S(2)}, u32[]{:S(2)}) collective-permute-start(bf16[8,256,128]{2,1,0:T(8,128)(2,1)S(1)} %get-tuple-element.53), channel_id=1, source_target_pairs={{0,64},{64,0},{128,192},{192,128},{1,65},{65,1},{129,193},{193,129... | collective-permute-start | bytes 1572872 | tf_op jit(solution)/shard_map/ppermute | solution.py:348
  93.1 1.5 %collective-permute-done.9.refs_1_ = bf16[8,256,128]{2,1,0:T(8,128)(2,1)S(1)} collective-permute-done((bf16[8,256,128]{2,1,0:T(8,128)(2,1)S(1)}, bf16[8,256,128]{2,1,0:T(8,128)(2,1)S(1)}, u32[]{:S(2)}, u32[]{:S(2)}) %collective-permute-start.9) | collective-permute-done | bytes 524320 | tf_op jit(solution)/shard_map/ppermute | solution.py:348
  94.7 0.1 shard_map.121.refs_0_
  94.8 5.4 %collective-permute-start.10 = (bf16[8,256,128]{2,1,0:T(8,128)(2,1)S(1)}, bf16[8,256,128]{2,1,0:T(8,128)(2,1)S(1)}, u32[]{:S(2)}, u32[]{:S(2)}) collective-permute-start(bf16[8,256,128]{2,1,0:T(8,128)(2,1)S(1)} %shard_map.121.refs_0_), channel_id=1, source_target_pairs={{0,128},{64,192},{128,0},{192,64},{1,129},{65,193},{129,1},{193,65... | collective-permute-start | bytes 1572872 | tf_op jit(solution)/shard_map/ppermute | solution.py:348
  100.2 1.0 shard_map.119
  101.2 6.7 %all-to-all-start.2 = ((bf16[16,4,64,128]{3,2,1,0:T(8,128)(2,1)}), bf16[16,4,64,128]{3,2,1,0:T(8,128)(2,1)S(1)}, u32[]{:S(2)}, u32[]{:S(2)}) async-start(bf16[16,4,64,128]{3,2,1,0:T(8,128)(2,1)} %shard_map.119), calls=%async_computation.2 | async-start | bytes 2097152 | tf_op jit(solution)/shard_map/all_to_all | solution.py:342
  107.9 14.8 %collective-permute-done.10.refs_1_ = bf16[8,256,128]{2,1,0:T(8,128)(2,1)S(1)} collective-permute-done((bf16[8,256,128]{2,1,0:T(8,128)(2,1)S(1)}, bf16[8,256,128]{2,1,0:T(8,128)(2,1)S(1)}, u32[]{:S(2)}, u32[]{:S(2)}) %collective-permute-start.10) | collective-permute-done | bytes 524320 | tf_op jit(solution)/shard_map/ppermute | solution.py:348
  122.6 0.4 shard_map.122.refs_0_
  123.0 0.6 collective-permute-start.11
  123.6 0.0 copy-done.1
  123.6 0.7 copy.15.refs_1_
  124.3 0.0 all-to-all-done.2.refs_2_
  124.3 3.4 %shard_map.120 = bf16[128,4096]{1,0:T(8,128)(2,1)} custom-call(bf16[512,512]{1,0:T(8,128)(2,1)} %refs_0_.7, f32[128,1]{1,0:T(8,128)} %copy.15.refs_1_, bf16[16,4,64,128]{3,2,1,0:T(8,128)(2,1)S(1)} %all-to-all-done.2.refs_2_, bf16[128,4096]{1,0:T(8,128)(2,1)} %bitcast.9), custom_call_target="tpu_custom_call" | custom-call | tf_op jit(solution)/shard_map/pallas_call | solution.py:122
  127.7 0.0 collective-permute-done.11.refs_1_
  127.7 1.1 shard_map.123
  (1 shorter events, 0.0 us)
Async XLA Ops:
  3.8 21.8 %all-to-all-start = ((bf16[16,4,64,128]{3,2,1,0:T(8,128)(2,1)}), bf16[16,4,64,128]{3,2,1,0:T(8,128)(2,1)S(1)}, u32[]{:S(2)}, u32[]{:S(2)}) async-start(bf16[16,4,64,128]{3,2,1,0:T(8,128)(2,1)} %shard_map.113), calls=%async_computation | async-start | bytes 2097152 | tf_op jit(solution)/shard_map/all_to_all | solution.py:342
  13.7 16.0 %collective-permute-start.6 = (bf16[16,64,128]{2,1,0:T(8,128)(2,1)}, bf16[16,64,128]{2,1,0:T(8,128)(2,1)S(1)}, u32[]{:S(2)}, u32[]{:S(2)}) collective-permute-start(bf16[16,64,128]{2,1,0:T(8,128)(2,1)} %get-tuple-element.42), channel_id=1, source_target_pairs={{0,16},{1,17},{2,18},{3,19},{4,20},{5,21},{6,22},{7,23},{8,24},{9,... | collective-permute-start | bytes 786440 | tf_op jit(solution)/shard_map/ppermute | solution.py:331
  13.8 16.1 %collective-permute-start.7 = (bf16[16,64,128]{2,1,0:T(8,128)(2,1)}, bf16[16,64,128]{2,1,0:T(8,128)(2,1)S(1)}, u32[]{:S(2)}, u32[]{:S(2)}) collective-permute-start(bf16[16,64,128]{2,1,0:T(8,128)(2,1)} %get-tuple-element.43), channel_id=1, source_target_pairs={{0,32},{1,33},{2,34},{3,35},{4,36},{5,37},{6,38},{7,39},{8,40},{9,... | collective-permute-start | bytes 786440 | tf_op jit(solution)/shard_map/ppermute | solution.py:331
  16.9 2.8 %copy-start = (bf16[512,512]{1,0:T(8,128)(2,1)S(1)}, bf16[512,512]{1,0:T(8,128)(2,1)}, u32[]{:S(2)}) copy-start(bf16[512,512]{1,0:T(8,128)(2,1)} %param.13) | copy-start | bytes 1572868
  16.9 23.0 %collective-permute-start.8 = (bf16[16,64,128]{2,1,0:T(8,128)(2,1)S(1)}, bf16[16,64,128]{2,1,0:T(8,128)(2,1)S(1)}, u32[]{:S(2)}, u32[]{:S(2)}) collective-permute-start(bf16[16,64,128]{2,1,0:T(8,128)(2,1)S(1)} %get-tuple-element.44), channel_id=1, source_target_pairs={{0,48},{1,49},{2,50},{3,51},{4,52},{5,53},{6,54},{7,55},{8,56},{9,... | collective-permute-start | bytes 786440 | tf_op jit(solution)/shard_map/ppermute | solution.py:331
  26.5 27.9 %collective-permute-start = (bf16[16,64,128]{2,1,0:T(8,128)(2,1)}, bf16[16,64,128]{2,1,0:T(8,128)(2,1)S(1)}, u32[]{:S(2)}, u32[]{:S(2)}) collective-permute-start(bf16[16,64,128]{2,1,0:T(8,128)(2,1)} %get-tuple-element.32), channel_id=1, source_target_pairs={{0,16},{1,17},{2,18},{3,19},{4,20},{5,21},{6,22},{7,23},{8,24},{9,... | collective-permute-start | bytes 786440 | tf_op jit(solution)/shard_map/ppermute | solution.py:331
  26.6 28.8 %collective-permute-start.1 = (bf16[16,64,128]{2,1,0:T(8,128)(2,1)}, bf16[16,64,128]{2,1,0:T(8,128)(2,1)S(1)}, u32[]{:S(2)}, u32[]{:S(2)}) collective-permute-start(bf16[16,64,128]{2,1,0:T(8,128)(2,1)} %get-tuple-element.33), channel_id=1, source_target_pairs={{0,32},{1,33},{2,34},{3,35},{4,36},{5,37},{6,38},{7,39},{8,40},{9,... | collective-permute-start | bytes 786440 | tf_op jit(solution)/shard_map/ppermute | solution.py:331
  29.7 32.2 %collective-permute-start.2 = (bf16[16,64,128]{2,1,0:T(8,128)(2,1)S(1)}, bf16[16,64,128]{2,1,0:T(8,128)(2,1)}, u32[]{:S(2)}, u32[]{:S(2)}) collective-permute-start(bf16[16,64,128]{2,1,0:T(8,128)(2,1)S(1)} %get-tuple-element.34), channel_id=1, source_target_pairs={{0,48},{1,49},{2,50},{3,51},{4,52},{5,53},{6,54},{7,55},{8,56},{9,... | collective-permute-start | bytes 786440 | tf_op jit(solution)/shard_map/ppermute | solution.py:331
  41.0 28.0 %all-to-all-start.1 = ((bf16[16,4,64,128]{3,2,1,0:T(8,128)(2,1)}), bf16[16,4,64,128]{3,2,1,0:T(8,128)(2,1)S(1)}, u32[]{:S(2)}, u32[]{:S(2)}) async-start(bf16[16,4,64,128]{3,2,1,0:T(8,128)(2,1)} %shard_map.117), calls=%async_computation.1 | async-start | bytes 2097152 | tf_op jit(solution)/shard_map/all_to_all | solution.py:342
  66.2 6.6 %collective-permute-start.3 = (bf16[16,64,128]{2,1,0:T(8,128)(2,1)S(1)}, bf16[16,64,128]{2,1,0:T(8,128)(2,1)S(1)}, u32[]{:S(2)}, u32[]{:S(2)}) collective-permute-start(bf16[16,64,128]{2,1,0:T(8,128)(2,1)S(1)} %get-tuple-element.38), channel_id=1, source_target_pairs={{0,16},{1,17},{2,18},{3,19},{4,20},{5,21},{6,22},{7,23},{8,24},{9,... | collective-permute-start | bytes 786440 | tf_op jit(solution)/shard_map/ppermute | solution.py:331
  66.3 12.3 %collective-permute-start.4 = (bf16[16,64,128]{2,1,0:T(8,128)(2,1)S(1)}, bf16[16,64,128]{2,1,0:T(8,128)(2,1)S(1)}, u32[]{:S(2)}, u32[]{:S(2)}) collective-permute-start(bf16[16,64,128]{2,1,0:T(8,128)(2,1)S(1)} %get-tuple-element.39), channel_id=1, source_target_pairs={{0,32},{1,33},{2,34},{3,35},{4,36},{5,37},{6,38},{7,39},{8,40},{9,... | collective-permute-start | bytes 786440 | tf_op jit(solution)/shard_map/ppermute | solution.py:331
  68.8 20.8 %collective-permute-start.5 = (bf16[16,64,128]{2,1,0:T(8,128)(2,1)S(1)}, bf16[16,64,128]{2,1,0:T(8,128)(2,1)S(1)}, u32[]{:S(2)}, u32[]{:S(2)}) collective-permute-start(bf16[16,64,128]{2,1,0:T(8,128)(2,1)S(1)} %get-tuple-element.40), channel_id=1, source_target_pairs={{0,48},{1,49},{2,50},{3,51},{4,52},{5,53},{6,54},{7,55},{8,56},{9,... | collective-permute-start | bytes 786440 | tf_op jit(solution)/shard_map/ppermute | solution.py:331
  89.6 5.1 %collective-permute-start.9 = (bf16[8,256,128]{2,1,0:T(8,128)(2,1)S(1)}, bf16[8,256,128]{2,1,0:T(8,128)(2,1)S(1)}, u32[]{:S(2)}, u32[]{:S(2)}) collective-permute-start(bf16[8,256,128]{2,1,0:T(8,128)(2,1)S(1)} %get-tuple-element.53), channel_id=1, source_target_pairs={{0,64},{64,0},{128,192},{192,128},{1,65},{65,1},{129,193},{193,129... | collective-permute-start | bytes 1572872 | tf_op jit(solution)/shard_map/ppermute | solution.py:348
  94.8 27.8 %collective-permute-start.10 = (bf16[8,256,128]{2,1,0:T(8,128)(2,1)S(1)}, bf16[8,256,128]{2,1,0:T(8,128)(2,1)S(1)}, u32[]{:S(2)}, u32[]{:S(2)}) collective-permute-start(bf16[8,256,128]{2,1,0:T(8,128)(2,1)S(1)} %shard_map.121.refs_0_), channel_id=1, source_target_pairs={{0,128},{64,192},{128,0},{192,64},{1,129},{65,193},{129,1},{193,65... | collective-permute-start | bytes 1572872 | tf_op jit(solution)/shard_map/ppermute | solution.py:348
  101.2 23.2 %all-to-all-start.2 = ((bf16[16,4,64,128]{3,2,1,0:T(8,128)(2,1)}), bf16[16,4,64,128]{3,2,1,0:T(8,128)(2,1)S(1)}, u32[]{:S(2)}, u32[]{:S(2)}) async-start(bf16[16,4,64,128]{3,2,1,0:T(8,128)(2,1)} %shard_map.119), calls=%async_computation.2 | async-start | bytes 2097152 | tf_op jit(solution)/shard_map/all_to_all | solution.py:342
  107.8 15.8 %copy-start.1 = (f32[128]{0:T(128)S(1)}, f32[128]{0:T(128)}, u32[]{:S(2)}) copy-start(f32[128]{0:T(128)} %param.19) | copy-start | bytes 1540
  123.0 4.7 %collective-permute-start.11 = (bf16[1024,256]{1,0:T(8,128)(2,1)S(1)}, bf16[1024,256]{1,0:T(8,128)(2,1)S(1)}, u32[]{:S(2)}, u32[]{:S(2)}) collective-permute-start(bf16[1024,256]{1,0:T(8,128)(2,1)S(1)} %shard_map.122.refs_0_), channel_id=1, source_target_pairs={{0,64},{64,0},{128,192},{192,128},{1,65},{65,1},{129,193},{193,129... | collective-permute-start | bytes 1572872 | tf_op jit(solution)/shard_map/ppermute | solution.py:348

commit v3 on v2

--- a/solution.py
+++ b/solution.py
@@ -16,8 +16,7 @@
 PART = WIDTH // Z_LO
 MSG = ROWS * ROWS
 PAIRS = ROWS // 2
-MIDDLE_US = 60
-GRAD_US = 60
+EXCHANGE_US = 60
 
 NT = (((1,), (1,)), ((), ()))
 NN = (((1,), (0,)), ((), ()))
@@ -269,10 +268,11 @@
     o_ref = outs[0]
     z = my_z()
     step = YX * MSG
+    for e in range(Z_LO):
+        scr[e * step : (e + 1) * step, :] = s_ref[:, e].astype(F32).reshape(step, LANES)
     flow.wait(0)
     for e in range(Z_LO):
         fscr[e * PART : (e + 1) * PART, :] = f_ref[part(z, e), :]
-        scr[e * step : (e + 1) * step, :] = s_ref[:, e].astype(F32).reshape(step, LANES)
     flow.wait(1, 3)
     gains = g_ref[...]
     for r in range(ROWS):
@@ -285,30 +285,31 @@
 
 
 def add_body(flow, ins, results, outs):
-    outs[0][...] = (ins[0][...].astype(F32) + ins[1][...].astype(F32)).astype(BF16)
+    for n, out in enumerate(outs):
+        span = slice(n * LANES, (n + 1) * LANES)
+        out[...] = (ins[0][:, span].astype(F32) + ins[1][:, span].astype(F32)).astype(BF16)
 
 
 def total_body(flow, ins, results, outs, scr):
     a_ref, b_ref = ins
-    for side in range(2):
-        span = slice(side * LANES, (side + 1) * LANES)
-        for k in range(ROWS):
-            total = a_ref[k, span, :].astype(F32) + b_ref[k, span, :].astype(F32)
-            scr[pl.ds(k, LANES, stride=ROWS), :] = total.T
-        outs[0][:, span] = scr[...].astype(BF16)
+    for k in range(ROWS):
+        total = a_ref[k].astype(F32) + b_ref[k].astype(F32)
+        scr[pl.ds(k, LANES, stride=ROWS), :] = total.T
+    outs[0][...] = scr[...].astype(BF16)
 
 
 def join_body(flow, ins, results, outs):
     core = my_core()
-    outs[0][:, halves(core)] = ins[0][...]
-    outs[0][:, halves(1 - core)] = ins[1][...]
+    for n, block in enumerate(ins):
+        owner = core if n < 2 else 1 - core
+        place = pl.multiple_of(owner * HALF + (n % 2) * LANES, LANES)
+        outs[0][:, pl.ds(place, LANES)] = block[...]
     flow.start(outs[0], results[0])
 
 
 def gather_body(flow, ins, results, outs):
     for e, block in enumerate(ins):
-        outs[0][:, e] = block[...]
-        flow.start(outs[0].at[:, e], results[0].at[:, e])
+        flow.start(block, results[0].at[:, e])
 
 
 def spread_body(flow, ins, results, outs):
@@ -317,7 +318,9 @@
 
 
 def gathered(blocks):
-    return call(gather_body, [Far(WHOLE)], [], *blocks, copies=Z_LO)[0]
+    return call(
+        gather_body, [Far(WHOLE)], [], *blocks, copies=Z_LO, weight_us=EXCHANGE_US
+    )[0]
 
 
 def scattered(whole):
@@ -368,19 +371,25 @@
         first_body,
         [Far(WHOLE)],
         [SQUARE, TALL],
-        Far(factor_one),
-        Far(twiddle_in),
-        Far(signal),
+        factor_one,
+        twiddle_in,
+        signal,
         copies=Z_LO,
+        weight_us=EXCHANGE_US,
     )[0]
     back = call(back_body, [BLOCK] * Z_LO, [SQUARE, TALL], Far(factor_four), Far(upstream))
     filt = jnp.transpose(filter_freq, (1, 2, 0))
     gains = skip_gain.reshape(chans, 1)
-    moved, filt, two, three, gains = tied(
-        across_yx(sent), filt, factor_two.T, factor_three.T, gains
+    moved, back_whole, filt, two, three, gains = tied(
+        across_yx(sent),
+        gathered(across_z(back)),
+        filt,
+        factor_two.T,
+        factor_three.T,
+        gains,
     )
     got = across_z(scattered(moved))
-    back_got = across_yx(gathered(across_z(back)))
+    back_got = across_yx(back_whole)
 
     spread, *mixed = call(
         middle_body,
@@ -392,7 +401,7 @@
         Far(filt),
         Far(three),
         copies=PAIRS,
-        weight_us=MIDDLE_US,
+        weight_us=EXCHANGE_US,
     )
     half = struct((ROWS, HALF, LANES))
     keep, send = call(
@@ -403,28 +412,35 @@
         Far(twiddle_out),
         back_got,
         Far(spread),
-        weight_us=GRAD_US,
-    )
-    mixed_arrived, keep, send = tied(across_z(mixed), keep, send)
-    pair = call(add_body, [half], [], keep, swap(send, 1))[0]
-    far = swap(pair, 2)
-    returned = across_yx(gathered(mixed_arrived))
-    flat = struct((LANES * ROWS, HALF))
-    mine = call(total_body, [flat], [pltpu.VMEM((LANES * ROWS, LANES), F32)], pair, far)[0]
-    filter_grad = call(
-        join_body, [Far(struct((LANES * ROWS, WIDTH)))], [], mine, swap(mine, 1), copies=1
-    )[0]
-
+        weight_us=EXCHANGE_US,
+    )
+    mixed_whole = gathered(across_z(mixed))
+    quarter = struct((ROWS, LANES, LANES))
+    pairs = call(add_body, [quarter] * 2, [], keep, swap(send, 1))
+    mixed_whole, pairs = tied(mixed_whole, pairs)
+    returned = across_yx(mixed_whole)
+    flat = struct((LANES * ROWS, LANES))
+    far = [swap(pair, 2) for pair in pairs]
     outputs = call(
         last_body,
         [Far(struct((chans, local_len)))],
         [SQUARE, TALL],
-        Far(factor_four),
-        Far(gains),
+        factor_four,
+        gains,
         returned,
-        Far(signal),
+        signal,
         copies=ROWS,
     )[0]
+    far[1], outputs = tied(far[1], outputs)
+    mine = [
+        call(total_body, [flat], [pltpu.VMEM(flat.shape, F32)], pair, got_far, weight_us=weight)[0]
+        for pair, got_far, weight in zip(pairs, far, (0, 0))
+    ]
+    other = [swap(total, 1) for total in mine]
+    filter_grad = call(
+        join_body, [Far(struct((LANES * ROWS, WIDTH)))], [], *mine, *other, copies=1
+    )[0]
+
     return (
         outputs.reshape(batch, chans, local_len),
         filter_grad.reshape(chans, ROWS, WIDTH),

time: 131 us -> 120 us (0.916); the launches traced: 129 us -> 119 us
  waiting for transfers between devices: 54.7 us -> 47.7 us
  Pallas kernels: 21 us -> 18.1 us
    all_to_all x3, starting transfers between devices: 27 us -> 19.7 us  [across_yx(): lax.all_to_all(whole, 'seq', split_axis=0, concat_axis=0, axis_index_grou...]
    ppermute x3 -> x5, starting transfers between devices: 9.46 us -> 16.4 us  [swap(): return lax.ppermute(block, 'dp', [(i, i ^ bit) for i in range(4)])]
    ppermute x3 -> x5, waiting for transfers between devices: 16.3 us -> 10.3 us  [swap(): return lax.ppermute(block, 'dp', [(i, i ^ bit) for i in range(4)])]
    pallas_call x11 -> x12, Pallas kernels: 21 us -> 18.1 us  [call(): pl.pallas_call(wrapped, out_shape=[pltpu.HBM(o.shape, o.dtype) if n in fa...]
    all_to_all x3, waiting for transfers between devices: 2.85 us -> 0.01 us  [across_yx(): lax.all_to_all(whole, 'seq', split_axis=0, concat_axis=0, axis_index_grou...]
    ppermute x9, waiting for transfers between devices: 35.6 us -> 37.4 us  [across_z(): lax.ppermute(blocks[e], 'seq', [(i, i ^ e * YX) for i in range(Z_LO * YX)])]
    unnamed x7 -> x21, local copies, waits for them, and re-layouts: 5.73 us -> 6.77 us
  transfers between devices with their start and end apart: 15 -> 17, of which waited for: 9 -> 8; matrix products, arithmetic and copies ran while one was open for 5% -> 5% of each run, Pallas kernels for 13% -> 11%
where the time goes in v3:
time: 120 us; the launch traced here: 119 us
  waiting for transfers between devices  47.7 us (40%)
  starting transfers between devices  45.7 us (38%)
  Pallas kernels  18.1 us (15%)
  local copies, waits for them, and re-layouts  6.88 us (6%)
    ppermute x9, waiting for transfers between devices, across_z(): lax.ppermute(blocks[e], 'seq', [(i, i ^ e * YX) for i in range(Z_LO * YX)])  37.4 us
    all_to_all x3, starting transfers between devices, across_yx(): lax.all_to_all(whole, 'seq', split_axis=0, concat_axis=0, axis_index_grou...  19.7 us
    pallas_call x12, Pallas kernels, call(): pl.pallas_call(wrapped, out_shape=[pltpu.HBM(o.shape, o.dtype) if n in fa...  18.1 us
    ppermute x5, starting transfers between devices, swap(): return lax.ppermute(block, 'dp', [(i, i ^ bit) for i in range(4)])  16.4 us
    ppermute x5, waiting for transfers between devices, swap(): return lax.ppermute(block, 'dp', [(i, i ^ bit) for i in range(4)])  10.3 us
    ppermute x9, starting transfers between devices, across_z(): lax.ppermute(blocks[e], 'seq', [(i, i ^ e * YX) for i in range(Z_LO * YX)])  9.53 us
    unnamed x21, local copies, waits for them, and re-layouts  6.77 us
  transfers between devices with their start and end apart: 17, of which 8 were waited for; matrix products, arithmetic and copies ran while one was open for 5% of the time, Pallas kernels for 11%

profile of v3, /device:TPU:35, one launch (start us, length us, event | category | flops | bytes accessed | tf_op | source)
XLA Modules:
  0.0 119.4 jit_solution(17355015753678990677)
XLA Ops:
  0.6 0.0 copy-start.1
  0.7 2.4 %shard_map.114 = (bf16[16,64,128]{2,1,0:T(8,128)(2,1)S(1)}, bf16[16,64,128]{2,1,0:T(8,128)(2,1)S(1)}, bf16[16,64,128]{2,1,0:T(8,128)(2,1)S(1)}, bf16[16,64,128]{2,1,0:T(8,128)(2,1)S(1)}) custom-call(bf16[512,512]{1,0:T(8,128)(2,1)} %refs_0_.7, bf16[128,4096]{1,0:T(8,128)(2,1)} %bitcast.11), custom_call_target="tpu_custom_call" | custom-call | tf_op jit(solution)/shard_map/pallas_call | solution.py:121
  3.1 0.1 collective-permute-start
  3.2 3.1 %collective-permute-start.1 = (bf16[16,64,128]{2,1,0:T(8,128)(2,1)S(1)}, bf16[16,64,128]{2,1,0:T(8,128)(2,1)S(1)}, u32[]{:S(2)}, u32[]{:S(2)}) collective-permute-start(bf16[16,64,128]{2,1,0:T(8,128)(2,1)S(1)} %get-tuple-element.32), channel_id=1, source_target_pairs={{0,32},{1,33},{2,34},{3,35},{4,36},{5,37},{6,38},{7,39},{8,40},{9,... | collective-permute-start | bytes 786440 | tf_op jit(solution)/shard_map/ppermute | solution.py:334
  6.3 0.2 collective-permute-start.2
  6.5 1.9 %shard_map.113 = bf16[16,4,64,128]{3,2,1,0:T(8,128)(2,1)} custom-call(bf16[512,512]{1,0:T(8,128)(2,1)S(1)} %copy-done.5, bf16[8,512]{1,0:T(8,128)(2,1)S(1)} %copy-done.6, bf16[128,4096]{1,0:T(8,128)(2,1)S(1)} %bitcast.8), custom_call_target="tpu_custom_call" | custom-call | flops 60000002048 | bytes 180000000 | tf_op jit(solution)/shard_map/pallas_call | solution.py:121
  8.3 6.9 %all-to-all-start = ((bf16[16,4,64,128]{3,2,1,0:T(8,128)(2,1)}), bf16[16,4,64,128]{3,2,1,0:T(8,128)(2,1)S(1)}, u32[]{:S(2)}, u32[]{:S(2)}) async-start(bf16[16,4,64,128]{3,2,1,0:T(8,128)(2,1)} %shard_map.113), calls=%async_computation | async-start | bytes 2097152 | tf_op jit(solution)/shard_map/all_to_all | solution.py:345
  15.3 2.7 %copy.12 = bf16[128,8,512]{0,2,1:T(8,128)(2,1)} copy(bf16[128,8,512]{2,1,0:T(8,128)(2,1)} %param.18) | data formatting | bytes 2097152 | tf_op args[8]
  18.0 1.0 copy.13
  19.0 2.0 %copy.14 = bf16[512,512]{0,1:T(8,128)(2,1)} copy(bf16[512,512]{1,0:T(8,128)(2,1)} %refs_0_.6) | data formatting | bytes 1048576 | tf_op args[4]
  21.1 1.4 %collective-permute-done.1.refs_2_ = bf16[16,64,128]{2,1,0:T(8,128)(2,1)S(1)} collective-permute-done((bf16[16,64,128]{2,1,0:T(8,128)(2,1)S(1)}, bf16[16,64,128]{2,1,0:T(8,128)(2,1)S(1)}, u32[]{:S(2)}, u32[]{:S(2)}) %collective-permute-start.1) | collective-permute-done | bytes 262176 | tf_op jit(solution)/shard_map/ppermute | solution.py:334
  22.4 6.7 %collective-permute-done.2.refs_3_ = bf16[16,64,128]{2,1,0:T(8,128)(2,1)S(1)} collective-permute-done((bf16[16,64,128]{2,1,0:T(8,128)(2,1)S(1)}, bf16[16,64,128]{2,1,0:T(8,128)(2,1)S(1)}, u32[]{:S(2)}, u32[]{:S(2)}) %collective-permute-start.2) | collective-permute-done | bytes 262176 | tf_op jit(solution)/shard_map/ppermute | solution.py:334
  29.1 1.0 shard_map.115
  30.2 0.1 shard_map.116
  30.3 0.8 collective-permute-start.3
  31.0 2.2 %collective-permute-start.4 = (bf16[16,64,128]{2,1,0:T(8,128)(2,1)S(1)}, bf16[16,64,128]{2,1,0:T(8,128)(2,1)S(1)}, u32[]{:S(2)}, u32[]{:S(2)}) collective-permute-start(bf16[16,64,128]{2,1,0:T(8,128)(2,1)S(1)} %get-tuple-element.38), channel_id=1, source_target_pairs={{0,32},{1,33},{2,34},{3,35},{4,36},{5,37},{6,38},{7,39},{8,40},{9,... | collective-permute-start | bytes 786440 | tf_op jit(solution)/shard_map/ppermute | solution.py:334
  33.2 0.2 collective-permute-start.5
  33.4 6.5 %all-to-all-start.1 = ((bf16[16,4,64,128]{3,2,1,0:T(8,128)(2,1)}), bf16[16,4,64,128]{3,2,1,0:T(8,128)(2,1)S(1)}, u32[]{:S(2)}, u32[]{:S(2)}) async-start(bf16[16,4,64,128]{3,2,1,0:T(8,128)(2,1)} %shard_map.115), calls=%async_computation.1 | async-start | bytes 2097152 | tf_op jit(solution)/shard_map/all_to_all | solution.py:345
  39.9 0.0 collective-permute-done.3.refs_3_
  39.9 2.4 %collective-permute-done.4.refs_4_ = bf16[16,64,128]{2,1,0:T(8,128)(2,1)S(1)} collective-permute-done((bf16[16,64,128]{2,1,0:T(8,128)(2,1)S(1)}, bf16[16,64,128]{2,1,0:T(8,128)(2,1)S(1)}, u32[]{:S(2)}, u32[]{:S(2)}) %collective-permute-start.4) | collective-permute-done | bytes 262176 | tf_op jit(solution)/shard_map/ppermute | solution.py:334
  42.3 12.0 %collective-permute-done.5.refs_5_ = bf16[16,64,128]{2,1,0:T(8,128)(2,1)S(1)} collective-permute-done((bf16[16,64,128]{2,1,0:T(8,128)(2,1)S(1)}, bf16[16,64,128]{2,1,0:T(8,128)(2,1)S(1)}, u32[]{:S(2)}, u32[]{:S(2)}) %collective-permute-start.5) | collective-permute-done | bytes 262176 | tf_op jit(solution)/shard_map/ppermute | solution.py:334
  54.3 3.3 %shard_map.117 = (bf16[8,512,128]{2,1,0:T(8,128)(2,1)}, bf16[16,64,128]{2,1,0:T(8,128)(2,1)S(1)}, bf16[16,64,128]{2,1,0:T(8,128)(2,1)S(1)}, bf16[16,64,128]{2,1,0:T(8,128)(2,1)S(1)}, bf16[16,64,128]{2,1,0:T(8,128)(2,1)S(1)}) custom-call(bf16[512,512]{1,0:T(8,128)(2,1)} %bitcast.14, bf16[8,512]{1,0:T(8,128)(2,1)} %refs_1_.5, ...), custom_call_target="tpu_custom_call" | custom-call | flops 60000002048 | bytes 180000000 | tf_op jit(solution)/shard_map/pallas_call | solution.py:121
  57.6 0.1 collective-permute-start.6
  57.7 3.0 %collective-permute-start.7 = (bf16[16,64,128]{2,1,0:T(8,128)(2,1)S(1)}, bf16[16,64,128]{2,1,0:T(8,128)(2,1)S(1)}, u32[]{:S(2)}, u32[]{:S(2)}) collective-permute-start(bf16[16,64,128]{2,1,0:T(8,128)(2,1)S(1)} %get-tuple-element.44), channel_id=1, source_target_pairs={{0,32},{1,33},{2,34},{3,35},{4,36},{5,37},{6,38},{7,39},{8,40},{9,... | collective-permute-start | bytes 786440 | tf_op jit(solution)/shard_map/ppermute | solution.py:334
  60.7 0.0 collective-permute-start.8
  60.7 2.6 %shard_map.119 = (bf16[8,256,128]{2,1,0:T(8,128)(2,1)S(1)}, bf16[8,256,128]{2,1,0:T(8,128)(2,1)S(1)}) custom-call(bf16[512,512]{1,0:T(8,128)(2,1)} %refs_0_.6, bf16[8,512]{1,0:T(8,128)(2,1)} %refs_1_.5, bf16[16,4,64,128]{3,2,1,0:T(8,128)(2,1)S(1)} %all-to-all-done.1.refs_2_, bf16[8,512,128]{2,1,0:T(8,128)(2,1)} %get-tuple-element.47.refs_3_), custom_call_target="tpu_custom_call" | custom-call | flops 60000002048 | bytes 180000000 | tf_op jit(solution)/shard_map/pallas_call | solution.py:121
  63.3 3.8 %collective-permute-start.9 = (bf16[8,256,128]{2,1,0:T(8,128)(2,1)S(1)}, bf16[8,256,128]{2,1,0:T(8,128)(2,1)S(1)}, u32[]{:S(2)}, u32[]{:S(2)}) collective-permute-start(bf16[8,256,128]{2,1,0:T(8,128)(2,1)S(1)} %get-tuple-element.49), channel_id=1, source_target_pairs={{0,64},{64,0},{128,192},{192,128},{1,65},{65,1},{129,193},{193,129... | collective-permute-start | bytes 1572872 | tf_op jit(solution)/shard_map/ppermute | solution.py:351
  67.1 2.6 %collective-permute-done.7.refs_2_ = bf16[16,64,128]{2,1,0:T(8,128)(2,1)S(1)} collective-permute-done((bf16[16,64,128]{2,1,0:T(8,128)(2,1)S(1)}, bf16[16,64,128]{2,1,0:T(8,128)(2,1)S(1)}, u32[]{:S(2)}, u32[]{:S(2)}) %collective-permute-start.7) | collective-permute-done | bytes 262176 | tf_op jit(solution)/shard_map/ppermute | solution.py:334
  69.7 12.3 %collective-permute-done.8.refs_3_ = bf16[16,64,128]{2,1,0:T(8,128)(2,1)S(1)} collective-permute-done((bf16[16,64,128]{2,1,0:T(8,128)(2,1)S(1)}, bf16[16,64,128]{2,1,0:T(8,128)(2,1)S(1)}, u32[]{:S(2)}, u32[]{:S(2)}) %collective-permute-start.8) | collective-permute-done | bytes 262176 | tf_op jit(solution)/shard_map/ppermute | solution.py:334
  82.0 1.0 shard_map.118
  83.0 0.1 shard_map.120
  83.2 0.0 copy-start.3
  83.2 0.0 copy-start.8
  83.2 0.0 copy-start.2
  83.2 6.3 %all-to-all-start.2 = ((bf16[16,4,64,128]{3,2,1,0:T(8,128)(2,1)}), bf16[16,4,64,128]{3,2,1,0:T(8,128)(2,1)S(1)}, u32[]{:S(2)}, u32[]{:S(2)}) async-start(bf16[16,4,64,128]{3,2,1,0:T(8,128)(2,1)} %shard_map.118), calls=%async_computation.2 | async-start | bytes 2097152 | tf_op jit(solution)/shard_map/all_to_all | solution.py:345
  89.5 0.0 copy-start
  89.5 5.5 %collective-permute-start.11 = (bf16[8,128,128]{2,1,0:T(8,128)(2,1)S(1)}, bf16[8,128,128]{2,1,0:T(8,128)(2,1)}, u32[]{:S(2)}, u32[]{:S(2)}) collective-permute-start(bf16[8,128,128]{2,1,0:T(8,128)(2,1)S(1)} %get-tuple-element.56.refs_0_), channel_id=1, source_target_pairs={{0,128},{64,192},{128,0},{192,64},{1,129},{65,193},{129,1},{193,65... | collective-permute-start | bytes 786440 | tf_op jit(solution)/shard_map/ppermute | solution.py:351
  95.0 0.1 collective-permute-start.10
  95.1 0.1 copy.15.refs_1_
  95.2 9.1 %collective-permute-done.11.refs_1_ = bf16[8,128,128]{2,1,0:T(8,128)(2,1)} collective-permute-done((bf16[8,128,128]{2,1,0:T(8,128)(2,1)S(1)}, bf16[8,128,128]{2,1,0:T(8,128)(2,1)}, u32[]{:S(2)}, u32[]{:S(2)}) %collective-permute-start.11) | collective-permute-done | bytes 262176 | tf_op jit(solution)/shard_map/ppermute | solution.py:351
  104.4 0.9 copy-done.4
  105.3 1.2 shard_map.122.refs_0_
  106.5 5.7 %collective-permute-start.12 = (bf16[1024,128]{1,0:T(8,128)(2,1)S(1)}, bf16[1024,128]{1,0:T(8,128)(2,1)}, u32[]{:S(2)}, u32[]{:S(2)}) collective-permute-start(bf16[1024,128]{1,0:T(8,128)(2,1)S(1)} %shard_map.122.refs_0_), channel_id=1, source_target_pairs={{0,64},{64,0},{128,192},{192,128},{1,65},{65,1},{129,193},{193,129... | collective-permute-start | bytes 786440 | tf_op jit(solution)/shard_map/ppermute | solution.py:351
  112.2 2.1 %shard_map.121 = bf16[128,4096]{1,0:T(8,128)(2,1)} custom-call(bf16[512,512]{1,0:T(8,128)(2,1)S(1)} %copy-done, f32[128,1]{1,0:T(8,128)S(1)} %copy.15.refs_1_, bf16[16,4,64,128]{3,2,1,0:T(8,128)(2,1)S(1)} %all-to-all-done.2.refs_2_, bf16[128,4096]{1,0:T(8,128)(2,1)S(1)} %bitcast.9), custom_call_target="tpu_custom_call" | custom-call | tf_op jit(solution)/shard_map/pallas_call | solution.py:121
  114.3 0.2 shard_map.123.refs_1_
  114.5 1.4 %collective-permute-start.13 = (bf16[1024,128]{1,0:T(8,128)(2,1)S(1)}, bf16[1024,128]{1,0:T(8,128)(2,1)S(1)}, u32[]{:S(2)}, u32[]{:S(2)}) collective-permute-start(bf16[1024,128]{1,0:T(8,128)(2,1)S(1)} %shard_map.123.refs_1_), channel_id=1, source_target_pairs={{0,64},{64,0},{128,192},{192,128},{1,65},{65,1},{129,193},{193,129... | collective-permute-start | bytes 786440 | tf_op jit(solution)/shard_map/ppermute | solution.py:351
  115.9 1.2 collective-permute-done.13.refs_3_
  117.1 2.2 %shard_map.124 = bf16[1024,512]{1,0:T(8,128)(2,1)} custom-call(bf16[1024,128]{1,0:T(8,128)(2,1)S(1)} %shard_map.122.refs_0_, bf16[1024,128]{1,0:T(8,128)(2,1)S(1)} %shard_map.123.refs_1_, bf16[1024,128]{1,0:T(8,128)(2,1)} %collective-permute-done.12.refs_2_, bf16[1024,128]{1,0:T(8,128)(2,1)S(1)} %collective-permute-done.13.refs_3_), custom_call_target="tpu_custom_call" | custom-call | tf_op jit(solution)/shard_map/pallas_call | solution.py:121
  (20 shorter events, 0.0 us)
Async XLA Ops:
  0.6 5.8 %copy-start.1 = (bf16[1,128,4096]{2,1,0:T(8,128)(2,1)S(1)}, bf16[1,128,4096]{2,1,0:T(8,128)(2,1)}, u32[]{:S(2)}) copy-start(bf16[1,128,4096]{2,1,0:T(8,128)(2,1)} %param.10) | copy-start | bytes 3145732
  0.6 5.8 %copy-start.5 = (bf16[512,512]{1,0:T(8,128)(2,1)S(1)}, bf16[512,512]{1,0:T(8,128)(2,1)}, u32[]{:S(2)}) copy-start(bf16[512,512]{1,0:T(8,128)(2,1)} %refs_0_.4) | copy-start | bytes 1572868
  0.7 5.8 %copy-start.6 = (bf16[8,512]{1,0:T(8,128)(2,1)S(1)}, bf16[8,512]{1,0:T(8,128)(2,1)}, u32[]{:S(2)}) copy-start(bf16[8,512]{1,0:T(8,128)(2,1)} %refs_1_.3) | copy-start | bytes 24580
  3.1 18.0 %collective-permute-start = (bf16[16,64,128]{2,1,0:T(8,128)(2,1)S(1)}, bf16[16,64,128]{2,1,0:T(8,128)(2,1)S(1)}, u32[]{:S(2)}, u32[]{:S(2)}) collective-permute-start(bf16[16,64,128]{2,1,0:T(8,128)(2,1)S(1)} %get-tuple-element.31), channel_id=1, source_target_pairs={{0,16},{1,17},{2,18},{3,19},{4,20},{5,21},{6,22},{7,23},{8,24},{9,... | collective-permute-start | bytes 786440 | tf_op jit(solution)/shard_map/ppermute | solution.py:334
  3.2 19.2 %collective-permute-start.1 = (bf16[16,64,128]{2,1,0:T(8,128)(2,1)S(1)}, bf16[16,64,128]{2,1,0:T(8,128)(2,1)S(1)}, u32[]{:S(2)}, u32[]{:S(2)}) collective-permute-start(bf16[16,64,128]{2,1,0:T(8,128)(2,1)S(1)} %get-tuple-element.32), channel_id=1, source_target_pairs={{0,32},{1,33},{2,34},{3,35},{4,36},{5,37},{6,38},{7,39},{8,40},{9,... | collective-permute-start | bytes 786440 | tf_op jit(solution)/shard_map/ppermute | solution.py:334
  6.3 22.8 %collective-permute-start.2 = (bf16[16,64,128]{2,1,0:T(8,128)(2,1)S(1)}, bf16[16,64,128]{2,1,0:T(8,128)(2,1)S(1)}, u32[]{:S(2)}, u32[]{:S(2)}) collective-permute-start(bf16[16,64,128]{2,1,0:T(8,128)(2,1)S(1)} %get-tuple-element.33), channel_id=1, source_target_pairs={{0,48},{1,49},{2,50},{3,51},{4,52},{5,53},{6,54},{7,55},{8,56},{9,... | collective-permute-start | bytes 786440 | tf_op jit(solution)/shard_map/ppermute | solution.py:334
  8.3 21.8 %all-to-all-start = ((bf16[16,4,64,128]{3,2,1,0:T(8,128)(2,1)}), bf16[16,4,64,128]{3,2,1,0:T(8,128)(2,1)S(1)}, u32[]{:S(2)}, u32[]{:S(2)}) async-start(bf16[16,4,64,128]{3,2,1,0:T(8,128)(2,1)} %shard_map.113), calls=%async_computation | async-start | bytes 2097152 | tf_op jit(solution)/shard_map/all_to_all | solution.py:345
  15.3 2.7 %copy-start.7 = (bf16[512,512]{1,0:T(8,128)(2,1)S(1)}, bf16[512,512]{1,0:T(8,128)(2,1)}, u32[]{:S(2)}) copy-start(bf16[512,512]{1,0:T(8,128)(2,1)} %param.13) | copy-start | bytes 1572868
  30.3 9.7 %collective-permute-start.3 = (bf16[16,64,128]{2,1,0:T(8,128)(2,1)S(1)}, bf16[16,64,128]{2,1,0:T(8,128)(2,1)S(1)}, u32[]{:S(2)}, u32[]{:S(2)}) collective-permute-start(bf16[16,64,128]{2,1,0:T(8,128)(2,1)S(1)} %get-tuple-element.37), channel_id=1, source_target_pairs={{0,16},{1,17},{2,18},{3,19},{4,20},{5,21},{6,22},{7,23},{8,24},{9,... | collective-permute-start | bytes 786440 | tf_op jit(solution)/shard_map/ppermute | solution.py:334
  31.0 11.3 %collective-permute-start.4 = (bf16[16,64,128]{2,1,0:T(8,128)(2,1)S(1)}, bf16[16,64,128]{2,1,0:T(8,128)(2,1)S(1)}, u32[]{:S(2)}, u32[]{:S(2)}) collective-permute-start(bf16[16,64,128]{2,1,0:T(8,128)(2,1)S(1)} %get-tuple-element.38), channel_id=1, source_target_pairs={{0,32},{1,33},{2,34},{3,35},{4,36},{5,37},{6,38},{7,39},{8,40},{9,... | collective-permute-start | bytes 786440 | tf_op jit(solution)/shard_map/ppermute | solution.py:334
  33.2 21.1 %collective-permute-start.5 = (bf16[16,64,128]{2,1,0:T(8,128)(2,1)S(1)}, bf16[16,64,128]{2,1,0:T(8,128)(2,1)S(1)}, u32[]{:S(2)}, u32[]{:S(2)}) collective-permute-start(bf16[16,64,128]{2,1,0:T(8,128)(2,1)S(1)} %get-tuple-element.39), channel_id=1, source_target_pairs={{0,48},{1,49},{2,50},{3,51},{4,52},{5,53},{6,54},{7,55},{8,56},{9,... | collective-permute-start | bytes 786440 | tf_op jit(solution)/shard_map/ppermute | solution.py:334
  33.4 27.4 %all-to-all-start.1 = ((bf16[16,4,64,128]{3,2,1,0:T(8,128)(2,1)}), bf16[16,4,64,128]{3,2,1,0:T(8,128)(2,1)S(1)}, u32[]{:S(2)}, u32[]{:S(2)}) async-start(bf16[16,4,64,128]{3,2,1,0:T(8,128)(2,1)} %shard_map.115), calls=%async_computation.1 | async-start | bytes 2097152 | tf_op jit(solution)/shard_map/all_to_all | solution.py:345
  57.6 9.5 %collective-permute-start.6 = (bf16[16,64,128]{2,1,0:T(8,128)(2,1)S(1)}, bf16[16,64,128]{2,1,0:T(8,128)(2,1)S(1)}, u32[]{:S(2)}, u32[]{:S(2)}) collective-permute-start(bf16[16,64,128]{2,1,0:T(8,128)(2,1)S(1)} %get-tuple-element.43), channel_id=1, source_target_pairs={{0,16},{1,17},{2,18},{3,19},{4,20},{5,21},{6,22},{7,23},{8,24},{9,... | collective-permute-start | bytes 786440 | tf_op jit(solution)/shard_map/ppermute | solution.py:334
  57.7 12.0 %collective-permute-start.7 = (bf16[16,64,128]{2,1,0:T(8,128)(2,1)S(1)}, bf16[16,64,128]{2,1,0:T(8,128)(2,1)S(1)}, u32[]{:S(2)}, u32[]{:S(2)}) collective-permute-start(bf16[16,64,128]{2,1,0:T(8,128)(2,1)S(1)} %get-tuple-element.44), channel_id=1, source_target_pairs={{0,32},{1,33},{2,34},{3,35},{4,36},{5,37},{6,38},{7,39},{8,40},{9,... | collective-permute-start | bytes 786440 | tf_op jit(solution)/shard_map/ppermute | solution.py:334
  60.7 21.3 %collective-permute-start.8 = (bf16[16,64,128]{2,1,0:T(8,128)(2,1)S(1)}, bf16[16,64,128]{2,1,0:T(8,128)(2,1)S(1)}, u32[]{:S(2)}, u32[]{:S(2)}) collective-permute-start(bf16[16,64,128]{2,1,0:T(8,128)(2,1)S(1)} %get-tuple-element.45), channel_id=1, source_target_pairs={{0,48},{1,49},{2,50},{3,51},{4,52},{5,53},{6,54},{7,55},{8,56},{9,... | collective-permute-start | bytes 786440 | tf_op jit(solution)/shard_map/ppermute | solution.py:334
  63.3 19.7 %collective-permute-start.9 = (bf16[8,256,128]{2,1,0:T(8,128)(2,1)S(1)}, bf16[8,256,128]{2,1,0:T(8,128)(2,1)S(1)}, u32[]{:S(2)}, u32[]{:S(2)}) collective-permute-start(bf16[8,256,128]{2,1,0:T(8,128)(2,1)S(1)} %get-tuple-element.49), channel_id=1, source_target_pairs={{0,64},{64,0},{128,192},{192,128},{1,65},{65,1},{129,193},{193,129... | collective-permute-start | bytes 1572872 | tf_op jit(solution)/shard_map/ppermute | solution.py:351
  83.2 6.3 %copy-start.3 = (bf16[8,128,128]{2,1,0:T(8,128)(2,1)}, bf16[8,128,128]{2,1,0:T(8,128)(2,1)S(1)}, u32[]{:S(2)}) copy-start(bf16[8,128,128]{2,1,0:T(8,128)(2,1)S(1)} %get-tuple-element.56.refs_0_) | copy-start | bytes 786436
  83.2 11.9 %copy-start.8 = (f32[128]{0:T(128)S(1)}, f32[128]{0:T(128)}, u32[]{:S(2)}) copy-start(f32[128]{0:T(128)} %param.19) | copy-start | bytes 1540
  83.2 29.0 %copy-start.2 = (bf16[1,128,4096]{2,1,0:T(8,128)(2,1)S(1)}, bf16[1,128,4096]{2,1,0:T(8,128)(2,1)}, u32[]{:S(2)}) copy-start(bf16[1,128,4096]{2,1,0:T(8,128)(2,1)} %param.10) | copy-start | bytes 3145732
  83.2 29.0 %all-to-all-start.2 = ((bf16[16,4,64,128]{3,2,1,0:T(8,128)(2,1)}), bf16[16,4,64,128]{3,2,1,0:T(8,128)(2,1)S(1)}, u32[]{:S(2)}, u32[]{:S(2)}) async-start(bf16[16,4,64,128]{3,2,1,0:T(8,128)(2,1)} %shard_map.118), calls=%async_computation.2 | async-start | bytes 2097152 | tf_op jit(solution)/shard_map/all_to_all | solution.py:345
  89.5 22.7 %copy-start = (bf16[512,512]{1,0:T(8,128)(2,1)S(1)}, bf16[512,512]{1,0:T(8,128)(2,1)}, u32[]{:S(2)}) copy-start(bf16[512,512]{1,0:T(8,128)(2,1)} %refs_0_.7) | copy-start | bytes 1572868
  89.5 14.9 %collective-permute-start.11 = (bf16[8,128,128]{2,1,0:T(8,128)(2,1)S(1)}, bf16[8,128,128]{2,1,0:T(8,128)(2,1)}, u32[]{:S(2)}, u32[]{:S(2)}) collective-permute-start(bf16[8,128,128]{2,1,0:T(8,128)(2,1)S(1)} %get-tuple-element.56.refs_0_), channel_id=1, source_target_pairs={{0,128},{64,192},{128,0},{192,64},{1,129},{65,193},{129,1},{193,65... | collective-permute-start | bytes 786440 | tf_op jit(solution)/shard_map/ppermute | solution.py:351
  95.0 19.3 %collective-permute-start.10 = (bf16[8,128,128]{2,1,0:T(8,128)(2,1)S(1)}, bf16[8,128,128]{2,1,0:T(8,128)(2,1)S(1)}, u32[]{:S(2)}, u32[]{:S(2)}) collective-permute-start(bf16[8,128,128]{2,1,0:T(8,128)(2,1)S(1)} %get-tuple-element.52.refs_0_), channel_id=1, source_target_pairs={{0,128},{64,192},{128,0},{192,64},{1,129},{65,193},{129,1},{193,65... | collective-permute-start | bytes 786440 | tf_op jit(solution)/shard_map/ppermute | solution.py:351
  104.4 1.0 copy-start.4
  106.5 9.4 %collective-permute-start.12 = (bf16[1024,128]{1,0:T(8,128)(2,1)S(1)}, bf16[1024,128]{1,0:T(8,128)(2,1)}, u32[]{:S(2)}, u32[]{:S(2)}) collective-permute-start(bf16[1024,128]{1,0:T(8,128)(2,1)S(1)} %shard_map.122.refs_0_), channel_id=1, source_target_pairs={{0,64},{64,0},{128,192},{192,128},{1,65},{65,1},{129,193},{193,129... | collective-permute-start | bytes 786440 | tf_op jit(solution)/shard_map/ppermute | solution.py:351
  114.5 2.5 %collective-permute-start.13 = (bf16[1024,128]{1,0:T(8,128)(2,1)S(1)}, bf16[1024,128]{1,0:T(8,128)(2,1)S(1)}, u32[]{:S(2)}, u32[]{:S(2)}) collective-permute-start(bf16[1024,128]{1,0:T(8,128)(2,1)S(1)} %shard_map.123.refs_1_), channel_id=1, source_target_pairs={{0,64},{64,0},{128,192},{192,128},{1,65},{65,1},{129,193},{193,129... | collective-permute-start | bytes 786440 | tf_op jit(solution)/shard_map/ppermute | solution.py:351

commit v4 on v3

--- a/solution.py
+++ b/solution.py
@@ -89,7 +89,7 @@
         self.pinned = pinned
 
 
-def call(body, outs, scratch, *args, copies=0, weight_us=0):
+def call(body, outs, scratch, *args, copies=0, weight_us=0, fetch=None, aliases=None):
     n_in, n_out = len(args), len(outs)
     far_in = [n for n, a in enumerate(args) if isinstance(a, Far)]
     far_out = [n for n, o in enumerate(outs) if isinstance(o, Far)]
@@ -103,12 +103,14 @@
     def space(n):
         return hbm if n in pinned else free if n in far_in else vmem
 
+    fetched = [n for n in far_in if fetch is None or n in fetch]
+
     def wrapped(*refs):
         refs = list(refs)
         ins, refs = refs[:n_in], refs[n_in:]
         results, refs = refs[:n_out], refs[n_out:]
         flow = Copies(refs.pop(0))
-        for n in far_in:
+        for n in fetched:
             near = refs.pop(0)
             flow.fetch(n, ins[n], near)
             ins[n] = near
@@ -126,9 +128,10 @@
         in_specs=[space(n) for n in range(n_in)],
         out_specs=[hbm if n in far_out else vmem for n in range(n_out)],
         scratch_shapes=[pltpu.SemaphoreType.DMA((max(1, len(far_in) + copies),))]
-        + [pltpu.VMEM(args[n].shape, args[n].dtype) for n in far_in]
+        + [pltpu.VMEM(args[n].shape, args[n].dtype) for n in fetched]
         + [pltpu.VMEM(outs[n].shape, outs[n].dtype) for n in far_out]
         + scratch,
+        input_output_aliases=aliases or {},
         compiler_params=pltpu.CompilerParams(vmem_limit_bytes=16 * 1024 * 1024),
         cost_estimate=pl.CostEstimate(
             flops=weight_us * 10**9, bytes_accessed=weight_us * 3 * 10**6, transcendentals=0
@@ -204,28 +207,34 @@
     )
 
 
-def middle_body(flow, ins, results, outs, f2s, f3s):
+def middle_body(flow, ins, results, outs, f2s, f3s, cols_scr, mid_scr):
     f2t_ref, tw_ref, u0, u1, u2, u3, filt_ref, f3t_ref = ins
     zt_ref, *blocks = outs
     z = my_z()
-    flow.wait(0, 1)
+    for pair in range(PAIRS):
+        cols = columns((u0, u1, u2, u3), pair)
+        for half in range(2):
+            span = slice(half * LANES, (half + 1) * LANES)
+            cols_scr[pair, :, span] = cols[half].astype(BF16)
+    flow.wait(0)
     for e in range(Z_LO):
         f2s[:, e * PART : (e + 1) * PART] = f2t_ref[:, part(z, e)]
-    twist = twist_columns(tw_ref, z)
     for pair in range(PAIRS):
         k = 2 * pair
-        cols = columns((u0, u1, u2, u3), pair)
-        rhs = jnp.concatenate([c.astype(BF16) for c in cols], axis=1)
-        spread = dot(f2s[...], rhs).astype(BF16)
+        spread = dot(f2s[...], cols_scr[pair]).astype(BF16)
         zt_ref[k] = spread[:, :LANES]
         zt_ref[k + 1] = spread[:, LANES:]
-        if pair == 0:
-            flow.wait(6, 7)
-            for e in range(Z_LO):
-                f3s[e * PART : (e + 1) * PART, :] = f3t_ref[part(z, e), :]
+        flow.start(zt_ref.at[k : k + 2], results[0].at[k : k + 2])
+        flow.wait(6)
         filt = jnp.concatenate([filt_ref[k], filt_ref[k + 1]], axis=1)
-        filtered = (spread.astype(F32) * filt.astype(F32)).astype(BF16)
-        third = dot(f3s[...], filtered)
+        mid_scr[pair] = (spread.astype(F32) * filt.astype(F32)).astype(BF16)
+    flow.wait(1, 7)
+    twist = twist_columns(tw_ref, z)
+    for e in range(Z_LO):
+        f3s[e * PART : (e + 1) * PART, :] = f3t_ref[part(z, e), :]
+    for pair in range(PAIRS):
+        k = 2 * pair
+        third = dot(f3s[...], mid_scr[pair])
         first = third[:, :LANES] * twist[:, k : k + 1]
         second = third[:, LANES:] * twist[:, k + 1 : k + 2]
         shaped = jnp.concatenate(
@@ -235,7 +244,6 @@
         rows = slice(pair * 16, (pair + 1) * 16)
         for e, block in enumerate(blocks):
             block[:, rows, :] = shaped[e * YX : (e + 1) * YX]
-        flow.start(zt_ref.at[k : k + 2], results[0].at[k : k + 2])
 
 
 def grad_body(flow, ins, results, outs, f3s):
@@ -298,13 +306,19 @@
     outs[0][...] = scr[...].astype(BF16)
 
 
-def join_body(flow, ins, results, outs):
+def place(flow, chunk, blocks, whole):
     core = my_core()
-    for n, block in enumerate(ins):
-        owner = core if n < 2 else 1 - core
-        place = pl.multiple_of(owner * HALF + (n % 2) * LANES, LANES)
-        outs[0][:, pl.ds(place, LANES)] = block[...]
-    flow.start(outs[0], results[0])
+    for owner, block in zip((core, 1 - core), blocks):
+        start = pl.multiple_of(owner * HALF + chunk * LANES, LANES)
+        flow.start(block, whole.at[:, pl.ds(start, LANES)])
+
+
+def start_body(flow, ins, results, outs):
+    place(flow, 0, ins, results[0])
+
+
+def end_body(flow, ins, results, outs):
+    place(flow, 1, ins[1:], results[0])
 
 
 def gather_body(flow, ins, results, outs):
@@ -328,10 +342,10 @@
 
 
 def across_z(blocks):
-    moved = [blocks[0]]
+    moved = list(blocks)
     for e in range(1, Z_LO):
-        moved.append(
-            lax.ppermute(blocks[e], "seq", [(i, i ^ (e * YX)) for i in range(Z_LO * YX)])
+        moved[e] = lax.ppermute(
+            blocks[e], "seq", [(i, i ^ (e * YX)) for i in range(Z_LO * YX)]
         )
     return moved
 
@@ -394,7 +408,7 @@
     spread, *mixed = call(
         middle_body,
         [Far(struct((ROWS, WIDTH, LANES)))] + [BLOCK] * Z_LO,
-        [SQUARE, SQUARE],
+        [SQUARE, SQUARE] + [pltpu.VMEM((PAIRS, WIDTH, 2 * LANES), BF16)] * 2,
         Far(two),
         Far(twiddle_out),
         *got,
@@ -437,10 +451,19 @@
         for pair, got_far, weight in zip(pairs, far, (0, 0))
     ]
     other = [swap(total, 1) for total in mine]
+    whole = struct((LANES * ROWS, WIDTH))
+    begun = call(start_body, [Far(whole)], [], mine[0], other[0], copies=2)[0]
     filter_grad = call(
-        join_body, [Far(struct((LANES * ROWS, WIDTH)))], [], *mine, *other, copies=1
+        end_body,
+        [Far(whole)],
+        [],
+        Far(begun),
+        mine[1],
+        other[1],
+        copies=2,
+        fetch=(),
+        aliases={0: 0},
     )[0]
-
     return (
         outputs.reshape(batch, chans, local_len),
         filter_grad.reshape(chans, ROWS, WIDTH),

time: 120 us -> 119 us (level)
  waiting for transfers between devices: 47.7 us -> 46.5 us
    pallas_call x12 -> x13, Pallas kernels: 18.1 us -> 18.3 us  [call(): pl.pallas_call(wrapped, out_shape=[pltpu.HBM(o.shape, o.dtype) if n in fa...]
  transfers between devices with their start and end apart: 17 -> 17, of which waited for: 8 -> 7; matrix products, arithmetic and copies ran while one was open for 5% -> 5% of each run, Pallas kernels for 11% -> 13%
where the time goes in v4:
time: 119 us; the launch traced here: 118 us
  waiting for transfers between devices  46.5 us (39%)
  starting transfers between devices  45.5 us (38%)
  Pallas kernels  18.3 us (15%)
  local copies, waits for them, and re-layouts  6.88 us (6%)
    ppermute x9, waiting for transfers between devices, across_z(): lax.ppermute(blocks[e], 'seq', [(i, i ^ e * YX) for i in range(Z_LO * YX)])  37.4 us
    all_to_all x3, starting transfers between devices, across_yx(): lax.all_to_all(whole, 'seq', split_axis=0, concat_axis=0, axis_index_grou...  19.7 us
    pallas_call x13, Pallas kernels, call(): pl.pallas_call(wrapped, out_shape=[pltpu.HBM(o.shape, o.dtype) if n in fa...  18.3 us
    ppermute x5, starting transfers between devices, swap(): return lax.ppermute(block, 'dp', [(i, i ^ bit) for i in range(4)])  16.3 us
    ppermute x9, starting transfers between devices, across_z(): lax.ppermute(blocks[e], 'seq', [(i, i ^ e * YX) for i in range(Z_LO * YX)])  9.54 us
    ppermute x5, waiting for transfers between devices, swap(): return lax.ppermute(block, 'dp', [(i, i ^ bit) for i in range(4)])  9.16 us
    unnamed x21, local copies, waits for them, and re-layouts  6.77 us
  transfers between devices with their start and end apart: 17, of which 7 were waited for; matrix products, arithmetic and copies ran while one was open for 5% of the time, Pallas kernels for 13%

profile of v4, /device:TPU:35, one launch (start us, length us, event | category | flops | bytes accessed | tf_op | source)
XLA Modules:
  0.0 118.2 jit_solution(5109912170851581995)
XLA Ops:
  0.6 0.0 copy-start.1
  0.7 2.4 %shard_map.114 = (bf16[16,64,128]{2,1,0:T(8,128)(2,1)S(1)}, bf16[16,64,128]{2,1,0:T(8,128)(2,1)S(1)}, bf16[16,64,128]{2,1,0:T(8,128)(2,1)S(1)}, bf16[16,64,128]{2,1,0:T(8,128)(2,1)S(1)}) custom-call(bf16[512,512]{1,0:T(8,128)(2,1)} %refs_0_.7, bf16[128,4096]{1,0:T(8,128)(2,1)} %bitcast.12), custom_call_target="tpu_custom_call" | custom-call | tf_op jit(solution)/shard_map/pallas_call | solution.py:123
  3.1 0.1 collective-permute-start
  3.2 3.1 %collective-permute-start.1 = (bf16[16,64,128]{2,1,0:T(8,128)(2,1)S(1)}, bf16[16,64,128]{2,1,0:T(8,128)(2,1)S(1)}, u32[]{:S(2)}, u32[]{:S(2)}) collective-permute-start(bf16[16,64,128]{2,1,0:T(8,128)(2,1)S(1)} %get-tuple-element.32), channel_id=1, source_target_pairs={{0,32},{1,33},{2,34},{3,35},{4,36},{5,37},{6,38},{7,39},{8,40},{9,... | collective-permute-start | bytes 786440 | tf_op jit(solution)/shard_map/ppermute | solution.py:347
  6.3 0.2 collective-permute-start.2
  6.5 1.9 %shard_map.113 = bf16[16,4,64,128]{3,2,1,0:T(8,128)(2,1)} custom-call(bf16[512,512]{1,0:T(8,128)(2,1)S(1)} %copy-done.5, bf16[8,512]{1,0:T(8,128)(2,1)S(1)} %copy-done.6, bf16[128,4096]{1,0:T(8,128)(2,1)S(1)} %bitcast.8), custom_call_target="tpu_custom_call" | custom-call | flops 60000002048 | bytes 180000000 | tf_op jit(solution)/shard_map/pallas_call | solution.py:123
  8.3 6.9 %all-to-all-start = ((bf16[16,4,64,128]{3,2,1,0:T(8,128)(2,1)}), bf16[16,4,64,128]{3,2,1,0:T(8,128)(2,1)S(1)}, u32[]{:S(2)}, u32[]{:S(2)}) async-start(bf16[16,4,64,128]{3,2,1,0:T(8,128)(2,1)} %shard_map.113), calls=%async_computation | async-start | bytes 2097152 | tf_op jit(solution)/shard_map/all_to_all | solution.py:359
  15.3 2.7 %copy.13 = bf16[128,8,512]{0,2,1:T(8,128)(2,1)} copy(bf16[128,8,512]{2,1,0:T(8,128)(2,1)} %param.18) | data formatting | bytes 2097152 | tf_op args[8]
  18.0 1.0 copy.14
  19.0 2.0 %copy.15 = bf16[512,512]{0,1:T(8,128)(2,1)} copy(bf16[512,512]{1,0:T(8,128)(2,1)} %refs_0_.6) | data formatting | bytes 1048576 | tf_op args[4]
  21.1 1.4 %collective-permute-done.1.refs_2_ = bf16[16,64,128]{2,1,0:T(8,128)(2,1)S(1)} collective-permute-done((bf16[16,64,128]{2,1,0:T(8,128)(2,1)S(1)}, bf16[16,64,128]{2,1,0:T(8,128)(2,1)S(1)}, u32[]{:S(2)}, u32[]{:S(2)}) %collective-permute-start.1) | collective-permute-done | bytes 262176 | tf_op jit(solution)/shard_map/ppermute | solution.py:347
  22.4 6.7 %collective-permute-done.2.refs_3_ = bf16[16,64,128]{2,1,0:T(8,128)(2,1)S(1)} collective-permute-done((bf16[16,64,128]{2,1,0:T(8,128)(2,1)S(1)}, bf16[16,64,128]{2,1,0:T(8,128)(2,1)S(1)}, u32[]{:S(2)}, u32[]{:S(2)}) %collective-permute-start.2) | collective-permute-done | bytes 262176 | tf_op jit(solution)/shard_map/ppermute | solution.py:347
  29.1 1.0 shard_map.115
  30.2 0.1 shard_map.116
  30.3 0.8 collective-permute-start.3
  31.0 2.2 %collective-permute-start.4 = (bf16[16,64,128]{2,1,0:T(8,128)(2,1)S(1)}, bf16[16,64,128]{2,1,0:T(8,128)(2,1)S(1)}, u32[]{:S(2)}, u32[]{:S(2)}) collective-permute-start(bf16[16,64,128]{2,1,0:T(8,128)(2,1)S(1)} %get-tuple-element.38), channel_id=1, source_target_pairs={{0,32},{1,33},{2,34},{3,35},{4,36},{5,37},{6,38},{7,39},{8,40},{9,... | collective-permute-start | bytes 786440 | tf_op jit(solution)/shard_map/ppermute | solution.py:347
  33.2 0.2 collective-permute-start.5
  33.4 6.5 %all-to-all-start.1 = ((bf16[16,4,64,128]{3,2,1,0:T(8,128)(2,1)}), bf16[16,4,64,128]{3,2,1,0:T(8,128)(2,1)S(1)}, u32[]{:S(2)}, u32[]{:S(2)}) async-start(bf16[16,4,64,128]{3,2,1,0:T(8,128)(2,1)} %shard_map.115), calls=%async_computation.1 | async-start | bytes 2097152 | tf_op jit(solution)/shard_map/all_to_all | solution.py:359
  39.9 2.4 %collective-permute-done.4.refs_4_ = bf16[16,64,128]{2,1,0:T(8,128)(2,1)S(1)} collective-permute-done((bf16[16,64,128]{2,1,0:T(8,128)(2,1)S(1)}, bf16[16,64,128]{2,1,0:T(8,128)(2,1)S(1)}, u32[]{:S(2)}, u32[]{:S(2)}) %collective-permute-start.4) | collective-permute-done | bytes 262176 | tf_op jit(solution)/shard_map/ppermute | solution.py:347
  42.3 12.0 %collective-permute-done.5.refs_5_ = bf16[16,64,128]{2,1,0:T(8,128)(2,1)S(1)} collective-permute-done((bf16[16,64,128]{2,1,0:T(8,128)(2,1)S(1)}, bf16[16,64,128]{2,1,0:T(8,128)(2,1)S(1)}, u32[]{:S(2)}, u32[]{:S(2)}) %collective-permute-start.5) | collective-permute-done | bytes 262176 | tf_op jit(solution)/shard_map/ppermute | solution.py:347
  54.3 3.1 %shard_map.117 = (bf16[8,512,128]{2,1,0:T(8,128)(2,1)}, bf16[16,64,128]{2,1,0:T(8,128)(2,1)S(1)}, bf16[16,64,128]{2,1,0:T(8,128)(2,1)S(1)}, bf16[16,64,128]{2,1,0:T(8,128)(2,1)S(1)}, bf16[16,64,128]{2,1,0:T(8,128)(2,1)S(1)}) custom-call(bf16[512,512]{1,0:T(8,128)(2,1)} %bitcast.14, bf16[8,512]{1,0:T(8,128)(2,1)} %refs_1_.5, ...), custom_call_target="tpu_custom_call" | custom-call | flops 60000002048 | bytes 180000000 | tf_op jit(solution)/shard_map/pallas_call | solution.py:123
  57.4 0.1 collective-permute-start.6
  57.5 3.0 %collective-permute-start.7 = (bf16[16,64,128]{2,1,0:T(8,128)(2,1)S(1)}, bf16[16,64,128]{2,1,0:T(8,128)(2,1)S(1)}, u32[]{:S(2)}, u32[]{:S(2)}) collective-permute-start(bf16[16,64,128]{2,1,0:T(8,128)(2,1)S(1)} %get-tuple-element.44), channel_id=1, source_target_pairs={{0,32},{1,33},{2,34},{3,35},{4,36},{5,37},{6,38},{7,39},{8,40},{9,... | collective-permute-start | bytes 786440 | tf_op jit(solution)/shard_map/ppermute | solution.py:347
  60.5 0.0 collective-permute-start.8
  60.5 0.0 all-to-all-done.1.refs_2_
  60.5 2.6 %shard_map.119 = (bf16[8,256,128]{2,1,0:T(8,128)(2,1)S(1)}, bf16[8,256,128]{2,1,0:T(8,128)(2,1)S(1)}) custom-call(bf16[512,512]{1,0:T(8,128)(2,1)} %refs_0_.6, bf16[8,512]{1,0:T(8,128)(2,1)} %refs_1_.5, bf16[16,4,64,128]{3,2,1,0:T(8,128)(2,1)S(1)} %all-to-all-done.1.refs_2_, bf16[8,512,128]{2,1,0:T(8,128)(2,1)} %get-tuple-element.47.refs_3_), custom_call_target="tpu_custom_call" | custom-call | flops 60000002048 | bytes 180000000 | tf_op jit(solution)/shard_map/pallas_call | solution.py:123
  63.1 3.8 %collective-permute-start.9 = (bf16[8,256,128]{2,1,0:T(8,128)(2,1)S(1)}, bf16[8,256,128]{2,1,0:T(8,128)(2,1)S(1)}, u32[]{:S(2)}, u32[]{:S(2)}) collective-permute-start(bf16[8,256,128]{2,1,0:T(8,128)(2,1)S(1)} %get-tuple-element.49), channel_id=1, source_target_pairs={{0,64},{64,0},{128,192},{192,128},{1,65},{65,1},{129,193},{193,129... | collective-permute-start | bytes 1572872 | tf_op jit(solution)/shard_map/ppermute | solution.py:365
  66.9 2.6 %collective-permute-done.7.refs_2_ = bf16[16,64,128]{2,1,0:T(8,128)(2,1)S(1)} collective-permute-done((bf16[16,64,128]{2,1,0:T(8,128)(2,1)S(1)}, bf16[16,64,128]{2,1,0:T(8,128)(2,1)S(1)}, u32[]{:S(2)}, u32[]{:S(2)}) %collective-permute-start.7) | collective-permute-done | bytes 262176 | tf_op jit(solution)/shard_map/ppermute | solution.py:347
  69.5 12.3 %collective-permute-done.8.refs_3_ = bf16[16,64,128]{2,1,0:T(8,128)(2,1)S(1)} collective-permute-done((bf16[16,64,128]{2,1,0:T(8,128)(2,1)S(1)}, bf16[16,64,128]{2,1,0:T(8,128)(2,1)S(1)}, u32[]{:S(2)}, u32[]{:S(2)}) %collective-permute-start.8) | collective-permute-done | bytes 262176 | tf_op jit(solution)/shard_map/ppermute | solution.py:347
  81.7 1.0 shard_map.118
  82.8 0.1 shard_map.120
  82.9 0.0 copy-start.3
  82.9 0.0 copy-start.8
  82.9 0.0 copy-start.2
  82.9 6.2 %all-to-all-start.2 = ((bf16[16,4,64,128]{3,2,1,0:T(8,128)(2,1)}), bf16[16,4,64,128]{3,2,1,0:T(8,128)(2,1)S(1)}, u32[]{:S(2)}, u32[]{:S(2)}) async-start(bf16[16,4,64,128]{3,2,1,0:T(8,128)(2,1)} %shard_map.118), calls=%async_computation.2 | async-start | bytes 2097152 | tf_op jit(solution)/shard_map/all_to_all | solution.py:359
  89.2 0.0 copy-start
  89.2 5.3 %collective-permute-start.11 = (bf16[8,128,128]{2,1,0:T(8,128)(2,1)S(1)}, bf16[8,128,128]{2,1,0:T(8,128)(2,1)}, u32[]{:S(2)}, u32[]{:S(2)}) collective-permute-start(bf16[8,128,128]{2,1,0:T(8,128)(2,1)S(1)} %get-tuple-element.56.refs_0_), channel_id=1, source_target_pairs={{0,128},{64,192},{128,0},{192,64},{1,129},{65,193},{129,1},{193,65... | collective-permute-start | bytes 786440 | tf_op jit(solution)/shard_map/ppermute | solution.py:365
  94.5 0.1 collective-permute-start.10
  94.7 0.1 copy.16.refs_1_
  94.8 9.1 %collective-permute-done.11.refs_1_ = bf16[8,128,128]{2,1,0:T(8,128)(2,1)} collective-permute-done((bf16[8,128,128]{2,1,0:T(8,128)(2,1)S(1)}, bf16[8,128,128]{2,1,0:T(8,128)(2,1)}, u32[]{:S(2)}, u32[]{:S(2)}) %collective-permute-start.11) | collective-permute-done | bytes 262176 | tf_op jit(solution)/shard_map/ppermute | solution.py:365
  103.9 0.9 copy-done.4
  104.9 1.2 %shard_map.122.refs_0_ = bf16[1024,128]{1,0:T(8,128)(2,1)S(1)} custom-call(bf16[8,128,128]{2,1,0:T(8,128)(2,1)S(1)} %copy-done.4, bf16[8,128,128]{2,1,0:T(8,128)(2,1)} %collective-permute-done.11.refs_1_), custom_call_target="tpu_custom_call" | custom-call | tf_op jit(solution)/shard_map/pallas_call | solution.py:123
  106.1 5.7 %collective-permute-start.12 = (bf16[1024,128]{1,0:T(8,128)(2,1)S(1)}, bf16[1024,128]{1,0:T(8,128)(2,1)}, u32[]{:S(2)}, u32[]{:S(2)}) collective-permute-start(bf16[1024,128]{1,0:T(8,128)(2,1)S(1)} %shard_map.122.refs_0_), channel_id=1, source_target_pairs={{0,64},{64,0},{128,192},{192,128},{1,65},{65,1},{129,193},{193,129... | collective-permute-start | bytes 786440 | tf_op jit(solution)/shard_map/ppermute | solution.py:365
  111.8 2.1 %shard_map.121 = bf16[128,4096]{1,0:T(8,128)(2,1)} custom-call(bf16[512,512]{1,0:T(8,128)(2,1)S(1)} %copy-done, f32[128,1]{1,0:T(8,128)S(1)} %copy.16.refs_1_, bf16[16,4,64,128]{3,2,1,0:T(8,128)(2,1)S(1)} %all-to-all-done.2.refs_2_, bf16[128,4096]{1,0:T(8,128)(2,1)S(1)} %bitcast.9), custom_call_target="tpu_custom_call" | custom-call | tf_op jit(solution)/shard_map/pallas_call | solution.py:123
  113.8 0.2 shard_map.124.refs_1_
  114.1 1.3 %collective-permute-start.13 = (bf16[1024,128]{1,0:T(8,128)(2,1)S(1)}, bf16[1024,128]{1,0:T(8,128)(2,1)S(1)}, u32[]{:S(2)}, u32[]{:S(2)}) collective-permute-start(bf16[1024,128]{1,0:T(8,128)(2,1)S(1)} %shard_map.124.refs_1_), channel_id=1, source_target_pairs={{0,64},{64,0},{128,192},{192,128},{1,65},{65,1},{129,193},{193,129... | collective-permute-start | bytes 786440 | tf_op jit(solution)/shard_map/ppermute | solution.py:365
  115.4 1.8 %shard_map.123.refs_0_ = bf16[1024,512]{1,0:T(8,128)(2,1)} custom-call(bf16[1024,128]{1,0:T(8,128)(2,1)S(1)} %shard_map.122.refs_0_, bf16[1024,128]{1,0:T(8,128)(2,1)} %collective-permute-done.12.refs_1_), custom_call_target="tpu_custom_call" | custom-call | tf_op jit(solution)/shard_map/pallas_call | solution.py:123
  117.2 0.8 shard_map.125
  (21 shorter events, 0.0 us)
Async XLA Ops:
  0.6 5.8 %copy-start.1 = (bf16[1,128,4096]{2,1,0:T(8,128)(2,1)S(1)}, bf16[1,128,4096]{2,1,0:T(8,128)(2,1)}, u32[]{:S(2)}) copy-start(bf16[1,128,4096]{2,1,0:T(8,128)(2,1)} %param.10) | copy-start | bytes 3145732
  0.6 5.8 %copy-start.5 = (bf16[512,512]{1,0:T(8,128)(2,1)S(1)}, bf16[512,512]{1,0:T(8,128)(2,1)}, u32[]{:S(2)}) copy-start(bf16[512,512]{1,0:T(8,128)(2,1)} %refs_0_.4) | copy-start | bytes 1572868
  0.7 5.8 %copy-start.6 = (bf16[8,512]{1,0:T(8,128)(2,1)S(1)}, bf16[8,512]{1,0:T(8,128)(2,1)}, u32[]{:S(2)}) copy-start(bf16[8,512]{1,0:T(8,128)(2,1)} %refs_1_.3) | copy-start | bytes 24580
  3.1 18.0 %collective-permute-start = (bf16[16,64,128]{2,1,0:T(8,128)(2,1)S(1)}, bf16[16,64,128]{2,1,0:T(8,128)(2,1)S(1)}, u32[]{:S(2)}, u32[]{:S(2)}) collective-permute-start(bf16[16,64,128]{2,1,0:T(8,128)(2,1)S(1)} %get-tuple-element.31), channel_id=1, source_target_pairs={{0,16},{1,17},{2,18},{3,19},{4,20},{5,21},{6,22},{7,23},{8,24},{9,... | collective-permute-start | bytes 786440 | tf_op jit(solution)/shard_map/ppermute | solution.py:347
  3.2 19.2 %collective-permute-start.1 = (bf16[16,64,128]{2,1,0:T(8,128)(2,1)S(1)}, bf16[16,64,128]{2,1,0:T(8,128)(2,1)S(1)}, u32[]{:S(2)}, u32[]{:S(2)}) collective-permute-start(bf16[16,64,128]{2,1,0:T(8,128)(2,1)S(1)} %get-tuple-element.32), channel_id=1, source_target_pairs={{0,32},{1,33},{2,34},{3,35},{4,36},{5,37},{6,38},{7,39},{8,40},{9,... | collective-permute-start | bytes 786440 | tf_op jit(solution)/shard_map/ppermute | solution.py:347
  6.3 22.8 %collective-permute-start.2 = (bf16[16,64,128]{2,1,0:T(8,128)(2,1)S(1)}, bf16[16,64,128]{2,1,0:T(8,128)(2,1)S(1)}, u32[]{:S(2)}, u32[]{:S(2)}) collective-permute-start(bf16[16,64,128]{2,1,0:T(8,128)(2,1)S(1)} %get-tuple-element.33), channel_id=1, source_target_pairs={{0,48},{1,49},{2,50},{3,51},{4,52},{5,53},{6,54},{7,55},{8,56},{9,... | collective-permute-start | bytes 786440 | tf_op jit(solution)/shard_map/ppermute | solution.py:347
  8.3 21.8 %all-to-all-start = ((bf16[16,4,64,128]{3,2,1,0:T(8,128)(2,1)}), bf16[16,4,64,128]{3,2,1,0:T(8,128)(2,1)S(1)}, u32[]{:S(2)}, u32[]{:S(2)}) async-start(bf16[16,4,64,128]{3,2,1,0:T(8,128)(2,1)} %shard_map.113), calls=%async_computation | async-start | bytes 2097152 | tf_op jit(solution)/shard_map/all_to_all | solution.py:359
  15.3 2.7 %copy-start.7 = (bf16[512,512]{1,0:T(8,128)(2,1)S(1)}, bf16[512,512]{1,0:T(8,128)(2,1)}, u32[]{:S(2)}) copy-start(bf16[512,512]{1,0:T(8,128)(2,1)} %param.13) | copy-start | bytes 1572868
  30.3 9.7 %collective-permute-start.3 = (bf16[16,64,128]{2,1,0:T(8,128)(2,1)S(1)}, bf16[16,64,128]{2,1,0:T(8,128)(2,1)S(1)}, u32[]{:S(2)}, u32[]{:S(2)}) collective-permute-start(bf16[16,64,128]{2,1,0:T(8,128)(2,1)S(1)} %get-tuple-element.37), channel_id=1, source_target_pairs={{0,16},{1,17},{2,18},{3,19},{4,20},{5,21},{6,22},{7,23},{8,24},{9,... | collective-permute-start | bytes 786440 | tf_op jit(solution)/shard_map/ppermute | solution.py:347
  31.0 11.3 %collective-permute-start.4 = (bf16[16,64,128]{2,1,0:T(8,128)(2,1)S(1)}, bf16[16,64,128]{2,1,0:T(8,128)(2,1)S(1)}, u32[]{:S(2)}, u32[]{:S(2)}) collective-permute-start(bf16[16,64,128]{2,1,0:T(8,128)(2,1)S(1)} %get-tuple-element.38), channel_id=1, source_target_pairs={{0,32},{1,33},{2,34},{3,35},{4,36},{5,37},{6,38},{7,39},{8,40},{9,... | collective-permute-start | bytes 786440 | tf_op jit(solution)/shard_map/ppermute | solution.py:347
  33.2 21.1 %collective-permute-start.5 = (bf16[16,64,128]{2,1,0:T(8,128)(2,1)S(1)}, bf16[16,64,128]{2,1,0:T(8,128)(2,1)S(1)}, u32[]{:S(2)}, u32[]{:S(2)}) collective-permute-start(bf16[16,64,128]{2,1,0:T(8,128)(2,1)S(1)} %get-tuple-element.39), channel_id=1, source_target_pairs={{0,48},{1,49},{2,50},{3,51},{4,52},{5,53},{6,54},{7,55},{8,56},{9,... | collective-permute-start | bytes 786440 | tf_op jit(solution)/shard_map/ppermute | solution.py:347
  33.4 27.1 %all-to-all-start.1 = ((bf16[16,4,64,128]{3,2,1,0:T(8,128)(2,1)}), bf16[16,4,64,128]{3,2,1,0:T(8,128)(2,1)S(1)}, u32[]{:S(2)}, u32[]{:S(2)}) async-start(bf16[16,4,64,128]{3,2,1,0:T(8,128)(2,1)} %shard_map.115), calls=%async_computation.1 | async-start | bytes 2097152 | tf_op jit(solution)/shard_map/all_to_all | solution.py:359
  57.4 9.5 %collective-permute-start.6 = (bf16[16,64,128]{2,1,0:T(8,128)(2,1)S(1)}, bf16[16,64,128]{2,1,0:T(8,128)(2,1)S(1)}, u32[]{:S(2)}, u32[]{:S(2)}) collective-permute-start(bf16[16,64,128]{2,1,0:T(8,128)(2,1)S(1)} %get-tuple-element.43), channel_id=1, source_target_pairs={{0,16},{1,17},{2,18},{3,19},{4,20},{5,21},{6,22},{7,23},{8,24},{9,... | collective-permute-start | bytes 786440 | tf_op jit(solution)/shard_map/ppermute | solution.py:347
  57.5 12.0 %collective-permute-start.7 = (bf16[16,64,128]{2,1,0:T(8,128)(2,1)S(1)}, bf16[16,64,128]{2,1,0:T(8,128)(2,1)S(1)}, u32[]{:S(2)}, u32[]{:S(2)}) collective-permute-start(bf16[16,64,128]{2,1,0:T(8,128)(2,1)S(1)} %get-tuple-element.44), channel_id=1, source_target_pairs={{0,32},{1,33},{2,34},{3,35},{4,36},{5,37},{6,38},{7,39},{8,40},{9,... | collective-permute-start | bytes 786440 | tf_op jit(solution)/shard_map/ppermute | solution.py:347
  60.5 21.3 %collective-permute-start.8 = (bf16[16,64,128]{2,1,0:T(8,128)(2,1)S(1)}, bf16[16,64,128]{2,1,0:T(8,128)(2,1)S(1)}, u32[]{:S(2)}, u32[]{:S(2)}) collective-permute-start(bf16[16,64,128]{2,1,0:T(8,128)(2,1)S(1)} %get-tuple-element.45), channel_id=1, source_target_pairs={{0,48},{1,49},{2,50},{3,51},{4,52},{5,53},{6,54},{7,55},{8,56},{9,... | collective-permute-start | bytes 786440 | tf_op jit(solution)/shard_map/ppermute | solution.py:347
  63.1 19.7 %collective-permute-start.9 = (bf16[8,256,128]{2,1,0:T(8,128)(2,1)S(1)}, bf16[8,256,128]{2,1,0:T(8,128)(2,1)S(1)}, u32[]{:S(2)}, u32[]{:S(2)}) collective-permute-start(bf16[8,256,128]{2,1,0:T(8,128)(2,1)S(1)} %get-tuple-element.49), channel_id=1, source_target_pairs={{0,64},{64,0},{128,192},{192,128},{1,65},{65,1},{129,193},{193,129... | collective-permute-start | bytes 1572872 | tf_op jit(solution)/shard_map/ppermute | solution.py:365
  82.9 6.3 %copy-start.3 = (bf16[8,128,128]{2,1,0:T(8,128)(2,1)}, bf16[8,128,128]{2,1,0:T(8,128)(2,1)S(1)}, u32[]{:S(2)}) copy-start(bf16[8,128,128]{2,1,0:T(8,128)(2,1)S(1)} %get-tuple-element.56.refs_0_) | copy-start | bytes 786436
  82.9 11.7 %copy-start.8 = (f32[128]{0:T(128)S(1)}, f32[128]{0:T(128)}, u32[]{:S(2)}) copy-start(f32[128]{0:T(128)} %param.19) | copy-start | bytes 1540
  82.9 28.8 %copy-start.2 = (bf16[1,128,4096]{2,1,0:T(8,128)(2,1)S(1)}, bf16[1,128,4096]{2,1,0:T(8,128)(2,1)}, u32[]{:S(2)}) copy-start(bf16[1,128,4096]{2,1,0:T(8,128)(2,1)} %param.10) | copy-start | bytes 3145732
  82.9 28.8 %all-to-all-start.2 = ((bf16[16,4,64,128]{3,2,1,0:T(8,128)(2,1)}), bf16[16,4,64,128]{3,2,1,0:T(8,128)(2,1)S(1)}, u32[]{:S(2)}, u32[]{:S(2)}) async-start(bf16[16,4,64,128]{3,2,1,0:T(8,128)(2,1)} %shard_map.118), calls=%async_computation.2 | async-start | bytes 2097152 | tf_op jit(solution)/shard_map/all_to_all | solution.py:359
  89.2 22.6 %copy-start = (bf16[512,512]{1,0:T(8,128)(2,1)S(1)}, bf16[512,512]{1,0:T(8,128)(2,1)}, u32[]{:S(2)}) copy-start(bf16[512,512]{1,0:T(8,128)(2,1)} %refs_0_.7) | copy-start | bytes 1572868
  89.2 14.7 %collective-permute-start.11 = (bf16[8,128,128]{2,1,0:T(8,128)(2,1)S(1)}, bf16[8,128,128]{2,1,0:T(8,128)(2,1)}, u32[]{:S(2)}, u32[]{:S(2)}) collective-permute-start(bf16[8,128,128]{2,1,0:T(8,128)(2,1)S(1)} %get-tuple-element.56.refs_0_), channel_id=1, source_target_pairs={{0,128},{64,192},{128,0},{192,64},{1,129},{65,193},{129,1},{193,65... | collective-permute-start | bytes 786440 | tf_op jit(solution)/shard_map/ppermute | solution.py:365
  94.5 19.3 %collective-permute-start.10 = (bf16[8,128,128]{2,1,0:T(8,128)(2,1)S(1)}, bf16[8,128,128]{2,1,0:T(8,128)(2,1)S(1)}, u32[]{:S(2)}, u32[]{:S(2)}) collective-permute-start(bf16[8,128,128]{2,1,0:T(8,128)(2,1)S(1)} %get-tuple-element.52.refs_0_), channel_id=1, source_target_pairs={{0,128},{64,192},{128,0},{192,64},{1,129},{65,193},{129,1},{193,65... | collective-permute-start | bytes 786440 | tf_op jit(solution)/shard_map/ppermute | solution.py:365
  103.9 1.0 copy-start.4
  106.1 9.4 %collective-permute-start.12 = (bf16[1024,128]{1,0:T(8,128)(2,1)S(1)}, bf16[1024,128]{1,0:T(8,128)(2,1)}, u32[]{:S(2)}, u32[]{:S(2)}) collective-permute-start(bf16[1024,128]{1,0:T(8,128)(2,1)S(1)} %shard_map.122.refs_0_), channel_id=1, source_target_pairs={{0,64},{64,0},{128,192},{192,128},{1,65},{65,1},{129,193},{193,129... | collective-permute-start | bytes 786440 | tf_op jit(solution)/shard_map/ppermute | solution.py:365
  114.1 3.1 %collective-permute-start.13 = (bf16[1024,128]{1,0:T(8,128)(2,1)S(1)}, bf16[1024,128]{1,0:T(8,128)(2,1)S(1)}, u32[]{:S(2)}, u32[]{:S(2)}) collective-permute-start(bf16[1024,128]{1,0:T(8,128)(2,1)S(1)} %shard_map.124.refs_1_), channel_id=1, source_target_pairs={{0,64},{64,0},{128,192},{192,128},{1,65},{65,1},{129,193},{193,129... | collective-permute-start | bytes 786440 | tf_op jit(solution)/shard_map/ppermute | solution.py:365

commit v5 on v4

--- a/solution.py
+++ b/solution.py
@@ -246,7 +246,7 @@
             block[:, rows, :] = shaped[e * YX : (e + 1) * YX]
 
 
-def grad_body(flow, ins, results, outs, f3s):
+def grad_body(flow, ins, results, outs, f3s, scr):
     f3_ref, tw_ref, d_ref, zt_ref = ins
     z = my_z()
     core = my_core()
@@ -266,9 +266,16 @@
         flow.wait(3)
         for h in range(2):
             value = grads[:, h * LANES : (h + 1) * LANES]
-            for n, (span, out) in enumerate(zip(spans, outs)):
+            for n, span in enumerate(spans):
                 spread = zt_ref[k + h, span, :].astype(F32)
-                out[k + h] = (spread * value[n * HALF : (n + 1) * HALF]).astype(BF16)
+                term = (spread * value[n * HALF : (n + 1) * HALF]).T
+                for side in range(2):
+                    scr[2 * n + side, pl.ds(k + h, LANES, stride=ROWS), :] = term[
+                        :, side * LANES : (side + 1) * LANES
+                    ]
+    for n, out in enumerate(outs):
+        for side in range(2):
+            out[:, side * LANES : (side + 1) * LANES] = scr[2 * n + side].astype(BF16)
 
 
 def last_body(flow, ins, results, outs, fscr, scr):
@@ -293,32 +300,15 @@
 
 
 def add_body(flow, ins, results, outs):
-    for n, out in enumerate(outs):
-        span = slice(n * LANES, (n + 1) * LANES)
-        out[...] = (ins[0][:, span].astype(F32) + ins[1][:, span].astype(F32)).astype(BF16)
-
-
-def total_body(flow, ins, results, outs, scr):
-    a_ref, b_ref = ins
-    for k in range(ROWS):
-        total = a_ref[k].astype(F32) + b_ref[k].astype(F32)
-        scr[pl.ds(k, LANES, stride=ROWS), :] = total.T
-    outs[0][...] = scr[...].astype(BF16)
-
-
-def place(flow, chunk, blocks, whole):
-    core = my_core()
-    for owner, block in zip((core, 1 - core), blocks):
-        start = pl.multiple_of(owner * HALF + chunk * LANES, LANES)
-        flow.start(block, whole.at[:, pl.ds(start, LANES)])
+    outs[0][...] = (ins[0][...].astype(F32) + ins[1][...].astype(F32)).astype(BF16)
 
 
 def start_body(flow, ins, results, outs):
-    place(flow, 0, ins, results[0])
+    flow.start(ins[0], results[0].at[:, halves(my_core())])
 
 
 def end_body(flow, ins, results, outs):
-    place(flow, 1, ins[1:], results[0])
+    flow.start(ins[1], results[0].at[:, halves(1 - my_core())])
 
 
 def gather_body(flow, ins, results, outs):
@@ -417,11 +407,11 @@
         copies=PAIRS,
         weight_us=EXCHANGE_US,
     )
-    half = struct((ROWS, HALF, LANES))
+    half = struct((LANES * ROWS, HALF))
     keep, send = call(
         grad_body,
         [half, half],
-        [SQUARE],
+        [SQUARE, pltpu.VMEM((4, LANES * ROWS, LANES), F32)],
         Far(factor_three),
         Far(twiddle_out),
         back_got,
@@ -429,12 +419,10 @@
         weight_us=EXCHANGE_US,
     )
     mixed_whole = gathered(across_z(mixed))
-    quarter = struct((ROWS, LANES, LANES))
-    pairs = call(add_body, [quarter] * 2, [], keep, swap(send, 1))
-    mixed_whole, pairs = tied(mixed_whole, pairs)
+    pair = call(add_body, [half], [], keep, swap(send, 1))[0]
+    mixed_whole, pair = tied(mixed_whole, pair)
     returned = across_yx(mixed_whole)
-    flat = struct((LANES * ROWS, LANES))
-    far = [swap(pair, 2) for pair in pairs]
+    far = swap(pair, 2)
     outputs = call(
         last_body,
         [Far(struct((chans, local_len)))],
@@ -444,25 +432,15 @@
         returned,
         signal,
         copies=ROWS,
+        weight_us=EXCHANGE_US,
     )[0]
-    far[1], outputs = tied(far[1], outputs)
-    mine = [
-        call(total_body, [flat], [pltpu.VMEM(flat.shape, F32)], pair, got_far, weight_us=weight)[0]
-        for pair, got_far, weight in zip(pairs, far, (0, 0))
-    ]
-    other = [swap(total, 1) for total in mine]
+    far, outputs = tied(far, outputs)
     whole = struct((LANES * ROWS, WIDTH))
-    begun = call(start_body, [Far(whole)], [], mine[0], other[0], copies=2)[0]
+    mine = call(add_body, [half], [], pair, far)[0]
+    other = swap(mine, 1)
+    begun = call(start_body, [Far(whole)], [], mine, copies=1)[0]
     filter_grad = call(
-        end_body,
-        [Far(whole)],
-        [],
-        Far(begun),
-        mine[1],
-        other[1],
-        copies=2,
-        fetch=(),
-        aliases={0: 0},
+        end_body, [Far(whole)], [], Far(begun), other, copies=1, fetch=(), aliases={0: 0}
     )[0]
     return (
         outputs.reshape(batch, chans, local_len),

time: 119 us -> 118 us (level)
  waiting for transfers between devices: 46.5 us -> 51.7 us
  starting transfers between devices: 45.5 us -> 41.2 us
  Pallas kernels: 18.3 us -> 16.4 us
    all_to_all x3, waiting for transfers between devices: 0.01 us -> 7.78 us  [across_yx(): lax.all_to_all(whole, 'seq', split_axis=0, concat_axis=0, axis_index_grou...]
    ppermute x5 -> x3, starting transfers between devices: 16.3 us -> 12 us  [swap(): return lax.ppermute(block, 'dp', [(i, i ^ bit) for i in range(4)])]
    ppermute x5 -> x3, waiting for transfers between devices: 9.16 us -> 7.12 us  [swap(): return lax.ppermute(block, 'dp', [(i, i ^ bit) for i in range(4)])]
    pallas_call x13 -> x12, Pallas kernels: 18.3 us -> 16.4 us  [call(): pl.pallas_call(wrapped, out_shape=[pltpu.HBM(o.shape, o.dtype) if n in fa...]
    unnamed x21 -> x17, local copies, waits for them, and re-layouts: 6.77 us -> 7.02 us
  transfers between devices with their start and end apart: 17 -> 15, of which waited for: 7 -> 9; matrix products, arithmetic and copies ran while one was open for 5% -> 5% of each run, Pallas kernels for 13% -> 11%
where the time goes in v5:
time: 118 us; the launch traced here: 117 us
  waiting for transfers between devices  51.7 us (44%)
  starting transfers between devices  41.2 us (35%)
  Pallas kernels  16.4 us (14%)
  local copies, waits for them, and re-layouts  7.13 us (6%)
    ppermute x9, waiting for transfers between devices, across_z(): lax.ppermute(blocks[e], 'seq', [(i, i ^ e * YX) for i in range(Z_LO * YX)])  36.8 us
    all_to_all x3, starting transfers between devices, across_yx(): lax.all_to_all(whole, 'seq', split_axis=0, concat_axis=0, axis_index_grou...  19.8 us
    pallas_call x12, Pallas kernels, call(): pl.pallas_call(wrapped, out_shape=[pltpu.HBM(o.shape, o.dtype) if n in fa...  16.4 us
    ppermute x3, starting transfers between devices, swap(): return lax.ppermute(block, 'dp', [(i, i ^ bit) for i in range(4)])  12 us
    ppermute x9, starting transfers between devices, across_z(): lax.ppermute(blocks[e], 'seq', [(i, i ^ e * YX) for i in range(Z_LO * YX)])  9.51 us
    all_to_all x3, waiting for transfers between devices, across_yx(): lax.all_to_all(whole, 'seq', split_axis=0, concat_axis=0, axis_index_grou...  7.78 us
    ppermute x3, waiting for transfers between devices, swap(): return lax.ppermute(block, 'dp', [(i, i ^ bit) for i in range(4)])  7.12 us
    unnamed x17, local copies, waits for them, and re-layouts  7.02 us
  transfers between devices with their start and end apart: 15, of which 9 were waited for; matrix products, arithmetic and copies ran while one was open for 5% of the time, Pallas kernels for 11%

profile of v5, /device:TPU:35, one launch (start us, length us, event | category | flops | bytes accessed | tf_op | source)
XLA Modules:
  0.0 117.4 jit_solution(10535879558036664611)
XLA Ops:
  0.6 0.0 copy-start.1
  0.7 2.4 %shard_map.114 = (bf16[16,64,128]{2,1,0:T(8,128)(2,1)S(1)}, bf16[16,64,128]{2,1,0:T(8,128)(2,1)S(1)}, bf16[16,64,128]{2,1,0:T(8,128)(2,1)S(1)}, bf16[16,64,128]{2,1,0:T(8,128)(2,1)S(1)}) custom-call(bf16[512,512]{1,0:T(8,128)(2,1)} %refs_0_.7, bf16[128,4096]{1,0:T(8,128)(2,1)} %bitcast.11), custom_call_target="tpu_custom_call" | custom-call | tf_op jit(solution)/shard_map/pallas_call | solution.py:123
  3.1 0.1 collective-permute-start
  3.2 3.1 %collective-permute-start.1 = (bf16[16,64,128]{2,1,0:T(8,128)(2,1)S(1)}, bf16[16,64,128]{2,1,0:T(8,128)(2,1)S(1)}, u32[]{:S(2)}, u32[]{:S(2)}) collective-permute-start(bf16[16,64,128]{2,1,0:T(8,128)(2,1)S(1)} %get-tuple-element.29), channel_id=1, source_target_pairs={{0,32},{1,33},{2,34},{3,35},{4,36},{5,37},{6,38},{7,39},{8,40},{9,... | collective-permute-start | bytes 786440 | tf_op jit(solution)/shard_map/ppermute | solution.py:337
  6.3 0.2 collective-permute-start.2
  6.5 1.9 %shard_map.113 = bf16[16,4,64,128]{3,2,1,0:T(8,128)(2,1)} custom-call(bf16[512,512]{1,0:T(8,128)(2,1)S(1)} %copy-done.3, bf16[8,512]{1,0:T(8,128)(2,1)S(1)} %copy-done.4, bf16[128,4096]{1,0:T(8,128)(2,1)S(1)} %bitcast.8), custom_call_target="tpu_custom_call" | custom-call | flops 60000002048 | bytes 180000000 | tf_op jit(solution)/shard_map/pallas_call | solution.py:123
  8.3 6.9 %all-to-all-start = ((bf16[16,4,64,128]{3,2,1,0:T(8,128)(2,1)}), bf16[16,4,64,128]{3,2,1,0:T(8,128)(2,1)S(1)}, u32[]{:S(2)}, u32[]{:S(2)}) async-start(bf16[16,4,64,128]{3,2,1,0:T(8,128)(2,1)} %shard_map.113), calls=%async_computation | async-start | bytes 2097152 | tf_op jit(solution)/shard_map/all_to_all | solution.py:349
  15.3 2.7 %copy.13 = bf16[128,8,512]{0,2,1:T(8,128)(2,1)} copy(bf16[128,8,512]{2,1,0:T(8,128)(2,1)} %param.18) | data formatting | bytes 2097152 | tf_op args[8]
  18.0 1.0 copy.14
  19.0 2.0 %copy.15 = bf16[512,512]{0,1:T(8,128)(2,1)} copy(bf16[512,512]{1,0:T(8,128)(2,1)} %refs_0_.6) | data formatting | bytes 1048576 | tf_op args[4]
  21.1 1.4 %collective-permute-done.1.refs_2_ = bf16[16,64,128]{2,1,0:T(8,128)(2,1)S(1)} collective-permute-done((bf16[16,64,128]{2,1,0:T(8,128)(2,1)S(1)}, bf16[16,64,128]{2,1,0:T(8,128)(2,1)S(1)}, u32[]{:S(2)}, u32[]{:S(2)}) %collective-permute-start.1) | collective-permute-done | bytes 262176 | tf_op jit(solution)/shard_map/ppermute | solution.py:337
  22.4 6.7 %collective-permute-done.2.refs_3_ = bf16[16,64,128]{2,1,0:T(8,128)(2,1)S(1)} collective-permute-done((bf16[16,64,128]{2,1,0:T(8,128)(2,1)S(1)}, bf16[16,64,128]{2,1,0:T(8,128)(2,1)S(1)}, u32[]{:S(2)}, u32[]{:S(2)}) %collective-permute-start.2) | collective-permute-done | bytes 262176 | tf_op jit(solution)/shard_map/ppermute | solution.py:337
  29.1 1.0 shard_map.115
  30.2 0.1 shard_map.116
  30.3 0.7 collective-permute-start.3
  31.0 2.2 %collective-permute-start.4 = (bf16[16,64,128]{2,1,0:T(8,128)(2,1)S(1)}, bf16[16,64,128]{2,1,0:T(8,128)(2,1)S(1)}, u32[]{:S(2)}, u32[]{:S(2)}) collective-permute-start(bf16[16,64,128]{2,1,0:T(8,128)(2,1)S(1)} %get-tuple-element.35), channel_id=1, source_target_pairs={{0,32},{1,33},{2,34},{3,35},{4,36},{5,37},{6,38},{7,39},{8,40},{9,... | collective-permute-start | bytes 786440 | tf_op jit(solution)/shard_map/ppermute | solution.py:337
  33.2 0.2 collective-permute-start.5
  33.4 6.6 %all-to-all-start.1 = ((bf16[16,4,64,128]{3,2,1,0:T(8,128)(2,1)}), bf16[16,4,64,128]{3,2,1,0:T(8,128)(2,1)S(1)}, u32[]{:S(2)}, u32[]{:S(2)}) async-start(bf16[16,4,64,128]{3,2,1,0:T(8,128)(2,1)} %shard_map.115), calls=%async_computation.1 | async-start | bytes 2097152 | tf_op jit(solution)/shard_map/all_to_all | solution.py:349
  39.9 0.0 collective-permute-done.3.refs_3_
  39.9 2.4 %collective-permute-done.4.refs_4_ = bf16[16,64,128]{2,1,0:T(8,128)(2,1)S(1)} collective-permute-done((bf16[16,64,128]{2,1,0:T(8,128)(2,1)S(1)}, bf16[16,64,128]{2,1,0:T(8,128)(2,1)S(1)}, u32[]{:S(2)}, u32[]{:S(2)}) %collective-permute-start.4) | collective-permute-done | bytes 262176 | tf_op jit(solution)/shard_map/ppermute | solution.py:337
  42.3 12.0 %collective-permute-done.5.refs_5_ = bf16[16,64,128]{2,1,0:T(8,128)(2,1)S(1)} collective-permute-done((bf16[16,64,128]{2,1,0:T(8,128)(2,1)S(1)}, bf16[16,64,128]{2,1,0:T(8,128)(2,1)S(1)}, u32[]{:S(2)}, u32[]{:S(2)}) %collective-permute-start.5) | collective-permute-done | bytes 262176 | tf_op jit(solution)/shard_map/ppermute | solution.py:337
  54.3 3.1 %shard_map.117 = (bf16[8,512,128]{2,1,0:T(8,128)(2,1)}, bf16[16,64,128]{2,1,0:T(8,128)(2,1)S(1)}, bf16[16,64,128]{2,1,0:T(8,128)(2,1)S(1)}, bf16[16,64,128]{2,1,0:T(8,128)(2,1)S(1)}, bf16[16,64,128]{2,1,0:T(8,128)(2,1)S(1)}) custom-call(bf16[512,512]{1,0:T(8,128)(2,1)} %bitcast.13, bf16[8,512]{1,0:T(8,128)(2,1)} %refs_1_.5, ...), custom_call_target="tpu_custom_call" | custom-call | flops 60000002048 | bytes 180000000 | tf_op jit(solution)/shard_map/pallas_call | solution.py:123
  57.4 0.1 collective-permute-start.6
  57.5 3.0 %collective-permute-start.7 = (bf16[16,64,128]{2,1,0:T(8,128)(2,1)S(1)}, bf16[16,64,128]{2,1,0:T(8,128)(2,1)S(1)}, u32[]{:S(2)}, u32[]{:S(2)}) collective-permute-start(bf16[16,64,128]{2,1,0:T(8,128)(2,1)S(1)} %get-tuple-element.41), channel_id=1, source_target_pairs={{0,32},{1,33},{2,34},{3,35},{4,36},{5,37},{6,38},{7,39},{8,40},{9,... | collective-permute-start | bytes 786440 | tf_op jit(solution)/shard_map/ppermute | solution.py:337
  60.4 0.0 collective-permute-start.8
  60.5 0.0 all-to-all-done.1.refs_2_
  60.5 3.0 %shard_map.119 = (bf16[1024,256]{1,0:T(8,128)(2,1)S(1)}, bf16[1024,256]{1,0:T(8,128)(2,1)S(1)}) custom-call(bf16[512,512]{1,0:T(8,128)(2,1)} %refs_0_.6, bf16[8,512]{1,0:T(8,128)(2,1)} %refs_1_.5, bf16[16,4,64,128]{3,2,1,0:T(8,128)(2,1)S(1)} %all-to-all-done.1.refs_2_, bf16[8,512,128]{2,1,0:T(8,128)(2,1)} %get-tuple-element.44.refs_3_), custom_call_target="tpu_custom_call" | custom-call | flops 60000002048 | bytes 180000000 | tf_op jit(solution)/shard_map/pallas_call | solution.py:123
  63.4 4.0 %collective-permute-start.9 = (bf16[1024,256]{1,0:T(8,128)(2,1)S(1)}, bf16[1024,256]{1,0:T(8,128)(2,1)S(1)}, u32[]{:S(2)}, u32[]{:S(2)}) collective-permute-start(bf16[1024,256]{1,0:T(8,128)(2,1)S(1)} %get-tuple-element.46), channel_id=1, source_target_pairs={{0,64},{64,0},{128,192},{192,128},{1,65},{65,1},{129,193},{193,129... | collective-permute-start | bytes 1572872 | tf_op jit(solution)/shard_map/ppermute | solution.py:355
  67.4 0.0 collective-permute-done.6.refs_1_
  67.4 2.0 %collective-permute-done.7.refs_2_ = bf16[16,64,128]{2,1,0:T(8,128)(2,1)S(1)} collective-permute-done((bf16[16,64,128]{2,1,0:T(8,128)(2,1)S(1)}, bf16[16,64,128]{2,1,0:T(8,128)(2,1)S(1)}, u32[]{:S(2)}, u32[]{:S(2)}) %collective-permute-start.7) | collective-permute-done | bytes 262176 | tf_op jit(solution)/shard_map/ppermute | solution.py:337
  69.4 12.3 %collective-permute-done.8.refs_3_ = bf16[16,64,128]{2,1,0:T(8,128)(2,1)S(1)} collective-permute-done((bf16[16,64,128]{2,1,0:T(8,128)(2,1)S(1)}, bf16[16,64,128]{2,1,0:T(8,128)(2,1)S(1)}, u32[]{:S(2)}, u32[]{:S(2)}) %collective-permute-start.8) | collective-permute-done | bytes 262176 | tf_op jit(solution)/shard_map/ppermute | solution.py:337
  81.7 1.0 shard_map.118
  82.7 0.0 collective-permute-done.9.refs_1_
  82.7 0.1 shard_map.120.refs_0_
  82.9 0.0 copy-start.6
  82.9 0.0 copy-start
  82.9 6.3 %all-to-all-start.2 = ((bf16[16,4,64,128]{3,2,1,0:T(8,128)(2,1)}), bf16[16,4,64,128]{3,2,1,0:T(8,128)(2,1)S(1)}, u32[]{:S(2)}, u32[]{:S(2)}) async-start(bf16[16,4,64,128]{3,2,1,0:T(8,128)(2,1)} %shard_map.118), calls=%async_computation.2 | async-start | bytes 2097152 | tf_op jit(solution)/shard_map/all_to_all | solution.py:349
  89.2 0.1 copy.16.refs_1_
  89.3 5.3 %collective-permute-start.10 = (bf16[1024,256]{1,0:T(8,128)(2,1)S(1)}, bf16[1024,256]{1,0:T(8,128)(2,1)S(1)}, u32[]{:S(2)}, u32[]{:S(2)}) collective-permute-start(bf16[1024,256]{1,0:T(8,128)(2,1)S(1)} %shard_map.120.refs_0_), channel_id=1, source_target_pairs={{0,128},{64,192},{128,0},{192,64},{1,129},{65,193},{129,1},{193,65... | collective-permute-start | bytes 1572872 | tf_op jit(solution)/shard_map/ppermute | solution.py:355
  94.7 7.8 %all-to-all-done.2.refs_2_ = bf16[16,4,64,128]{3,2,1,0:T(8,128)(2,1)S(1)} async-done(((bf16[16,4,64,128]{3,2,1,0:T(8,128)(2,1)}), bf16[16,4,64,128]{3,2,1,0:T(8,128)(2,1)S(1)}, u32[]{:S(2)}, u32[]{:S(2)}) %all-to-all-start.2) | async-done | bytes 1048608 | tf_op jit(solution)/shard_map/all_to_all | solution.py:349
  102.4 1.2 %copy-done.2 = bf16[1,128,4096]{2,1,0:T(8,128)(2,1)S(1)} copy-done((bf16[1,128,4096]{2,1,0:T(8,128)(2,1)S(1)}, bf16[1,128,4096]{2,1,0:T(8,128)(2,1)}, u32[]{:S(2)}) %copy-start.2) | copy-done | bytes 1048600
  103.7 2.1 %shard_map.121 = bf16[128,4096]{1,0:T(8,128)(2,1)} custom-call(bf16[512,512]{1,0:T(8,128)(2,1)S(1)} %copy-done, f32[128,1]{1,0:T(8,128)S(1)} %copy.16.refs_1_, bf16[16,4,64,128]{3,2,1,0:T(8,128)(2,1)S(1)} %all-to-all-done.2.refs_2_, bf16[128,4096]{1,0:T(8,128)(2,1)S(1)} %bitcast.9), custom_call_target="tpu_custom_call" | custom-call | flops 60000002048 | bytes 180000000 | tf_op jit(solution)/shard_map/pallas_call | solution.py:123
  105.7 6.4 %collective-permute-done.10.refs_1_ = bf16[1024,256]{1,0:T(8,128)(2,1)S(1)} collective-permute-done((bf16[1024,256]{1,0:T(8,128)(2,1)S(1)}, bf16[1024,256]{1,0:T(8,128)(2,1)S(1)}, u32[]{:S(2)}, u32[]{:S(2)}) %collective-permute-start.10) | collective-permute-done | bytes 524320 | tf_op jit(solution)/shard_map/ppermute | solution.py:355
  112.1 0.1 shard_map.122.refs_0_
  112.2 2.7 %collective-permute-start.11 = (bf16[1024,256]{1,0:T(8,128)(2,1)S(1)}, bf16[1024,256]{1,0:T(8,128)(2,1)S(1)}, u32[]{:S(2)}, u32[]{:S(2)}) collective-permute-start(bf16[1024,256]{1,0:T(8,128)(2,1)S(1)} %shard_map.122.refs_0_), channel_id=1, source_target_pairs={{0,64},{64,0},{128,192},{192,128},{1,65},{65,1},{129,193},{193,129... | collective-permute-start | bytes 1572872 | tf_op jit(solution)/shard_map/ppermute | solution.py:355
  114.9 0.8 shard_map.123.refs_0_
  115.7 0.7 collective-permute-done.11.refs_1_
  116.4 0.8 shard_map.124
  (12 shorter events, 0.0 us)
Async XLA Ops:
  0.6 5.8 %copy-start.1 = (bf16[1,128,4096]{2,1,0:T(8,128)(2,1)S(1)}, bf16[1,128,4096]{2,1,0:T(8,128)(2,1)}, u32[]{:S(2)}) copy-start(bf16[1,128,4096]{2,1,0:T(8,128)(2,1)} %param.10) | copy-start | bytes 3145732
  0.6 5.8 %copy-start.3 = (bf16[512,512]{1,0:T(8,128)(2,1)S(1)}, bf16[512,512]{1,0:T(8,128)(2,1)}, u32[]{:S(2)}) copy-start(bf16[512,512]{1,0:T(8,128)(2,1)} %refs_0_.4) | copy-start | bytes 1572868
  0.7 5.8 %copy-start.4 = (bf16[8,512]{1,0:T(8,128)(2,1)S(1)}, bf16[8,512]{1,0:T(8,128)(2,1)}, u32[]{:S(2)}) copy-start(bf16[8,512]{1,0:T(8,128)(2,1)} %refs_1_.3) | copy-start | bytes 24580
  3.1 18.0 %collective-permute-start = (bf16[16,64,128]{2,1,0:T(8,128)(2,1)S(1)}, bf16[16,64,128]{2,1,0:T(8,128)(2,1)S(1)}, u32[]{:S(2)}, u32[]{:S(2)}) collective-permute-start(bf16[16,64,128]{2,1,0:T(8,128)(2,1)S(1)} %get-tuple-element.28), channel_id=1, source_target_pairs={{0,16},{1,17},{2,18},{3,19},{4,20},{5,21},{6,22},{7,23},{8,24},{9,... | collective-permute-start | bytes 786440 | tf_op jit(solution)/shard_map/ppermute | solution.py:337
  3.2 19.2 %collective-permute-start.1 = (bf16[16,64,128]{2,1,0:T(8,128)(2,1)S(1)}, bf16[16,64,128]{2,1,0:T(8,128)(2,1)S(1)}, u32[]{:S(2)}, u32[]{:S(2)}) collective-permute-start(bf16[16,64,128]{2,1,0:T(8,128)(2,1)S(1)} %get-tuple-element.29), channel_id=1, source_target_pairs={{0,32},{1,33},{2,34},{3,35},{4,36},{5,37},{6,38},{7,39},{8,40},{9,... | collective-permute-start | bytes 786440 | tf_op jit(solution)/shard_map/ppermute | solution.py:337
  6.3 22.8 %collective-permute-start.2 = (bf16[16,64,128]{2,1,0:T(8,128)(2,1)S(1)}, bf16[16,64,128]{2,1,0:T(8,128)(2,1)S(1)}, u32[]{:S(2)}, u32[]{:S(2)}) collective-permute-start(bf16[16,64,128]{2,1,0:T(8,128)(2,1)S(1)} %get-tuple-element.30), channel_id=1, source_target_pairs={{0,48},{1,49},{2,50},{3,51},{4,52},{5,53},{6,54},{7,55},{8,56},{9,... | collective-permute-start | bytes 786440 | tf_op jit(solution)/shard_map/ppermute | solution.py:337
  8.3 21.8 %all-to-all-start = ((bf16[16,4,64,128]{3,2,1,0:T(8,128)(2,1)}), bf16[16,4,64,128]{3,2,1,0:T(8,128)(2,1)S(1)}, u32[]{:S(2)}, u32[]{:S(2)}) async-start(bf16[16,4,64,128]{3,2,1,0:T(8,128)(2,1)} %shard_map.113), calls=%async_computation | async-start | bytes 2097152 | tf_op jit(solution)/shard_map/all_to_all | solution.py:349
  15.3 2.7 %copy-start.5 = (bf16[512,512]{1,0:T(8,128)(2,1)S(1)}, bf16[512,512]{1,0:T(8,128)(2,1)}, u32[]{:S(2)}) copy-start(bf16[512,512]{1,0:T(8,128)(2,1)} %param.13) | copy-start | bytes 1572868
  30.3 9.7 %collective-permute-start.3 = (bf16[16,64,128]{2,1,0:T(8,128)(2,1)S(1)}, bf16[16,64,128]{2,1,0:T(8,128)(2,1)S(1)}, u32[]{:S(2)}, u32[]{:S(2)}) collective-permute-start(bf16[16,64,128]{2,1,0:T(8,128)(2,1)S(1)} %get-tuple-element.34), channel_id=1, source_target_pairs={{0,16},{1,17},{2,18},{3,19},{4,20},{5,21},{6,22},{7,23},{8,24},{9,... | collective-permute-start | bytes 786440 | tf_op jit(solution)/shard_map/ppermute | solution.py:337
  31.0 11.3 %collective-permute-start.4 = (bf16[16,64,128]{2,1,0:T(8,128)(2,1)S(1)}, bf16[16,64,128]{2,1,0:T(8,128)(2,1)S(1)}, u32[]{:S(2)}, u32[]{:S(2)}) collective-permute-start(bf16[16,64,128]{2,1,0:T(8,128)(2,1)S(1)} %get-tuple-element.35), channel_id=1, source_target_pairs={{0,32},{1,33},{2,34},{3,35},{4,36},{5,37},{6,38},{7,39},{8,40},{9,... | collective-permute-start | bytes 786440 | tf_op jit(solution)/shard_map/ppermute | solution.py:337
  33.2 21.1 %collective-permute-start.5 = (bf16[16,64,128]{2,1,0:T(8,128)(2,1)S(1)}, bf16[16,64,128]{2,1,0:T(8,128)(2,1)S(1)}, u32[]{:S(2)}, u32[]{:S(2)}) collective-permute-start(bf16[16,64,128]{2,1,0:T(8,128)(2,1)S(1)} %get-tuple-element.36), channel_id=1, source_target_pairs={{0,48},{1,49},{2,50},{3,51},{4,52},{5,53},{6,54},{7,55},{8,56},{9,... | collective-permute-start | bytes 786440 | tf_op jit(solution)/shard_map/ppermute | solution.py:337
  33.4 27.1 %all-to-all-start.1 = ((bf16[16,4,64,128]{3,2,1,0:T(8,128)(2,1)}), bf16[16,4,64,128]{3,2,1,0:T(8,128)(2,1)S(1)}, u32[]{:S(2)}, u32[]{:S(2)}) async-start(bf16[16,4,64,128]{3,2,1,0:T(8,128)(2,1)} %shard_map.115), calls=%async_computation.1 | async-start | bytes 2097152 | tf_op jit(solution)/shard_map/all_to_all | solution.py:349
  57.4 10.0 %collective-permute-start.6 = (bf16[16,64,128]{2,1,0:T(8,128)(2,1)S(1)}, bf16[16,64,128]{2,1,0:T(8,128)(2,1)S(1)}, u32[]{:S(2)}, u32[]{:S(2)}) collective-permute-start(bf16[16,64,128]{2,1,0:T(8,128)(2,1)S(1)} %get-tuple-element.40), channel_id=1, source_target_pairs={{0,16},{1,17},{2,18},{3,19},{4,20},{5,21},{6,22},{7,23},{8,24},{9,... | collective-permute-start | bytes 786440 | tf_op jit(solution)/shard_map/ppermute | solution.py:337
  57.5 11.9 %collective-permute-start.7 = (bf16[16,64,128]{2,1,0:T(8,128)(2,1)S(1)}, bf16[16,64,128]{2,1,0:T(8,128)(2,1)S(1)}, u32[]{:S(2)}, u32[]{:S(2)}) collective-permute-start(bf16[16,64,128]{2,1,0:T(8,128)(2,1)S(1)} %get-tuple-element.41), channel_id=1, source_target_pairs={{0,32},{1,33},{2,34},{3,35},{4,36},{5,37},{6,38},{7,39},{8,40},{9,... | collective-permute-start | bytes 786440 | tf_op jit(solution)/shard_map/ppermute | solution.py:337
  60.4 21.3 %collective-permute-start.8 = (bf16[16,64,128]{2,1,0:T(8,128)(2,1)S(1)}, bf16[16,64,128]{2,1,0:T(8,128)(2,1)S(1)}, u32[]{:S(2)}, u32[]{:S(2)}) collective-permute-start(bf16[16,64,128]{2,1,0:T(8,128)(2,1)S(1)} %get-tuple-element.42), channel_id=1, source_target_pairs={{0,48},{1,49},{2,50},{3,51},{4,52},{5,53},{6,54},{7,55},{8,56},{9,... | collective-permute-start | bytes 786440 | tf_op jit(solution)/shard_map/ppermute | solution.py:337
  63.4 19.3 %collective-permute-start.9 = (bf16[1024,256]{1,0:T(8,128)(2,1)S(1)}, bf16[1024,256]{1,0:T(8,128)(2,1)S(1)}, u32[]{:S(2)}, u32[]{:S(2)}) collective-permute-start(bf16[1024,256]{1,0:T(8,128)(2,1)S(1)} %get-tuple-element.46), channel_id=1, source_target_pairs={{0,64},{64,0},{128,192},{192,128},{1,65},{65,1},{129,193},{193,129... | collective-permute-start | bytes 1572872 | tf_op jit(solution)/shard_map/ppermute | solution.py:355
  82.9 6.3 %copy-start.6 = (f32[128]{0:T(128)S(1)}, f32[128]{0:T(128)}, u32[]{:S(2)}) copy-start(f32[128]{0:T(128)} %param.19) | copy-start | bytes 1540
  82.9 19.5 %copy-start = (bf16[512,512]{1,0:T(8,128)(2,1)S(1)}, bf16[512,512]{1,0:T(8,128)(2,1)}, u32[]{:S(2)}) copy-start(bf16[512,512]{1,0:T(8,128)(2,1)} %refs_0_.7) | copy-start | bytes 1572868
  82.9 19.5 %all-to-all-start.2 = ((bf16[16,4,64,128]{3,2,1,0:T(8,128)(2,1)}), bf16[16,4,64,128]{3,2,1,0:T(8,128)(2,1)S(1)}, u32[]{:S(2)}, u32[]{:S(2)}) async-start(bf16[16,4,64,128]{3,2,1,0:T(8,128)(2,1)} %shard_map.118), calls=%async_computation.2 | async-start | bytes 2097152 | tf_op jit(solution)/shard_map/all_to_all | solution.py:349
  89.3 22.8 %collective-permute-start.10 = (bf16[1024,256]{1,0:T(8,128)(2,1)S(1)}, bf16[1024,256]{1,0:T(8,128)(2,1)S(1)}, u32[]{:S(2)}, u32[]{:S(2)}) collective-permute-start(bf16[1024,256]{1,0:T(8,128)(2,1)S(1)} %shard_map.120.refs_0_), channel_id=1, source_target_pairs={{0,128},{64,192},{128,0},{192,64},{1,129},{65,193},{129,1},{193,65... | collective-permute-start | bytes 1572872 | tf_op jit(solution)/shard_map/ppermute | solution.py:355
  102.4 1.2 %copy-start.2 = (bf16[1,128,4096]{2,1,0:T(8,128)(2,1)S(1)}, bf16[1,128,4096]{2,1,0:T(8,128)(2,1)}, u32[]{:S(2)}) copy-start(bf16[1,128,4096]{2,1,0:T(8,128)(2,1)} %param.10) | copy-start | bytes 3145732
  112.2 4.2 %collective-permute-start.11 = (bf16[1024,256]{1,0:T(8,128)(2,1)S(1)}, bf16[1024,256]{1,0:T(8,128)(2,1)S(1)}, u32[]{:S(2)}, u32[]{:S(2)}) collective-permute-start(bf16[1024,256]{1,0:T(8,128)(2,1)S(1)} %shard_map.122.refs_0_), channel_id=1, source_target_pairs={{0,64},{64,0},{128,192},{192,128},{1,65},{65,1},{129,193},{193,129... | collective-permute-start | bytes 1572872 | tf_op jit(solution)/shard_map/ppermute | solution.py:355

commit v6 on v5

--- a/solution.py
+++ b/solution.py
@@ -13,6 +13,7 @@
 HALF = WIDTH // 2
 Z_LO = 4
 YX = 16
+OFFSETS = (0, 1, 3, 2)
 PART = WIDTH // Z_LO
 MSG = ROWS * ROWS
 PAIRS = ROWS // 2
@@ -36,7 +37,7 @@
 
 
 def part(z, e):
-    return pl.ds(pl.multiple_of((z ^ e) * PART, PART), PART)
+    return pl.ds(pl.multiple_of((z ^ OFFSETS[e]) * PART, PART), PART)
 
 
 def halves(core):
@@ -335,7 +336,7 @@
     moved = list(blocks)
     for e in range(1, Z_LO):
         moved[e] = lax.ppermute(
-            blocks[e], "seq", [(i, i ^ (e * YX)) for i in range(Z_LO * YX)]
+            blocks[e], "seq", [(i, i ^ (OFFSETS[e] * YX)) for i in range(Z_LO * YX)]
         )
     return moved
 

time: 118 us -> 124 us (1.051)
  the two profiles are of different devices: /device:TPU:35 before, /device:TPU:1 now
where the time goes in v6:
time: 124 us
  waiting for transfers between devices  56.7 us (46%)
  starting transfers between devices  42.8 us (35%)
  Pallas kernels  16.3 us (13%)
  local copies, waits for them, and re-layouts  7.13 us (6%)
    ppermute x9, waiting for transfers between devices, across_z(): lax.ppermute(blocks[e], 'seq', [(i, i ^ OFFSETS[e] * YX) for i in range(Z...  35.2 us
    all_to_all x3, starting transfers between devices, across_yx(): lax.all_to_all(whole, 'seq', split_axis=0, concat_axis=0, axis_index_grou...  20.1 us
    pallas_call x12, Pallas kernels, call(): pl.pallas_call(wrapped, out_shape=[pltpu.HBM(o.shape, o.dtype) if n in fa...  16.3 us
    ppermute x9, starting transfers between devices, across_z(): lax.ppermute(blocks[e], 'seq', [(i, i ^ OFFSETS[e] * YX) for i in range(Z...  12 us
    ppermute x3, waiting for transfers between devices, swap(): return lax.ppermute(block, 'dp', [(i, i ^ bit) for i in range(4)])  11.5 us
    ppermute x3, starting transfers between devices, swap(): return lax.ppermute(block, 'dp', [(i, i ^ bit) for i in range(4)])  10.7 us
    all_to_all x3, waiting for transfers between devices, across_yx(): lax.all_to_all(whole, 'seq', split_axis=0, concat_axis=0, axis_index_grou...  10 us
    unnamed x17, local copies, waits for them, and re-layouts  7.02 us
  transfers between devices with their start and end apart: 15, of which 9 were waited for; matrix products, arithmetic and copies ran while one was open for 5% of the time, Pallas kernels for 10%

profile of v6, /device:TPU:1, one launch (start us, length us, event | category | flops | bytes accessed | tf_op | source)
XLA Modules:
  0.0 124.0 jit_solution(7992227354627721900)
XLA Ops:
  0.6 0.0 copy-start.1
  0.7 2.4 %shard_map.114 = (bf16[16,64,128]{2,1,0:T(8,128)(2,1)S(1)}, bf16[16,64,128]{2,1,0:T(8,128)(2,1)S(1)}, bf16[16,64,128]{2,1,0:T(8,128)(2,1)S(1)}, bf16[16,64,128]{2,1,0:T(8,128)(2,1)S(1)}) custom-call(bf16[512,512]{1,0:T(8,128)(2,1)} %refs_0_.7, bf16[128,4096]{1,0:T(8,128)(2,1)} %bitcast.11), custom_call_target="tpu_custom_call" | custom-call | tf_op jit(solution)/shard_map/pallas_call | solution.py:124
  3.1 2.6 %collective-permute-start = (bf16[16,64,128]{2,1,0:T(8,128)(2,1)S(1)}, bf16[16,64,128]{2,1,0:T(8,128)(2,1)S(1)}, u32[]{:S(2)}, u32[]{:S(2)}) collective-permute-start(bf16[16,64,128]{2,1,0:T(8,128)(2,1)S(1)} %get-tuple-element.28), channel_id=1, source_target_pairs={{0,16},{1,17},{2,18},{3,19},{4,20},{5,21},{6,22},{7,23},{8,24},{9,... | collective-permute-start | bytes 786440 | tf_op jit(solution)/shard_map/ppermute | solution.py:338
  5.7 2.8 %collective-permute-start.1 = (bf16[16,64,128]{2,1,0:T(8,128)(2,1)S(1)}, bf16[16,64,128]{2,1,0:T(8,128)(2,1)S(1)}, u32[]{:S(2)}, u32[]{:S(2)}) collective-permute-start(bf16[16,64,128]{2,1,0:T(8,128)(2,1)S(1)} %get-tuple-element.29), channel_id=1, source_target_pairs={{0,48},{1,49},{2,50},{3,51},{4,52},{5,53},{6,54},{7,55},{8,56},{9,... | collective-permute-start | bytes 786440 | tf_op jit(solution)/shard_map/ppermute | solution.py:338
  8.5 0.2 collective-permute-start.2
  8.7 1.9 %shard_map.113 = bf16[16,4,64,128]{3,2,1,0:T(8,128)(2,1)} custom-call(bf16[512,512]{1,0:T(8,128)(2,1)S(1)} %copy-done.3, bf16[8,512]{1,0:T(8,128)(2,1)S(1)} %copy-done.4, bf16[128,4096]{1,0:T(8,128)(2,1)S(1)} %bitcast.8), custom_call_target="tpu_custom_call" | custom-call | flops 60000002048 | bytes 180000000 | tf_op jit(solution)/shard_map/pallas_call | solution.py:124
  10.5 6.8 %all-to-all-start = ((bf16[16,4,64,128]{3,2,1,0:T(8,128)(2,1)}), bf16[16,4,64,128]{3,2,1,0:T(8,128)(2,1)S(1)}, u32[]{:S(2)}, u32[]{:S(2)}) async-start(bf16[16,4,64,128]{3,2,1,0:T(8,128)(2,1)} %shard_map.113), calls=%async_computation | async-start | bytes 2097152 | tf_op jit(solution)/shard_map/all_to_all | solution.py:350
  17.3 0.0 copy-start.5
  17.3 2.7 %copy.13 = bf16[128,8,512]{0,2,1:T(8,128)(2,1)} copy(bf16[128,8,512]{2,1,0:T(8,128)(2,1)} %param.18) | data formatting | bytes 2097152 | tf_op args[8]
  20.0 1.0 copy.14
  21.0 2.0 %copy.15 = bf16[512,512]{0,1:T(8,128)(2,1)} copy(bf16[512,512]{1,0:T(8,128)(2,1)} %refs_0_.6) | data formatting | bytes 1048576 | tf_op args[4]
  23.1 0.0 collective-permute-done.refs_1_
  23.1 8.1 %collective-permute-done.2.refs_3_ = bf16[16,64,128]{2,1,0:T(8,128)(2,1)S(1)} collective-permute-done((bf16[16,64,128]{2,1,0:T(8,128)(2,1)S(1)}, bf16[16,64,128]{2,1,0:T(8,128)(2,1)S(1)}, u32[]{:S(2)}, u32[]{:S(2)}) %collective-permute-start.2) | collective-permute-done | bytes 262176 | tf_op jit(solution)/shard_map/ppermute | solution.py:338
  31.2 1.0 shard_map.115
  32.2 0.5 all-to-all-done.refs_0_
  32.7 0.1 shard_map.116
  32.8 0.5 collective-permute-start.3
  33.3 2.9 %collective-permute-start.4 = (bf16[16,64,128]{2,1,0:T(8,128)(2,1)S(1)}, bf16[16,64,128]{2,1,0:T(8,128)(2,1)S(1)}, u32[]{:S(2)}, u32[]{:S(2)}) collective-permute-start(bf16[16,64,128]{2,1,0:T(8,128)(2,1)S(1)} %get-tuple-element.35), channel_id=1, source_target_pairs={{0,48},{1,49},{2,50},{3,51},{4,52},{5,53},{6,54},{7,55},{8,56},{9,... | collective-permute-start | bytes 786440 | tf_op jit(solution)/shard_map/ppermute | solution.py:338
  36.2 0.0 collective-permute-start.5
  36.2 5.6 %all-to-all-start.1 = ((bf16[16,4,64,128]{3,2,1,0:T(8,128)(2,1)}), bf16[16,4,64,128]{3,2,1,0:T(8,128)(2,1)S(1)}, u32[]{:S(2)}, u32[]{:S(2)}) async-start(bf16[16,4,64,128]{3,2,1,0:T(8,128)(2,1)} %shard_map.115), calls=%async_computation.1 | async-start | bytes 2097152 | tf_op jit(solution)/shard_map/all_to_all | solution.py:350
  41.9 0.0 collective-permute-done.3.refs_3_
  41.9 3.0 %collective-permute-done.4.refs_4_ = bf16[16,64,128]{2,1,0:T(8,128)(2,1)S(1)} collective-permute-done((bf16[16,64,128]{2,1,0:T(8,128)(2,1)S(1)}, bf16[16,64,128]{2,1,0:T(8,128)(2,1)S(1)}, u32[]{:S(2)}, u32[]{:S(2)}) %collective-permute-start.4) | collective-permute-done | bytes 262176 | tf_op jit(solution)/shard_map/ppermute | solution.py:338
  44.9 11.3 %collective-permute-done.5.refs_5_ = bf16[16,64,128]{2,1,0:T(8,128)(2,1)S(1)} collective-permute-done((bf16[16,64,128]{2,1,0:T(8,128)(2,1)S(1)}, bf16[16,64,128]{2,1,0:T(8,128)(2,1)S(1)}, u32[]{:S(2)}, u32[]{:S(2)}) %collective-permute-start.5) | collective-permute-done | bytes 262176 | tf_op jit(solution)/shard_map/ppermute | solution.py:338
  56.2 3.0 %shard_map.117 = (bf16[8,512,128]{2,1,0:T(8,128)(2,1)}, bf16[16,64,128]{2,1,0:T(8,128)(2,1)S(1)}, bf16[16,64,128]{2,1,0:T(8,128)(2,1)S(1)}, bf16[16,64,128]{2,1,0:T(8,128)(2,1)S(1)}, bf16[16,64,128]{2,1,0:T(8,128)(2,1)S(1)}) custom-call(bf16[512,512]{1,0:T(8,128)(2,1)} %bitcast.13, bf16[8,512]{1,0:T(8,128)(2,1)} %refs_1_.5, ...), custom_call_target="tpu_custom_call" | custom-call | flops 60000002048 | bytes 180000000 | tf_op jit(solution)/shard_map/pallas_call | solution.py:124
  59.3 0.1 collective-permute-start.6
  59.4 2.8 %collective-permute-start.7 = (bf16[16,64,128]{2,1,0:T(8,128)(2,1)S(1)}, bf16[16,64,128]{2,1,0:T(8,128)(2,1)S(1)}, u32[]{:S(2)}, u32[]{:S(2)}) collective-permute-start(bf16[16,64,128]{2,1,0:T(8,128)(2,1)S(1)} %get-tuple-element.41), channel_id=1, source_target_pairs={{0,48},{1,49},{2,50},{3,51},{4,52},{5,53},{6,54},{7,55},{8,56},{9,... | collective-permute-start | bytes 786440 | tf_op jit(solution)/shard_map/ppermute | solution.py:338
  62.1 0.2 collective-permute-start.8
  62.3 3.0 %shard_map.119 = (bf16[1024,256]{1,0:T(8,128)(2,1)S(1)}, bf16[1024,256]{1,0:T(8,128)(2,1)S(1)}) custom-call(bf16[512,512]{1,0:T(8,128)(2,1)} %refs_0_.6, bf16[8,512]{1,0:T(8,128)(2,1)} %refs_1_.5, bf16[16,4,64,128]{3,2,1,0:T(8,128)(2,1)S(1)} %all-to-all-done.1.refs_2_, bf16[8,512,128]{2,1,0:T(8,128)(2,1)} %get-tuple-element.44.refs_3_), custom_call_target="tpu_custom_call" | custom-call | flops 60000002048 | bytes 180000000 | tf_op jit(solution)/shard_map/pallas_call | solution.py:124
  65.3 4.5 %collective-permute-start.9 = (bf16[1024,256]{1,0:T(8,128)(2,1)S(1)}, bf16[1024,256]{1,0:T(8,128)(2,1)S(1)}, u32[]{:S(2)}, u32[]{:S(2)}) collective-permute-start(bf16[1024,256]{1,0:T(8,128)(2,1)S(1)} %get-tuple-element.46), channel_id=1, source_target_pairs={{0,64},{64,0},{128,192},{192,128},{1,65},{65,1},{129,193},{193,129... | collective-permute-start | bytes 1572872 | tf_op jit(solution)/shard_map/ppermute | solution.py:356
  69.8 0.0 collective-permute-done.6.refs_1_
  69.8 1.2 collective-permute-done.7.refs_2_
  71.0 11.6 %collective-permute-done.8.refs_3_ = bf16[16,64,128]{2,1,0:T(8,128)(2,1)S(1)} collective-permute-done((bf16[16,64,128]{2,1,0:T(8,128)(2,1)S(1)}, bf16[16,64,128]{2,1,0:T(8,128)(2,1)S(1)}, u32[]{:S(2)}, u32[]{:S(2)}) %collective-permute-start.8) | collective-permute-done | bytes 262176 | tf_op jit(solution)/shard_map/ppermute | solution.py:338
  82.5 1.0 shard_map.118
  83.5 0.1 shard_map.120.refs_0_
  83.7 0.0 copy-start.6
  83.7 0.0 copy-start
  83.7 7.7 %all-to-all-start.2 = ((bf16[16,4,64,128]{3,2,1,0:T(8,128)(2,1)}), bf16[16,4,64,128]{3,2,1,0:T(8,128)(2,1)S(1)}, u32[]{:S(2)}, u32[]{:S(2)}) async-start(bf16[16,4,64,128]{3,2,1,0:T(8,128)(2,1)} %shard_map.118), calls=%async_computation.2 | async-start | bytes 2097152 | tf_op jit(solution)/shard_map/all_to_all | solution.py:350
  91.5 0.1 copy.16.refs_1_
  91.6 4.3 %collective-permute-start.10 = (bf16[1024,256]{1,0:T(8,128)(2,1)S(1)}, bf16[1024,256]{1,0:T(8,128)(2,1)S(1)}, u32[]{:S(2)}, u32[]{:S(2)}) collective-permute-start(bf16[1024,256]{1,0:T(8,128)(2,1)S(1)} %shard_map.120.refs_0_), channel_id=1, source_target_pairs={{0,128},{64,192},{128,0},{192,64},{1,129},{65,193},{129,1},{193,65... | collective-permute-start | bytes 1572872 | tf_op jit(solution)/shard_map/ppermute | solution.py:356
  95.9 9.5 %all-to-all-done.2.refs_2_ = bf16[16,4,64,128]{3,2,1,0:T(8,128)(2,1)S(1)} async-done(((bf16[16,4,64,128]{3,2,1,0:T(8,128)(2,1)}), bf16[16,4,64,128]{3,2,1,0:T(8,128)(2,1)S(1)}, u32[]{:S(2)}, u32[]{:S(2)}) %all-to-all-start.2) | async-done | bytes 1048608 | tf_op jit(solution)/shard_map/all_to_all | solution.py:350
  105.4 1.2 copy-done.2
  106.7 2.1 %shard_map.121 = bf16[128,4096]{1,0:T(8,128)(2,1)} custom-call(bf16[512,512]{1,0:T(8,128)(2,1)S(1)} %copy-done, f32[128,1]{1,0:T(8,128)S(1)} %copy.16.refs_1_, bf16[16,4,64,128]{3,2,1,0:T(8,128)(2,1)S(1)} %all-to-all-done.2.refs_2_, bf16[128,4096]{1,0:T(8,128)(2,1)S(1)} %bitcast.9), custom_call_target="tpu_custom_call" | custom-call | flops 60000002048 | bytes 180000000 | tf_op jit(solution)/shard_map/pallas_call | solution.py:124
  108.7 10.8 %collective-permute-done.10.refs_1_ = bf16[1024,256]{1,0:T(8,128)(2,1)S(1)} collective-permute-done((bf16[1024,256]{1,0:T(8,128)(2,1)S(1)}, bf16[1024,256]{1,0:T(8,128)(2,1)S(1)}, u32[]{:S(2)}, u32[]{:S(2)}) %collective-permute-start.10) | collective-permute-done | bytes 524320 | tf_op jit(solution)/shard_map/ppermute | solution.py:356
  119.5 0.1 shard_map.122.refs_0_
  119.6 1.9 %collective-permute-start.11 = (bf16[1024,256]{1,0:T(8,128)(2,1)S(1)}, bf16[1024,256]{1,0:T(8,128)(2,1)S(1)}, u32[]{:S(2)}, u32[]{:S(2)}) collective-permute-start(bf16[1024,256]{1,0:T(8,128)(2,1)S(1)} %shard_map.122.refs_0_), channel_id=1, source_target_pairs={{0,64},{64,0},{128,192},{192,128},{1,65},{65,1},{129,193},{193,129... | collective-permute-start | bytes 1572872 | tf_op jit(solution)/shard_map/ppermute | solution.py:356
  121.5 0.8 shard_map.123.refs_0_
  122.3 0.7 collective-permute-done.11.refs_1_
  123.0 0.8 shard_map.124
  (12 shorter events, 0.0 us)
Async XLA Ops:
  0.6 8.0 %copy-start.1 = (bf16[1,128,4096]{2,1,0:T(8,128)(2,1)S(1)}, bf16[1,128,4096]{2,1,0:T(8,128)(2,1)}, u32[]{:S(2)}) copy-start(bf16[1,128,4096]{2,1,0:T(8,128)(2,1)} %param.10) | copy-start | bytes 3145732
  0.6 8.0 %copy-start.3 = (bf16[512,512]{1,0:T(8,128)(2,1)S(1)}, bf16[512,512]{1,0:T(8,128)(2,1)}, u32[]{:S(2)}) copy-start(bf16[512,512]{1,0:T(8,128)(2,1)} %refs_0_.4) | copy-start | bytes 1572868
  0.7 8.0 %copy-start.4 = (bf16[8,512]{1,0:T(8,128)(2,1)S(1)}, bf16[8,512]{1,0:T(8,128)(2,1)}, u32[]{:S(2)}) copy-start(bf16[8,512]{1,0:T(8,128)(2,1)} %refs_1_.3) | copy-start | bytes 24580
  3.1 20.0 %collective-permute-start = (bf16[16,64,128]{2,1,0:T(8,128)(2,1)S(1)}, bf16[16,64,128]{2,1,0:T(8,128)(2,1)S(1)}, u32[]{:S(2)}, u32[]{:S(2)}) collective-permute-start(bf16[16,64,128]{2,1,0:T(8,128)(2,1)S(1)} %get-tuple-element.28), channel_id=1, source_target_pairs={{0,16},{1,17},{2,18},{3,19},{4,20},{5,21},{6,22},{7,23},{8,24},{9,... | collective-permute-start | bytes 786440 | tf_op jit(solution)/shard_map/ppermute | solution.py:338
  5.7 17.4 %collective-permute-start.1 = (bf16[16,64,128]{2,1,0:T(8,128)(2,1)S(1)}, bf16[16,64,128]{2,1,0:T(8,128)(2,1)S(1)}, u32[]{:S(2)}, u32[]{:S(2)}) collective-permute-start(bf16[16,64,128]{2,1,0:T(8,128)(2,1)S(1)} %get-tuple-element.29), channel_id=1, source_target_pairs={{0,48},{1,49},{2,50},{3,51},{4,52},{5,53},{6,54},{7,55},{8,56},{9,... | collective-permute-start | bytes 786440 | tf_op jit(solution)/shard_map/ppermute | solution.py:338
  8.5 22.7 %collective-permute-start.2 = (bf16[16,64,128]{2,1,0:T(8,128)(2,1)S(1)}, bf16[16,64,128]{2,1,0:T(8,128)(2,1)S(1)}, u32[]{:S(2)}, u32[]{:S(2)}) collective-permute-start(bf16[16,64,128]{2,1,0:T(8,128)(2,1)S(1)} %get-tuple-element.30), channel_id=1, source_target_pairs={{0,32},{1,33},{2,34},{3,35},{4,36},{5,37},{6,38},{7,39},{8,40},{9,... | collective-permute-start | bytes 786440 | tf_op jit(solution)/shard_map/ppermute | solution.py:338
  10.5 22.2 %all-to-all-start = ((bf16[16,4,64,128]{3,2,1,0:T(8,128)(2,1)}), bf16[16,4,64,128]{3,2,1,0:T(8,128)(2,1)S(1)}, u32[]{:S(2)}, u32[]{:S(2)}) async-start(bf16[16,4,64,128]{3,2,1,0:T(8,128)(2,1)} %shard_map.113), calls=%async_computation | async-start | bytes 2097152 | tf_op jit(solution)/shard_map/all_to_all | solution.py:350
  17.3 2.7 %copy-start.5 = (bf16[512,512]{1,0:T(8,128)(2,1)S(1)}, bf16[512,512]{1,0:T(8,128)(2,1)}, u32[]{:S(2)}) copy-start(bf16[512,512]{1,0:T(8,128)(2,1)} %param.13) | copy-start | bytes 1572868
  32.8 9.1 %collective-permute-start.3 = (bf16[16,64,128]{2,1,0:T(8,128)(2,1)S(1)}, bf16[16,64,128]{2,1,0:T(8,128)(2,1)S(1)}, u32[]{:S(2)}, u32[]{:S(2)}) collective-permute-start(bf16[16,64,128]{2,1,0:T(8,128)(2,1)S(1)} %get-tuple-element.34), channel_id=1, source_target_pairs={{0,16},{1,17},{2,18},{3,19},{4,20},{5,21},{6,22},{7,23},{8,24},{9,... | collective-permute-start | bytes 786440 | tf_op jit(solution)/shard_map/ppermute | solution.py:338
  33.3 11.6 %collective-permute-start.4 = (bf16[16,64,128]{2,1,0:T(8,128)(2,1)S(1)}, bf16[16,64,128]{2,1,0:T(8,128)(2,1)S(1)}, u32[]{:S(2)}, u32[]{:S(2)}) collective-permute-start(bf16[16,64,128]{2,1,0:T(8,128)(2,1)S(1)} %get-tuple-element.35), channel_id=1, source_target_pairs={{0,48},{1,49},{2,50},{3,51},{4,52},{5,53},{6,54},{7,55},{8,56},{9,... | collective-permute-start | bytes 786440 | tf_op jit(solution)/shard_map/ppermute | solution.py:338
  36.2 20.0 %collective-permute-start.5 = (bf16[16,64,128]{2,1,0:T(8,128)(2,1)S(1)}, bf16[16,64,128]{2,1,0:T(8,128)(2,1)S(1)}, u32[]{:S(2)}, u32[]{:S(2)}) collective-permute-start(bf16[16,64,128]{2,1,0:T(8,128)(2,1)S(1)} %get-tuple-element.36), channel_id=1, source_target_pairs={{0,32},{1,33},{2,34},{3,35},{4,36},{5,37},{6,38},{7,39},{8,40},{9,... | collective-permute-start | bytes 786440 | tf_op jit(solution)/shard_map/ppermute | solution.py:338
  36.2 26.1 %all-to-all-start.1 = ((bf16[16,4,64,128]{3,2,1,0:T(8,128)(2,1)}), bf16[16,4,64,128]{3,2,1,0:T(8,128)(2,1)S(1)}, u32[]{:S(2)}, u32[]{:S(2)}) async-start(bf16[16,4,64,128]{3,2,1,0:T(8,128)(2,1)} %shard_map.115), calls=%async_computation.1 | async-start | bytes 2097152 | tf_op jit(solution)/shard_map/all_to_all | solution.py:350
  59.3 10.5 %collective-permute-start.6 = (bf16[16,64,128]{2,1,0:T(8,128)(2,1)S(1)}, bf16[16,64,128]{2,1,0:T(8,128)(2,1)S(1)}, u32[]{:S(2)}, u32[]{:S(2)}) collective-permute-start(bf16[16,64,128]{2,1,0:T(8,128)(2,1)S(1)} %get-tuple-element.40), channel_id=1, source_target_pairs={{0,16},{1,17},{2,18},{3,19},{4,20},{5,21},{6,22},{7,23},{8,24},{9,... | collective-permute-start | bytes 786440 | tf_op jit(solution)/shard_map/ppermute | solution.py:338
  59.4 11.6 %collective-permute-start.7 = (bf16[16,64,128]{2,1,0:T(8,128)(2,1)S(1)}, bf16[16,64,128]{2,1,0:T(8,128)(2,1)S(1)}, u32[]{:S(2)}, u32[]{:S(2)}) collective-permute-start(bf16[16,64,128]{2,1,0:T(8,128)(2,1)S(1)} %get-tuple-element.41), channel_id=1, source_target_pairs={{0,48},{1,49},{2,50},{3,51},{4,52},{5,53},{6,54},{7,55},{8,56},{9,... | collective-permute-start | bytes 786440 | tf_op jit(solution)/shard_map/ppermute | solution.py:338
  62.1 20.4 %collective-permute-start.8 = (bf16[16,64,128]{2,1,0:T(8,128)(2,1)S(1)}, bf16[16,64,128]{2,1,0:T(8,128)(2,1)S(1)}, u32[]{:S(2)}, u32[]{:S(2)}) collective-permute-start(bf16[16,64,128]{2,1,0:T(8,128)(2,1)S(1)} %get-tuple-element.42), channel_id=1, source_target_pairs={{0,32},{1,33},{2,34},{3,35},{4,36},{5,37},{6,38},{7,39},{8,40},{9,... | collective-permute-start | bytes 786440 | tf_op jit(solution)/shard_map/ppermute | solution.py:338
  65.3 18.3 %collective-permute-start.9 = (bf16[1024,256]{1,0:T(8,128)(2,1)S(1)}, bf16[1024,256]{1,0:T(8,128)(2,1)S(1)}, u32[]{:S(2)}, u32[]{:S(2)}) collective-permute-start(bf16[1024,256]{1,0:T(8,128)(2,1)S(1)} %get-tuple-element.46), channel_id=1, source_target_pairs={{0,64},{64,0},{128,192},{192,128},{1,65},{65,1},{129,193},{193,129... | collective-permute-start | bytes 1572872 | tf_op jit(solution)/shard_map/ppermute | solution.py:356
  83.7 7.8 %copy-start.6 = (f32[128]{0:T(128)S(1)}, f32[128]{0:T(128)}, u32[]{:S(2)}) copy-start(f32[128]{0:T(128)} %param.19) | copy-start | bytes 1540
  83.7 21.7 %copy-start = (bf16[512,512]{1,0:T(8,128)(2,1)S(1)}, bf16[512,512]{1,0:T(8,128)(2,1)}, u32[]{:S(2)}) copy-start(bf16[512,512]{1,0:T(8,128)(2,1)} %refs_0_.7) | copy-start | bytes 1572868
  83.7 21.7 %all-to-all-start.2 = ((bf16[16,4,64,128]{3,2,1,0:T(8,128)(2,1)}), bf16[16,4,64,128]{3,2,1,0:T(8,128)(2,1)S(1)}, u32[]{:S(2)}, u32[]{:S(2)}) async-start(bf16[16,4,64,128]{3,2,1,0:T(8,128)(2,1)} %shard_map.118), calls=%async_computation.2 | async-start | bytes 2097152 | tf_op jit(solution)/shard_map/all_to_all | solution.py:350
  91.6 27.9 %collective-permute-start.10 = (bf16[1024,256]{1,0:T(8,128)(2,1)S(1)}, bf16[1024,256]{1,0:T(8,128)(2,1)S(1)}, u32[]{:S(2)}, u32[]{:S(2)}) collective-permute-start(bf16[1024,256]{1,0:T(8,128)(2,1)S(1)} %shard_map.120.refs_0_), channel_id=1, source_target_pairs={{0,128},{64,192},{128,0},{192,64},{1,129},{65,193},{129,1},{193,65... | collective-permute-start | bytes 1572872 | tf_op jit(solution)/shard_map/ppermute | solution.py:356
  105.4 1.2 copy-start.2
  119.6 3.4 %collective-permute-start.11 = (bf16[1024,256]{1,0:T(8,128)(2,1)S(1)}, bf16[1024,256]{1,0:T(8,128)(2,1)S(1)}, u32[]{:S(2)}, u32[]{:S(2)}) collective-permute-start(bf16[1024,256]{1,0:T(8,128)(2,1)S(1)} %shard_map.122.refs_0_), channel_id=1, source_target_pairs={{0,64},{64,0},{128,192},{192,128},{1,65},{65,1},{129,193},{193,129... | collective-permute-start | bytes 1572872 | tf_op jit(solution)/shard_map/ppermute | solution.py:356
